TPU v7x, 32 devices: a whole 2x2x4 slice. The times are simulated.
32 devices in a mesh: grp: 2 (over x), hor: 8 (over z, y), dep: 2 (over core).
Axes of the slice: x: 2, y: 2, z: 4, core: 2. Of those that a mesh axis runs over, the one named last changes fastest.
Arguments:
- residual: float32 [64, 64, 1024], P(('grp', 'dep'), 'hor'), parts along dimension 0, may hold values from -6 to 6
- focus_bins: int32 [64, 64, 1024], P(('grp', 'dep'), 'hor'), parts along dimension 0, may hold values from 0 to 15
- layer_class: int32 [64], P('grp'), parts along dimension 0, may hold values from 0 to 7
Outputs:
- preconditioned: float32 [64, 64, 1024], P(('grp', 'dep'), 'hor'), parts along dimension 0
There are 2 independent parts, one for each index of `grp`. A program takes and returns all parts, laid end to end along the dimension named above; each array names one. Nothing has to cross between parts.
All inputs are finite; a program needn't handle non-finite values.
Results may differ from a plain program's by a relative error of at most 0.0003.
Values sent between devices are 32-bit elements; how exact they have to be, the bound alone decides.
No kernel may reach another device: no remote copies, remote signals or barrier semaphores. Data moves between devices by JAX's collectives and lax.ppermute only.
A program may use at most 128 MiB of HBM per device.

v0:
```python
import math

import jax
import jax.numpy as jnp
from jax import lax
from jax.sharding import PartitionSpec as P

damping = 0.01
smoothing = 1.0
coupling_scale = 1.0
weight_base = 0.5
weight_step = 0.2
focus_base = 0.5
focus_step = 0.09242
highest = lax.Precision.HIGHEST


def partner_2(value, axis, distance):
    mask = 2**distance
    pairs = [(source, source ^ mask) for source in range(lax.axis_size(axis))]
    return lax.ppermute(value, axis, pairs)


def depth_weights(layer_class):
    return weight_base * jnp.exp(weight_step * layer_class.astype(jnp.float32))


def focusing(focus_bins):
    return focus_base * jnp.exp(focus_step * focus_bins.astype(jnp.float32))


def couplings(weights):
    inner = coupling_scale * weights[:-1] * weights[1:]
    zero_end = jnp.zeros((1,), jnp.float32)
    return (jnp.concatenate([zero_end, inner]), jnp.concatenate([inner, zero_end]))


def symbol(frequency, length):
    return 2.0 - 2.0 * jnp.cos(frequency * (2.0 * math.pi / length))


def cas_table(length):
    position = jnp.arange(length, dtype=jnp.int32)
    product = position[:, None] * position[None, :] % length
    angles = product.astype(jnp.float32) * (2.0 * math.pi / length)
    return jnp.cos(angles) + jnp.sin(angles)


def shift_down(values, distance, fill_value):
    filler = jnp.full(values.shape[:-2] + (distance, values.shape[-1]), fill_value, values.dtype)
    return jnp.concatenate([filler, values[..., :-distance, :]], axis=-2)


def shift_up(values, distance, fill_value):
    filler = jnp.full(values.shape[:-2] + (distance, values.shape[-1]), fill_value, values.dtype)
    return jnp.concatenate([values[..., distance:, :], filler], axis=-2)


def reduce_step(lower, middle, upper, source, rows_below, rows_above):
    lower_below, middle_below, upper_below, source_below = rows_below
    lower_above, middle_above, upper_above, source_above = rows_above
    ratio_below = -lower / middle_below
    ratio_above = -upper / middle_above
    new_lower = ratio_below * lower_below
    new_middle = middle + ratio_below * upper_below + ratio_above * lower_above
    new_upper = ratio_above * upper_above
    new_source = source + ratio_below * source_below + ratio_above * source_above
    return (new_lower, new_middle, new_upper, new_source)


def local_solve(lower, middle, upper, source):
    layer_count = middle.shape[0]
    distance = 1
    while distance < layer_count:
        rows_below = (
            shift_down(lower, distance, 0.0),
            shift_down(middle, distance, 1.0),
            shift_down(upper, distance, 0.0),
            shift_down(source, distance, 0.0),
        )
        rows_above = (
            shift_up(lower, distance, 0.0),
            shift_up(middle, distance, 1.0),
            shift_up(upper, distance, 0.0),
            shift_up(source, distance, 0.0),
        )
        lower, middle, upper, source = reduce_step(
            lower, middle, upper, source, rows_below, rows_above
        )
        distance = distance * 2
    return source / middle


def body(residual, focus_bins, layer_class):
    depth_rows, y_rows, x_cells = residual.shape
    hor_count = lax.axis_size("hor")
    y_cells = y_rows * hor_count
    focus_map = focusing(focus_bins)
    scaled = focus_map * residual
    weights = depth_weights(layer_class)
    couple_prev, couple_next = couplings(weights)
    first_row = lax.axis_index("dep") * depth_rows
    table_x = cas_table(x_cells)
    table_y = cas_table(y_cells)
    symbol_y = symbol(jnp.arange(y_cells, dtype=jnp.float32), y_cells)
    block_width = x_cells // hor_count
    block_index = lax.axis_index("hor")
    spectra = jnp.einsum(
        "zcx,xbj->bzcj", scaled, table_x.reshape(x_cells, hor_count, block_width), precision=highest
    )
    spectra = spectra.reshape(hor_count, depth_rows, y_rows * block_width)
    table_rows = table_y.reshape(hor_count, y_rows, y_cells)
    portion = lax.all_to_all(spectra, "hor", split_axis=0, concat_axis=0, tiled=True)
    item_count = portion.shape[1]
    arranged = portion.reshape(hor_count, item_count, y_rows, block_width)
    spectrum = jnp.einsum("hzcj,hcy->zjy", arranged, table_rows, precision=highest)
    spectrum = spectrum.reshape(depth_rows, block_width * y_cells)
    wave_x = (block_index * block_width + jnp.arange(block_width, dtype=jnp.int32)).astype(
        jnp.float32
    )
    wave_term = (
        damping + smoothing * (symbol_y[None, :] + symbol(wave_x, x_cells)[:, None])
    ).reshape(-1)
    weight_local = lax.dynamic_slice_in_dim(weights, first_row, depth_rows)
    prev_local = lax.dynamic_slice_in_dim(couple_prev, first_row, depth_rows)
    next_local = lax.dynamic_slice_in_dim(couple_next, first_row, depth_rows)
    middle = weight_local[:, None] * wave_term[None, :] + (prev_local + next_local)[:, None]
    lower = jnp.broadcast_to(-prev_local[:, None], middle.shape)
    upper = jnp.broadcast_to(-next_local[:, None], middle.shape)
    row_index = jnp.arange(depth_rows, dtype=jnp.int32)
    edge_term = jnp.where(row_index == 0, prev_local[0], 0.0) + jnp.where(
        row_index == depth_rows - 1, next_local[depth_rows - 1], 0.0
    )
    source = jnp.stack([spectrum, jnp.broadcast_to(edge_term[:, None], spectrum.shape)])
    solutions = local_solve(lower, middle, upper, source)
    base_part = solutions[0]
    response = solutions[1]
    edge_row = (1 - lax.axis_index("dep")) * (depth_rows - 1)
    base_edge = lax.dynamic_index_in_dim(base_part, edge_row, 0, keepdims=False)
    response_edge = lax.dynamic_index_in_dim(response, edge_row, 0, keepdims=False)
    partner = partner_2(jnp.stack([base_edge, response_edge]), "dep", 0)
    divisor = 1.0 - response_edge * partner[1]
    interface = (partner[0] + partner[1] * base_edge) / divisor
    solved = base_part + response * interface[None, :]
    solved = solved.reshape(depth_rows, block_width, y_cells)
    returned = jnp.einsum(
        "zjk,khc->hzcj", solved, table_y.reshape(y_cells, hor_count, y_rows), precision=highest
    )
    returned = returned.reshape(hor_count, depth_rows, y_rows * block_width)
    table_back = table_x.reshape(hor_count, block_width, x_cells)
    portion = lax.all_to_all(returned, "hor", split_axis=0, concat_axis=0, tiled=True)
    item_count = portion.shape[1]
    arranged = portion.reshape(hor_count, item_count, y_rows, block_width)
    result_field = jnp.einsum("bzcj,bjx->zcx", arranged, table_back, precision=highest)
    return focus_map * result_field / (x_cells * y_cells)


def solution(mesh):
    return jax.shard_map(
        body,
        mesh=mesh,
        in_specs=(P(("grp", "dep"), "hor", None), P(("grp", "dep"), "hor", None), P("grp")),
        out_specs=P(("grp", "dep"), "hor", None),
        check_vma=False,
    )
```

profile of v0, /device:TPU:0, one launch (start us, length us, event | category | flops | bytes accessed | tf_op | source)
XLA Modules:
  0.0 95.7 jit_solution(13671068101681887568)
XLA Ops:
  0.0 1.3 %fusion.57 = f32[16,8,1024]{2,1,0:T(8,128)S(1)} fusion(f32[16,8,1024]{2,1,0:T(8,128)} %param.3, s32[16,8,1024]{2,1,0:T(8,128)} %param.4), kind=kLoop, calls=%fused_computation.81 | loop fusion | flops 524288 | bytes 1572864 | tf_op jit(solution)/shard_map/mul | solution.py:99
  1.3 20.2 %fusion.36 = f32[8,8,2,8,128]{4,3,2,1,0:T(8,128)S(1)} fusion(s32[8,128]{1,0:T(8,128)S(1)} %multiply_add_fusion.8, f32[16,8,1024]{2,1,0:T(8,128)S(1)} %fusion.57), kind=kOutput, calls=%fused_computation.44 | convolution fusion | flops 1626341376 | bytes 1052672 | tf_op jit(solution)/shard_map/zcx,xbj->bzcj/dot_general | solution.py:108
  21.5 0.9 copy.34
  22.4 7.3 %all-to-all-start = ((f32[8,16,1024]{2,1,0:T(8,128)}), f32[8,16,1024]{2,1,0:T(8,128)}, u32[]{:S(2)}, u32[]{:S(2)}) async-start(f32[8,16,1024]{2,1,0:T(8,128)} %bitcast.76), calls=%async_computation | async-start | bytes 1048576 | tf_op jit(solution)/shard_map/all_to_all | solution.py:113
  29.7 0.1 slice_multiply_fusion
  29.8 0.1 dynamic_slice.22
  29.9 0.1 pad_maximum_fusion.2
  29.9 0.1 fusion.97
  30.0 0.1 fusion.111
  30.1 0.1 add_add_fusion
  30.2 0.1 add.306
  30.3 0.1 multiply_add_fusion.7
  30.4 0.1 fusion.110
  30.5 0.1 fusion.112
  30.6 0.1 concatenate.110
  30.7 0.1 broadcast_multiply_fusion
  30.8 0.1 fusion.107
  30.9 0.1 concatenate.112
  31.0 0.1 broadcast_multiply_fusion.1
  31.1 0.2 multiply_add_fusion.6
  31.3 0.1 fusion.109
  31.4 0.5 copy-done
  32.0 0.1 pad_multiply_fusion.2
  32.1 0.1 fusion.104
  32.2 0.2 pad_multiply_fusion.3
  32.3 0.2 multiply_add_fusion.5
  32.5 0.1 fusion.106
  32.6 0.1 fusion.105
  32.7 0.2 pad_multiply_fusion.1
  32.9 0.1 pad_multiply_fusion
  33.0 0.2 multiply_add_fusion.4
  33.3 1.2 %multiply_add_fusion.3 = (f32[16,8192]{1,0:T(8,128)}, f32[16,8192]{1,0:T(8,128)}, f32[16,8192]{1,0:T(8,128)}) fusion(f32[8,8192]{1,0:T(8,128)S(1)} %slice.184, f32[16,8192]{1,0:T(8,128)S(1)} %multiply_add_fusion.4, f32[8,8192]{1,0:T(8,128)S(1)} %slice.183, f32[8,8192]{1,0:T(8,128)S(1)} %get-tuple-element.35, f32[16,8192]{1,0:T(8,128)S(1)} %get-tuple-element.8, ...), kind=kLoop, calls=%fused_computation.63 | loop fusion | flops 1048576 | bytes 4194304 | tf_op jit(solution)/shard_map/add | solution.py:65
  34.5 0.6 slice.122
  35.1 0.1 copy.9
  35.2 0.6 fusion.84
  35.8 0.2 add_bitcast_fusion
  36.0 8.2 %all-to-all-done = f32[8,16,1024]{2,1,0:T(8,128)} async-done(((f32[8,16,1024]{2,1,0:T(8,128)}), f32[8,16,1024]{2,1,0:T(8,128)}, u32[]{:S(2)}, u32[]{:S(2)}) %all-to-all-start) | async-done | bytes 524320 | tf_op jit(solution)/shard_map/all_to_all | solution.py:113
  44.2 1.1 %copy.25 = f32[16,8,8,128]{3,2,1,0:T(8,128)S(1)} copy(f32[16,8,8,128]{3,1,2,0:T(8,128)} %bitcast.29) | data formatting | bytes 1048576
  45.4 2.8 %convolution_bitcast_fusion = f32[16,128,64]{2,1,0:T(8,128)} fusion(f32[8,8,64,1]{2,0,1,3:T(8,128)S(1)} %add_bitcast_fusion, f32[8,16,8,128]{3,2,1,0:T(8,128)S(1)} %bitcast.83), kind=kOutput, calls=%fused_computation.43 | convolution fusion | flops 100663296 | bytes 1064960 | tf_op jit(solution)/shard_map/hzcj,hcy->zjy/dot_general | solution.py:116
  48.2 1.6 %stack_reshape.3 = f32[1,16,8192]{2,1,0:T(8,128)S(1)} reshape(f32[16,128,64]{2,1,0:T(8,128)} %convolution_bitcast_fusion) | data formatting | bytes 1048576 | tf_op jit(solution)/shard_map/stack;reshape | solution.py:134
  49.7 0.1 stack_broadcast_in_dim.2
  49.9 0.1 fusion.48
  50.0 0.9 copy-done.1
  50.9 0.3 fusion.51
  51.2 0.1 fusion.102
  51.3 0.3 multiply_add_fusion.1
  51.6 0.1 fusion.101
  51.7 0.3 multiply_add_fusion
  52.0 0.1 fusion.100
  52.1 0.9 copy-done.2
  53.0 0.2 copy-done.3
  53.2 0.2 copy-done.4
  53.4 0.2 add_divide_fusion
  53.5 0.1 fusion.99
  53.8 0.1 collective-permute-start
  53.9 1.2 %collective-permute-done = f32[2,8192]{1,0:T(2,128)S(1)} collective-permute-done((f32[2,8192]{1,0:T(2,128)S(1)}, f32[2,8192]{1,0:T(2,128)S(1)}, u32[]{:S(2)}, u32[]{:S(2)}) %collective-permute-start) | collective-permute-done | bytes 65568 | tf_op jit(solution)/shard_map/ppermute | solution.py:21
  55.1 0.1 fusion.64
  55.2 0.1 multiply_add_fusion.2
  55.3 0.4 add.329
  55.7 1.4 %convolution_bitcast_fusion.1 = f32[8,16,8,128]{3,2,1,0:T(8,128)S(1)} fusion(f32[16,128,64]{2,1,0:T(8,128)S(1)} %add.329, s32[8,8]{1,0:T(8,128)S(1)} %multiply_add_fusion.9), kind=kOutput, calls=%fused_computation.46 | convolution fusion | flops 100724736 | bytes 1048832 | tf_op jit(solution)/shard_map/zjk,khc->hzcj/dot_general | solution.py:146
  57.2 0.1 reshape.255
  57.3 18.4 %all_to_all.10 = f32[8,16,1024]{2,1,0:T(8,128)S(1)} all-to-all(f32[8,16,1024]{2,1,0:T(8,128)S(1)} %reshape.255), channel_id=1, replica_groups=mesh['grp'=2,'hor'=8,'dep'=2] {'hor'}, dimensions={0} | all-to-all | bytes 1048576 | tf_op jit(solution)/shard_map/all_to_all | solution.py:151
  75.6 0.1 copy.26
  75.7 19.9 %fusion.45 = f32[16,8,1024]{2,1,0:T(8,128)} fusion(s32[8,128]{1,0:T(8,128)S(1)} %multiply_add_fusion.8, s32[16,8,1024]{2,1,0:T(8,128)S(1)} %copy-done.5, f32[8,16,8,128]{3,2,1,0:T(8,128)S(1)} %bitcast.84), kind=kOutput, calls=%fused_computation.48 | convolution fusion | flops 1626996736 | bytes 1576960 | tf_op jit(solution)/shard_map/bzcj,bjx->zcx/dot_general | solution.py:154
  (24 shorter events, 0.4 us)
Async XLA Ops:
  21.5 8.2 %copy-start.6 = (s32[32]{0:T(128)S(1)}, s32[32]{0:T(128)}, u32[]{:S(2)}) copy-start(s32[32]{0:T(128)} %param.5) | copy-start | bytes 388
  22.4 21.9 %all-to-all-start = ((f32[8,16,1024]{2,1,0:T(8,128)}), f32[8,16,1024]{2,1,0:T(8,128)}, u32[]{:S(2)}, u32[]{:S(2)}) async-start(f32[8,16,1024]{2,1,0:T(8,128)} %bitcast.76), calls=%async_computation | async-start | bytes 1048576 | tf_op jit(solution)/shard_map/all_to_all | solution.py:113
  31.1 0.8 copy-start
  49.8 1.0 %copy-start.1 = (f32[16,8192]{1,0:T(8,128)S(1)}, f32[16,8192]{1,0:T(8,128)}, u32[]{:S(2)}) copy-start(f32[16,8192]{1,0:T(8,128)} %copy-done) | copy-start | bytes 1572868
  52.0 1.0 %copy-start.2 = (f32[16,8192]{1,0:T(8,128)S(1)}, f32[16,8192]{1,0:T(8,128)}, u32[]{:S(2)}) copy-start(f32[16,8192]{1,0:T(8,128)} %get-tuple-element.5) | copy-start | bytes 1572868
  52.0 1.2 %copy-start.3 = (f32[16,8192]{1,0:T(8,128)S(1)}, f32[16,8192]{1,0:T(8,128)}, u32[]{:S(2)}) copy-start(f32[16,8192]{1,0:T(8,128)} %get-tuple-element.6) | copy-start | bytes 1572868
  52.0 1.3 %copy-start.4 = (f32[16,8192]{1,0:T(8,128)S(1)}, f32[16,8192]{1,0:T(8,128)}, u32[]{:S(2)}) copy-start(f32[16,8192]{1,0:T(8,128)} %get-tuple-element.7) | copy-start | bytes 1572868
  53.8 1.3 %collective-permute-start = (f32[2,8192]{1,0:T(2,128)S(1)}, f32[2,8192]{1,0:T(2,128)S(1)}, u32[]{:S(2)}, u32[]{:S(2)}) collective-permute-start(f32[2,8192]{1,0:T(2,128)S(1)} %pad_maximum_fusion.1), channel_id=1, source_target_pairs={{0,1},{1,0},{2,3},{3,2},{4,5},{5,4},{6,7},{7,6},{8,9},{9,8},{10,11... | collective-permute-start | bytes 196616 | tf_op jit(solution)/shard_map/ppermute | solution.py:21
  57.2 18.5 %copy-start.5 = (s32[16,8,1024]{2,1,0:T(8,128)S(1)}, s32[16,8,1024]{2,1,0:T(8,128)}, u32[]{:S(2)}) copy-start(s32[16,8,1024]{2,1,0:T(8,128)} %param.4) | copy-start | bytes 1572868
where the time goes:
time: 96.1 us; the launch traced here: 95.7 us
  matrix products  44.3 us (46%)
  blocking collectives  18.4 us (19%)
  waiting for transfers between devices  9.43 us (10%)
  local copies, waits for them, and re-layouts  9.11 us (9%)
  starting transfers between devices  7.35 us (8%)
  other arithmetic  6.73 us (7%)
    dot_general x1, matrix products, body(): jnp.einsum('zcx,xbj->bzcj', scaled, table_x.reshape(x_cells, hor_count, b...  20.2 us
    dot_general x1, matrix products, body(): jnp.einsum('bzcj,bjx->zcx', arranged, table_back, precision=highest)  19.9 us
    all_to_all x1, blocking collectives, body(): lax.all_to_all(returned, 'hor', split_axis=0, concat_axis=0, tiled=True)  18.4 us
    all_to_all x1, waiting for transfers between devices, body(): lax.all_to_all(spectra, 'hor', split_axis=0, concat_axis=0, tiled=True)  8.19 us
    all_to_all x1, starting transfers between devices, body(): lax.all_to_all(spectra, 'hor', split_axis=0, concat_axis=0, tiled=True)  7.28 us
    unnamed x16, local copies, waits for them, and re-layouts  3.92 us
    dot_general x1, matrix products, body(): jnp.einsum('hzcj,hcy->zjy', arranged, table_rows, precision=highest)  2.79 us
  transfers between devices with their start and end apart: 2, of which 2 were waited for; matrix products, arithmetic and copies ran while one was open for 6% of the time, Pallas kernels for 0%

commit v1 on v0

v1 whole, which is shorter than its diff:
```python
import functools
import math

import jax
import jax.numpy as jnp
import ml_dtypes
import numpy as np
from jax import lax
from jax.experimental import pallas as pl
from jax.experimental.pallas import tpu as pltpu
from jax.sharding import PartitionSpec as P

damping = 0.01
smoothing = 1.0
coupling_scale = 1.0
weight_base = 0.5
weight_step = 0.2
focus_base = 0.5
focus_step = 0.09242
lanes = 128
f32 = jnp.float32
bf16 = jnp.bfloat16


def cas(angle):
    return np.cos(angle) + np.sin(angle)


def split_table(table):
    table = table.astype(np.float32)
    high = table.astype(ml_dtypes.bfloat16)
    low = (table - high.astype(np.float32)).astype(ml_dtypes.bfloat16)
    return high, low


def fold_tables(length):
    half = length // 2
    cell = np.arange(half)[:, None]
    tables = []
    for parity in range(2):
        wave = 2 * np.arange(half)[None, :] + parity
        tables.append(cas(2.0 * np.pi * (cell * wave % length) / length))
    return split_table(np.stack(tables))


def sine_matrix(rows):
    index = np.arange(1, rows)
    matrix = np.zeros((rows, rows))
    matrix[0, 0] = 1.0
    matrix[1:, 1:] = np.sqrt(2.0 / rows) * np.sin(np.pi * np.outer(index, index) / rows)
    return matrix


def symbol_of(angle):
    return 2.0 - 2.0 * np.cos(angle)


def split(values):
    high = values.astype(bf16)
    low = (values - high.astype(f32)).astype(bf16)
    return high, low


def dot3(left, right, dims=(((1,), (0,)), ((), ()))):
    dot = functools.partial(lax.dot_general, dimension_numbers=dims, preferred_element_type=f32)
    left_high, left_low = left
    right_high, right_low = right
    return dot(left_high, right_high) + (dot(left_low, right_high) + dot(left_high, right_low))


def focusing(focus_bins):
    return focus_base * jnp.exp(focus_step * focus_bins.astype(f32))


def layer_terms(class_ref, layers, plane_tiles, axis):
    weights = []
    for layer in range(layers):
        level = jnp.full((8, lanes), class_ref[layer], jnp.int32).astype(f32)
        weights.append(weight_base * jnp.exp(weight_step * level))
    couple = [coupling_scale * weights[k] * weights[k + 1] for k in range(layers - 1)]

    def spread(values):
        return [jnp.concatenate([value] * plane_tiles, axis=axis) for value in values]

    return spread(weights), spread(couple)


def diagonal(layer, weights, couple, wave):
    total = weights[layer] * wave
    if layer > 0:
        total = total + couple[layer - 1]
    if layer < len(couple):
        total = total + couple[layer]
    return total


def factor(weights, couple, wave, inverse_ref):
    layers = len(weights)
    half = layers // 2
    top = 1.0 / diagonal(0, weights, couple, wave)
    bottom = 1.0 / diagonal(layers - 1, weights, couple, wave)
    inverse_ref[0] = top
    inverse_ref[layers - 1] = bottom
    for step in range(1, half):
        low = step
        link = couple[low - 1]
        top = 1.0 / (diagonal(low, weights, couple, wave) - link * link * top)
        inverse_ref[low] = top
        high = layers - 1 - step
        link = couple[high]
        pivot = diagonal(high, weights, couple, wave) - link * link * bottom
        if step == half - 1:
            link = couple[half - 1]
            pivot = pivot - link * link * top
        bottom = 1.0 / pivot
        inverse_ref[high] = bottom


def substitute(couple, inverse_ref, partial_ref, source, emit):
    layers = len(couple) + 1
    half = layers // 2
    top = source(0)
    bottom = source(layers - 1)
    partial_ref[0] = top
    partial_ref[layers - 1] = bottom
    for step in range(1, half):
        low = step
        top = source(low) + couple[low - 1] * inverse_ref[low - 1] * top
        partial_ref[low] = top
        high = layers - 1 - step
        bottom = source(high) + couple[high] * inverse_ref[high + 1] * bottom
        partial_ref[high] = bottom
    link = couple[half - 1]
    bottom = (bottom + link * inverse_ref[half - 1] * top) * inverse_ref[half]
    top = (top + link * bottom) * inverse_ref[half - 1]
    emit(half, bottom)
    emit(half - 1, top)
    for step in range(1, half):
        low = half - 1 - step
        top = (partial_ref[low] + couple[low] * top) * inverse_ref[low]
        emit(low, top)
        high = half + step
        bottom = (partial_ref[high] + couple[high - 1] * bottom) * inverse_ref[high]
        emit(high, bottom)


def turn(values, shift):
    shift = shift % lanes
    return values if shift == 0 else pltpu.roll(values, shift, values.ndim - 1)


def fold_kernel(dep_ref, residual_ref, bins_ref, own_ref, send_ref):
    half = own_ref.shape[-1]
    sign = jnp.where(dep_ref[0] == 0, 1.0, -1.0).astype(f32)
    scaled = focusing(bins_ref[...]) * residual_ref[...]
    left = scaled[..., :half]
    right = sign * scaled[..., half:]
    own_ref[...] = left + right
    send_ref[...] = left - right


def interior_kernel(
    dep_ref,
    class_ref,
    own_ref,
    recv_ref,
    table_high,
    table_low,
    sine_high,
    sine_low,
    edge_high,
    edge_low,
    wave_ref,
    packed_ref,
    source_ref,
    inverse_ref,
    stage_ref,
    partial_ref,
):
    depth, rows, half = own_ref.shape
    layers = 2 * depth
    hor_count = packed_ref.shape[0]
    chunk = half // hor_count
    place = dep_ref[0] * depth
    stage_ref[pl.ds(place, depth)] = own_ref[...]
    stage_ref[pl.ds(depth - place, depth)] = recv_ref[...]
    weights, couple = layer_terms(class_ref, layers, half // lanes, 1)
    factor(weights, couple, wave_ref[0], inverse_ref)
    cells = stage_ref[...].reshape(layers * rows, half)
    waves = dot3(split(cells), (table_high[0], table_low[0]))
    block = depth * rows
    sine = (sine_high[...], sine_low[...])
    for part in range(2):
        piece = waves[part * block : (part + 1) * block]
        source_ref[part * depth : (part + 1) * depth] = dot3(sine, split(piece)).reshape(
            depth, rows, half
        )
    edge_row = lax.broadcasted_iota(jnp.int32, (rows, half), 0) == 0

    def emit(layer, values):
        stage_ref[layer] = jnp.where(edge_row, source_ref[layer], weights[layer] * values)

    substitute(couple, inverse_ref, partial_ref, lambda layer: source_ref[layer], emit)
    edge = (edge_high[...], edge_low[...])
    lower = []
    upper = []
    for part in range(2):
        piece = stage_ref[part * depth : (part + 1) * depth].reshape(block, half)
        both = dot3(edge, split(piece))
        lower.append(both[:depth])
        upper.append(both[depth:])
    lower = jnp.concatenate(lower, axis=0)
    upper = jnp.concatenate(upper, axis=0)
    lane = lax.broadcasted_iota(jnp.int32, (layers, lanes), 1)
    for index in range(hor_count):
        tile = index * chunk // lanes * lanes
        offset = index * chunk % lanes
        packed_ref[index] = jnp.where(
            lane < chunk,
            turn(lower[:, tile : tile + lanes], -offset),
            turn(upper[:, tile : tile + lanes], chunk - offset),
        )


def small_hartley(count, read, write, shape):
    if count <= 8:
        table = cas(2.0 * np.pi * (np.outer(np.arange(count), np.arange(count)) % count) / count)
        parts = [read(index) for index in range(count)]
        for wave in range(count):
            total = None
            for index in range(count):
                value = float(table[wave, index])
                if abs(value) < 1e-12:
                    continue
                if abs(value - 1.0) < 1e-12:
                    term = parts[index]
                elif abs(value + 1.0) < 1e-12:
                    term = -parts[index]
                else:
                    term = parts[index] * value
                total = term if total is None else total + term
            write(wave, total)
        return

    def outer(wave, carry):
        def inner(index, total):
            angle = jnp.full(shape, wave * index % count, jnp.int32).astype(f32)
            angle = angle * (2.0 * math.pi / count)
            return total + read(index) * (jnp.cos(angle) + jnp.sin(angle))

        write(wave, lax.fori_loop(0, count, inner, jnp.zeros(shape, f32)))
        return carry

    lax.fori_loop(0, count, outer, 0)


def interface_kernel(
    spot_ref,
    class_ref,
    packed_ref,
    wave_y_ref,
    wave_x_ref,
    back_ref,
    sum_ref,
    wave_ref,
    answer_ref,
    inverse_ref,
    partial_ref,
    *,
    chunk,
):
    hor_count, layers, _ = packed_ref.shape
    rows = wave_y_ref.shape[0]
    subsets = lanes // chunk
    classes = max(1, hor_count // rows)
    repeats = max(1, rows // hor_count)
    lane = lax.broadcasted_iota(jnp.int32, (layers, lanes), 1)
    first = lane % (2 * chunk) < chunk

    def halves(index):
        values = packed_ref[index]
        width = 2 * chunk
        while width < lanes:
            values = jnp.where(lane < width, values, turn(values, width))
            width = width * 2
        return values

    def joined(index):
        here = halves(index)
        before = halves((index + hor_count - 1) % hor_count)
        return jnp.where(first, here, turn(here, chunk)) + jnp.where(
            first, turn(before, -chunk), before
        )

    def put_sum(index, values):
        sum_ref[index] = values

    if hor_count <= 8:
        small_hartley(hor_count, joined, lambda k, v: wave_ref.__setitem__(k, v), (layers, lanes))
    else:
        lax.fori_loop(0, hor_count, lambda k, c: (put_sum(k, joined(k)), c)[1], 0)
        small_hartley(
            hor_count,
            lambda k: sum_ref[k],
            lambda k, v: wave_ref.__setitem__(k, v),
            (layers, lanes),
        )
    weights, couple = layer_terms(class_ref, layers, rows // 8, 0)
    wave = damping + smoothing * (wave_y_ref[...] + wave_x_ref[pl.ds(spot_ref[0], 1), :])
    factor(weights, couple, wave, inverse_ref)
    plane_lane = lax.broadcasted_iota(jnp.int32, (rows, lanes), 1)
    group = plane_lane // chunk % classes

    def source(layer):
        if classes == 1:
            return jnp.concatenate([wave_ref[:, layer, :]] * repeats, axis=0)
        total = wave_ref[0:rows, layer, :]
        for part in range(1, classes):
            piece = wave_ref[part * rows : (part + 1) * rows, layer, :]
            total = jnp.where(group == part, piece, total)
        return total

    def emit(layer, values):
        if classes == 1:
            total = values[0:hor_count]
            for part in range(1, repeats):
                total = total + values[part * hor_count : (part + 1) * hor_count]
            answer_ref[:, layer, :] = total
            return
        for part in range(classes):
            answer_ref[part * rows : (part + 1) * rows, layer, :] = jnp.where(
                group == part, values, 0.0
            )

    substitute(couple, inverse_ref, partial_ref, source, emit)

    def gathered(index):
        values = answer_ref[index]
        shift = chunk
        while shift < lanes:
            values = values + turn(values, shift)
            shift = shift * 2
        return values

    scale = 1.0 / (rows * subsets)

    def put_scaled(index, values):
        sum_ref[index] = values * scale

    if hor_count <= 8:
        small_hartley(hor_count, gathered, put_scaled, (layers, lanes))
    else:
        lax.fori_loop(
            0, hor_count, lambda k, c: (wave_ref.__setitem__(k, gathered(k)), c)[1], 0
        )
        small_hartley(hor_count, lambda k: wave_ref[k], put_scaled, (layers, lanes))
    for index in range(hor_count):
        back_ref[index] = jnp.where(first, sum_ref[index], sum_ref[(index + 1) % hor_count])


def finish_kernel(
    dep_ref,
    class_ref,
    back_ref,
    source_ref,
    inverse_ref,
    table_high,
    table_low,
    sine_high,
    sine_low,
    near_ref,
    far_ref,
    own_ref,
    send_ref,
    left_ref,
    right_ref,
    stage_ref,
    partial_ref,
):
    layers, rows, half = source_ref.shape
    depth = layers // 2
    hor_count = back_ref.shape[0]
    chunk = half // hor_count
    lane = lax.broadcasted_iota(jnp.int32, (layers, lanes), 1)
    for tile in range(half // lanes):
        left = None
        right = None
        for index in range(tile * lanes // chunk, (tile + 1) * lanes // chunk):
            offset = index * chunk % lanes
            values = back_ref[index]
            left_part = turn(values, offset)
            right_part = turn(values, offset - chunk)
            inside = lane >= offset
            left = left_part if left is None else jnp.where(inside, left_part, left)
            right = right_part if right is None else jnp.where(inside, right_part, right)
        left_ref[:, tile * lanes : (tile + 1) * lanes] = left
        right_ref[:, tile * lanes : (tile + 1) * lanes] = right
    weights, couple = layer_terms(class_ref, layers, half // lanes, 1)
    near = near_ref[...]
    far = far_ref[...]
    edge_row = lax.broadcasted_iota(jnp.int32, (rows, half), 0) == 0

    def row_of(ref, layer):
        return jnp.broadcast_to(ref[pl.ds(layer, 1), :], (rows, half))

    def source(layer):
        pull = near * row_of(left_ref, layer) + far * row_of(right_ref, layer)
        return source_ref[layer] + weights[layer] * pull

    def emit(layer, values):
        stage_ref[layer] = jnp.where(edge_row, row_of(left_ref, layer), values)

    substitute(couple, inverse_ref, partial_ref, source, emit)
    block = depth * rows
    sine = (sine_high[...], sine_low[...])
    parts = []
    for part in range(2):
        piece = stage_ref[part * depth : (part + 1) * depth].reshape(block, half)
        parts.append(dot3(sine, split(piece)))
    waves = jnp.concatenate(parts, axis=0)
    cells = dot3(split(waves), (table_high[0], table_low[0]), (((1,), (1,)), ((), ())))
    stage_ref[...] = cells.reshape(layers, rows, half)
    place = dep_ref[0] * depth
    own_ref[...] = stage_ref[pl.ds(place, depth)]
    send_ref[...] = stage_ref[pl.ds(depth - place, depth)]


def unfold_kernel(dep_ref, own_ref, recv_ref, bins_ref, out_ref, *, scale):
    half = own_ref.shape[-1]
    sign = jnp.where(dep_ref[0] == 0, scale, -scale).astype(f32)
    focus_map = focusing(bins_ref[...])
    own = own_ref[...]
    recv = recv_ref[...]
    out_ref[..., :half] = focus_map[..., :half] * ((own + recv) * scale)
    out_ref[..., half:] = focus_map[..., half:] * ((own - recv) * sign)


def whole(shape):
    return pl.BlockSpec(shape, lambda i, *_: (0,) * len(shape))


def call(kernel, scalars, in_specs, out_specs, out_shape, scratch=(), grid=(1,)):
    return pl.pallas_call(
        kernel,
        grid_spec=pltpu.PrefetchScalarGridSpec(
            num_scalar_prefetch=scalars,
            grid=grid,
            in_specs=in_specs,
            out_specs=out_specs,
            scratch_shapes=list(scratch),
        ),
        out_shape=out_shape,
        compiler_params=pltpu.CompilerParams(vmem_limit_bytes=48 * 1024 * 1024),
    )


def body(residual, focus_bins, layer_class):
    depth, rows, x_cells = residual.shape
    half = x_cells // 2
    layers = layer_class.shape[0]
    hor_count = lax.axis_size("hor")
    y_cells = rows * hor_count
    chunk = half // hor_count
    plane_rows = rows * half // lanes
    dep = lax.axis_index("dep").astype(jnp.int32)
    hor = lax.axis_index("hor").astype(jnp.int32)
    dep_index = dep.reshape(1)
    spot = (hor * 2 + dep).reshape(1)

    table_high, table_low = fold_tables(x_cells)
    sine = sine_matrix(rows)
    sine_high, sine_low = split_table(np.kron(np.eye(depth), sine))
    lower_row = np.concatenate([[1.0], sine[1, 1:]])
    upper_row = np.concatenate([[0.0], sine[rows - 1, 1:]])
    edge_high, edge_low = split_table(
        np.concatenate([np.kron(np.eye(depth), row[None, :]) for row in (lower_row, upper_row)])
    )
    wave_x = np.stack(
        [symbol_of(2.0 * np.pi * (2 * np.arange(half) + parity) / x_cells) for parity in range(2)]
    )
    mode = symbol_of(np.pi * np.arange(rows) / rows)
    wave_inner = damping + smoothing * (mode[None, :, None] + wave_x[:, None, :])
    wave_inner = wave_inner.astype(np.float32)
    near = np.broadcast_to((lower_row * (np.arange(rows) > 0))[:, None], (rows, half))
    far = np.broadcast_to(upper_row[:, None], (rows, half))
    lane = np.arange(lanes)
    wave_number = (lane // chunk)[None, :] * plane_rows + np.arange(plane_rows)[:, None]
    wave_y = symbol_of(2.0 * np.pi * wave_number / y_cells).astype(np.float32)
    spots = np.arange(hor_count)[:, None, None] * chunk + (lane % chunk)[None, None, :]
    spots = 2 * spots + np.arange(2)[None, :, None]
    wave_spots = symbol_of(2.0 * np.pi * spots / x_cells).reshape(2 * hor_count, lanes)

    def shape(*dims):
        return jax.ShapeDtypeStruct(dims, f32)

    slab = (depth, rows, half)
    field = (layers, rows, half)
    packed = (hor_count, layers, lanes)
    steps = 2
    piece = depth // steps
    cut = pl.BlockSpec((piece, rows, x_cells), lambda i, *_: (i, 0, 0))
    cut_half = pl.BlockSpec((piece, rows, half), lambda i, *_: (i, 0, 0))
    own, send = call(
        fold_kernel, 1, [cut, cut], [cut_half, cut_half], [shape(*slab)] * 2, grid=(steps,)
    )(dep_index, residual, focus_bins)
    pairs = [(0, 1), (1, 0)]
    recv = lax.ppermute(send, "dep", pairs)

    table_spec = pl.BlockSpec((1, half, half), lambda i, dep_ref, *_: (dep_ref[0], 0, 0))
    sine_spec = whole(sine_high.shape)
    edge_spec = whole(edge_high.shape)
    wave_spec = pl.BlockSpec((1, rows, half), lambda i, dep_ref, *_: (dep_ref[0], 0, 0))
    outgoing, source, inverse = call(
        interior_kernel,
        2,
        [whole(slab)] * 2
        + [table_spec] * 2
        + [sine_spec] * 2
        + [edge_spec] * 2
        + [wave_spec],
        [whole(packed), whole(field), whole(field)],
        [shape(*packed), shape(*field), shape(*field)],
        [pltpu.VMEM(field, f32)] * 2,
    )(
        dep_index,
        layer_class,
        own,
        recv,
        jnp.asarray(table_high),
        jnp.asarray(table_low),
        jnp.asarray(sine_high),
        jnp.asarray(sine_low),
        jnp.asarray(edge_high),
        jnp.asarray(edge_low),
        jnp.asarray(wave_inner),
    )
    incoming = lax.all_to_all(outgoing, "hor", split_axis=0, concat_axis=0, tiled=True)
    plane = (layers, plane_rows, lanes)
    answered = call(
        functools.partial(interface_kernel, chunk=chunk),
        2,
        [whole(packed), whole(wave_y.shape), whole(wave_spots.shape)],
        whole(packed),
        shape(*packed),
        [pltpu.VMEM(packed, f32)] * 3 + [pltpu.VMEM(plane, f32)] * 2,
    )(
        spot,
        layer_class,
        incoming,
        jnp.asarray(wave_y),
        jnp.asarray(wave_spots.astype(np.float32)),
    )
    edges = lax.all_to_all(answered, "hor", split_axis=0, concat_axis=0, tiled=True)
    own, send = call(
        finish_kernel,
        2,
        [whole(packed), whole(field), whole(field)]
        + [table_spec] * 2
        + [sine_spec] * 2
        + [whole((rows, half))] * 2,
        [whole(slab)] * 2,
        [shape(*slab)] * 2,
        [pltpu.VMEM((layers, half), f32)] * 2 + [pltpu.VMEM(field, f32)] * 2,
    )(
        dep_index,
        layer_class,
        edges,
        source,
        inverse,
        jnp.asarray(table_high),
        jnp.asarray(table_low),
        jnp.asarray(sine_high),
        jnp.asarray(sine_low),
        jnp.asarray(near.astype(np.float32)),
        jnp.asarray(far.astype(np.float32)),
    )
    recv = lax.ppermute(send, "dep", pairs)
    return call(
        functools.partial(unfold_kernel, scale=1.0 / x_cells),
        1,
        [cut_half, cut_half, cut],
        cut,
        shape(depth, rows, x_cells),
        grid=(steps,),
    )(dep_index, own, recv, focus_bins)


def solution(mesh):
    return jax.shard_map(
        body,
        mesh=mesh,
        in_specs=(P(("grp", "dep"), "hor", None), P(("grp", "dep"), "hor", None), P("grp")),
        out_specs=P(("grp", "dep"), "hor", None),
        check_vma=False,
    )
```

time: 96.1 us -> 40.8 us (0.42)
  matrix products: 44.3 us -> 0 us
  blocking collectives: 18.4 us -> 9.92 us
  other arithmetic: 6.73 us -> 0 us
  Pallas kernels: 0 us -> 6.47 us
  local copies, waits for them, and re-layouts: 9.11 us -> 5.73 us
    dot_general x4 -> x0, matrix products: 44.3 us -> none  [the longest x1 20.2 us: body(): jnp.einsum('zcx,xbj->bzcj', scaled, table_x.reshape(x_cells, hor_count, b...]
    all_to_all x1, blocking collectives: 18.4 us -> 9.92 us  [body(): lax.all_to_all(answered, 'hor', split_axis=0, concat_axis=0, tiled=True)]
    pallas_call x0 -> x5, Pallas kernels: none -> 6.47 us  [the longest x1 2.56 us: body(): call(interior_kernel, 2, [whole(slab)] * 2 + [table_spec] * 2 + [sine_spe...]
    add x13 -> x0, other arithmetic: 3.72 us -> none  [the longest x4 1.78 us: reduce_step(): new_middle = middle + ratio_below * upper_below + ratio_above * lower_above]
    mul x11 -> x0, other arithmetic: 2.25 us -> none  [the longest x1 1.31 us: body(): scaled = focus_map * residual]
    unnamed x16 -> x36, local copies, waits for them, and re-layouts: 3.92 us -> 5.73 us
    slice x17 -> x0, local copies, waits for them, and re-layouts: 1.73 us -> none  [the longest x10 0.79 us: shift_down(): return jnp.concatenate([filler, values[..., :-distance, :]], axis=-2)]
    another operation x2 -> x0, local copies, waits for them, and re-layouts: 1.68 us -> none  [body(): jnp.stack([spectrum, jnp.broadcast_to(edge_term[:, None], spectrum.shape)])]
  transfers between devices with their start and end apart: 2 -> 3, of which waited for: 2 -> 3; matrix products, arithmetic and copies ran while one was open for 6% -> 0% of each run, Pallas kernels for 0% -> 0%
where the time goes in v1:
time: 40.8 us; the launch traced here: 40.2 us
  waiting for transfers between devices  10 us (25%)
  blocking collectives  9.92 us (24%)
  starting transfers between devices  7.93 us (19%)
  Pallas kernels  6.47 us (16%)
  local copies, waits for them, and re-layouts  5.73 us (14%)
    all_to_all x1, blocking collectives, body(): lax.all_to_all(answered, 'hor', split_axis=0, concat_axis=0, tiled=True)  9.92 us
    all_to_all x1, starting transfers between devices, body(): lax.all_to_all(outgoing, 'hor', split_axis=0, concat_axis=0, tiled=True)  7.34 us
    all_to_all x1, waiting for transfers between devices, body(): lax.all_to_all(outgoing, 'hor', split_axis=0, concat_axis=0, tiled=True)  7.33 us
    unnamed x36, local copies, waits for them, and re-layouts  5.73 us
    ppermute x2, waiting for transfers between devices, body(): recv = lax.ppermute(send, 'dep', pairs)  2.68 us
    pallas_call x1, Pallas kernels, body(): call(interior_kernel, 2, [whole(slab)] * 2 + [table_spec] * 2 + [sine_spe...  2.56 us
    pallas_call x1, Pallas kernels, body(): call(finish_kernel, 2, [whole(packed), whole(field), whole(field)] + [tab...  1.75 us
    pallas_call x1, Pallas kernels, body(): call(functools.partial(interface_kernel, chunk=chunk), 2, [whole(packed),...  1.12 us
  transfers between devices with their start and end apart: 3, of which 3 were waited for; matrix products, arithmetic and copies ran while one was open for 0% of the time, Pallas kernels for 0%

profile of v1, /device:TPU:0, one launch (start us, length us, event | category | flops | bytes accessed | tf_op | source)
XLA Modules:
  0.0 40.2 jit_solution(9969751332814983033)
XLA Ops:
  0.0 0.0 copy-start
  0.0 0.0 copy-start.3
  0.0 1.1 %copy-done.3 = s32[16,8,1024]{2,1,0:T(8,128)S(1)} copy-done((s32[16,8,1024]{2,1,0:T(8,128)S(1)}, s32[16,8,1024]{2,1,0:T(8,128)}, u32[]{:S(2)}) %copy-start.3) | copy-done | bytes 524312
  1.1 0.0 copy-start.5
  1.1 1.0 %copy-done.5 = f32[16,8,1024]{2,1,0:T(8,128)S(1)} copy-done((f32[16,8,1024]{2,1,0:T(8,128)S(1)}, f32[16,8,1024]{2,1,0:T(8,128)}, u32[]{:S(2)}) %copy-start.5) | copy-done | bytes 524312
  2.2 0.0 copy-start.14
  2.2 0.0 copy-start.15
  2.2 0.2 shard_map.136
  2.3 0.0 copy-start.17
  2.4 0.5 %collective-permute-start = (f32[16,8,512]{2,1,0:T(8,128)S(1)}, f32[16,8,512]{2,1,0:T(8,128)S(1)}, u32[]{:S(2)}, u32[]{:S(2)}) collective-permute-start(f32[16,8,512]{2,1,0:T(8,128)S(1)} %get-tuple-element.13), channel_id=1, source_target_pairs={{0,1},{1,0},{2,3},{3,2},{4,5},{5,4},{6,7},{7,6},{8,9},{9,8},{10,11... | collective-permute-start | bytes 786440 | tf_op jit(solution)/shard_map/ppermute | solution.py:507
  2.9 1.2 %collective-permute-done.recv_ref = f32[16,8,512]{2,1,0:T(8,128)S(1)} collective-permute-done((f32[16,8,512]{2,1,0:T(8,128)S(1)}, f32[16,8,512]{2,1,0:T(8,128)S(1)}, u32[]{:S(2)}, u32[]{:S(2)}) %collective-permute-start) | collective-permute-done | bytes 262176 | tf_op jit(solution)/shard_map/ppermute | solution.py:507
  4.0 0.0 copy-done
  4.0 0.0 copy-done.14
  4.0 0.0 copy-done.15
  4.0 0.0 copy-done.17
  4.1 0.0 copy-start.1
  4.1 1.2 %copy-done.1 = bf16[2,512,512]{2,1,0:T(8,128)(2,1)S(1)} copy-done((bf16[2,512,512]{2,1,0:T(8,128)(2,1)S(1)}, bf16[2,512,512]{2,1,0:T(8,128)(2,1)}, u32[]{:S(2)}) %copy-start.1) | copy-done | bytes 1048600
  5.3 0.0 copy-start.6
  5.3 0.8 %copy-done.6 = bf16[128,128]{1,0:T(8,128)(2,1)S(1)} copy-done((bf16[128,128]{1,0:T(8,128)(2,1)S(1)}, bf16[128,128]{1,0:T(8,128)(2,1)}, u32[]{:S(2)}) %copy-start.6) | copy-done | bytes 32792
  6.0 0.0 copy-start.8
  6.0 0.8 %copy-done.8 = bf16[128,128]{1,0:T(8,128)(2,1)S(1)} copy-done((bf16[128,128]{1,0:T(8,128)(2,1)S(1)}, bf16[128,128]{1,0:T(8,128)(2,1)}, u32[]{:S(2)}) %copy-start.8) | copy-done | bytes 32792
  6.8 0.0 copy-start.10
  6.8 0.8 %copy-done.10 = f32[2,8,512]{2,1,0:T(8,128)S(1)} copy-done((f32[2,8,512]{2,1,0:T(8,128)S(1)}, f32[2,8,512]{2,1,0:T(8,128)}, u32[]{:S(2)}) %copy-start.10) | copy-done | bytes 32792
  7.6 0.0 copy-start.2
  7.6 2.6 %shard_map.137 = (f32[8,32,128]{2,1,0:T(8,128)}, f32[32,8,512]{2,1,0:T(8,128)S(1)}, f32[32,8,512]{2,1,0:T(8,128)S(1)}) custom-call(s32[1]{0:T(128)} %bitcast.dep_ref, s32[32]{0:T(128)S(1)} %copy-done.17, f32[16,8,512]{2,1,0:T(8,128)S(1)} %get-tuple-element.12.own_ref, f32[16,8,512]{2,1,0:T(8,128)S(1)} %collective-permute-done.recv_ref, ...), custom_call_target="tpu_custom_call" | custom-call | tf_op jit(solution)/shard_map/pallas_call | solution.py:513
  10.1 0.0 copy-start.13
  10.1 7.3 %all-to-all-start = ((f32[8,32,128]{2,1,0:T(8,128)}), f32[8,32,128]{2,1,0:T(8,128)S(1)}, u32[]{:S(2)}, u32[]{:S(2)}) async-start(f32[8,32,128]{2,1,0:T(8,128)} %get-tuple-element.14), calls=%async_computation | async-start | bytes 262144 | tf_op jit(solution)/shard_map/all_to_all | solution.py:537
  17.5 0.0 copy-start.16
  17.5 7.3 %all-to-all-done.packed_ref = f32[8,32,128]{2,1,0:T(8,128)S(1)} async-done(((f32[8,32,128]{2,1,0:T(8,128)}), f32[8,32,128]{2,1,0:T(8,128)S(1)}, u32[]{:S(2)}, u32[]{:S(2)}) %all-to-all-start) | async-done | bytes 131104 | tf_op jit(solution)/shard_map/all_to_all | solution.py:537
  24.8 0.0 copy-done.13
  24.8 0.0 copy-done.16
  24.8 1.1 %shard_map.138 = f32[8,32,128]{2,1,0:T(8,128)S(1)} custom-call(s32[1]{0:T(128)} %bitcast.1.spot_ref, s32[32]{0:T(128)S(1)} %copy-done.17, f32[8,32,128]{2,1,0:T(8,128)S(1)} %all-to-all-done.packed_ref, f32[32,128]{1,0:T(8,128)S(1)} %copy-done.13, f32[16,128]{1,0:T(8,128)S(1)} %copy-done.16), custom_call_target="tpu_custom_call" | custom-call | tf_op jit(solution)/shard_map/pallas_call | solution.py:539
  25.9 0.0 copy-start.7
  26.0 0.0 copy-start.9
  26.0 0.0 copy-start.11
  26.0 0.0 copy-start.12
  26.0 9.9 %all_to_all.10.back_ref = f32[8,32,128]{2,1,0:T(8,128)S(1)} all-to-all(f32[8,32,128]{2,1,0:T(8,128)S(1)} %shard_map.138), channel_id=1, replica_groups=mesh['grp'=2,'hor'=8,'dep'=2] {'hor'}, dimensions={0} | all-to-all | bytes 262144 | tf_op jit(solution)/shard_map/all_to_all | solution.py:553
  35.9 0.0 copy-done.2
  35.9 0.0 copy-done.7
  35.9 0.0 copy-done.9
  35.9 0.0 copy-done.11
  35.9 0.0 copy-done.12
  35.9 0.0 copy-start.4
  36.0 1.8 %shard_map.139 = (f32[16,8,512]{2,1,0:T(8,128)S(1)}, f32[16,8,512]{2,1,0:T(8,128)S(1)}) custom-call(s32[1]{0:T(128)} %bitcast.dep_ref, s32[32]{0:T(128)S(1)} %copy-done.17, f32[8,32,128]{2,1,0:T(8,128)S(1)} %all_to_all.10.back_ref, f32[32,8,512]{2,1,0:T(8,128)S(1)} %get-tuple-element.15.source_ref, f32[32,8,512]{2,1,0:T(8,128)S(1)} %get-tuple-element.16.inverse_ref, ...), custom_call_target="tpu_custom_call" | custom-call | tf_op jit(solution)/shard_map/pallas_call | solution.py:554
  37.7 0.1 collective-permute-start.1
  37.8 1.5 %collective-permute-done.1.recv_ref = f32[16,8,512]{2,1,0:T(8,128)S(1)} collective-permute-done((f32[16,8,512]{2,1,0:T(8,128)S(1)}, f32[16,8,512]{2,1,0:T(8,128)S(1)}, u32[]{:S(2)}, u32[]{:S(2)}) %collective-permute-start.1) | collective-permute-done | bytes 262176 | tf_op jit(solution)/shard_map/ppermute | solution.py:577
  39.3 0.0 copy-done.4
  39.3 0.9 %shard_map.140 = f32[16,8,1024]{2,1,0:T(8,128)} custom-call(s32[1]{0:T(128)} %bitcast.dep_ref, f32[16,8,512]{2,1,0:T(8,128)S(1)} %get-tuple-element.17.own_ref, f32[16,8,512]{2,1,0:T(8,128)S(1)} %collective-permute-done.1.recv_ref, s32[16,8,1024]{2,1,0:T(8,128)S(1)} %copy-done.4), custom_call_target="tpu_custom_call" | custom-call | tf_op jit(solution)/shard_map/pallas_call | solution.py:578
Async XLA Ops:
  0.0 4.0 %copy-start = (bf16[2,512,512]{2,1,0:T(8,128)(2,1)S(1)}, bf16[2,512,512]{2,1,0:T(8,128)(2,1)}, u32[]{:S(2)}) copy-start(bf16[2,512,512]{2,1,0:T(8,128)(2,1)} %constant.33.clone.table_low) | copy-start | bytes 3145732
  0.0 1.1 %copy-start.3 = (s32[16,8,1024]{2,1,0:T(8,128)S(1)}, s32[16,8,1024]{2,1,0:T(8,128)}, u32[]{:S(2)}) copy-start(s32[16,8,1024]{2,1,0:T(8,128)} %bins_ref.3) | copy-start | bytes 1572868
  1.1 1.0 %copy-start.5 = (f32[16,8,1024]{2,1,0:T(8,128)S(1)}, f32[16,8,1024]{2,1,0:T(8,128)}, u32[]{:S(2)}) copy-start(f32[16,8,1024]{2,1,0:T(8,128)} %residual_ref.1) | copy-start | bytes 1572868
  2.2 1.9 %copy-start.14 = (bf16[32,128]{1,0:T(8,128)(2,1)S(1)}, bf16[32,128]{1,0:T(8,128)(2,1)}, u32[]{:S(2)}) copy-start(bf16[32,128]{1,0:T(8,128)(2,1)} %constant.37.clone.edge_low) | copy-start | bytes 24580
  2.2 1.9 %copy-start.15 = (bf16[32,128]{1,0:T(8,128)(2,1)S(1)}, bf16[32,128]{1,0:T(8,128)(2,1)}, u32[]{:S(2)}) copy-start(bf16[32,128]{1,0:T(8,128)(2,1)} %constant.36.clone.edge_high) | copy-start | bytes 24580
  2.3 1.7 %copy-start.17 = (s32[32]{0:T(128)S(1)}, s32[32]{0:T(128)}, u32[]{:S(2)}) copy-start(s32[32]{0:T(128)} %class_ref.5) | copy-start | bytes 388
  2.4 1.7 %collective-permute-start = (f32[16,8,512]{2,1,0:T(8,128)S(1)}, f32[16,8,512]{2,1,0:T(8,128)S(1)}, u32[]{:S(2)}, u32[]{:S(2)}) collective-permute-start(f32[16,8,512]{2,1,0:T(8,128)S(1)} %get-tuple-element.13), channel_id=1, source_target_pairs={{0,1},{1,0},{2,3},{3,2},{4,5},{5,4},{6,7},{7,6},{8,9},{9,8},{10,11... | collective-permute-start | bytes 786440 | tf_op jit(solution)/shard_map/ppermute | solution.py:507
  4.1 1.2 %copy-start.1 = (bf16[2,512,512]{2,1,0:T(8,128)(2,1)S(1)}, bf16[2,512,512]{2,1,0:T(8,128)(2,1)}, u32[]{:S(2)}) copy-start(bf16[2,512,512]{2,1,0:T(8,128)(2,1)} %constant.32.clone.table_high) | copy-start | bytes 3145732
  5.3 0.8 %copy-start.6 = (bf16[128,128]{1,0:T(8,128)(2,1)S(1)}, bf16[128,128]{1,0:T(8,128)(2,1)}, u32[]{:S(2)}) copy-start(bf16[128,128]{1,0:T(8,128)(2,1)} %constant.35.clone.sine_low) | copy-start | bytes 98308
  6.0 0.8 %copy-start.8 = (bf16[128,128]{1,0:T(8,128)(2,1)S(1)}, bf16[128,128]{1,0:T(8,128)(2,1)}, u32[]{:S(2)}) copy-start(bf16[128,128]{1,0:T(8,128)(2,1)} %constant.34.clone.sine_high) | copy-start | bytes 98308
  6.8 0.8 %copy-start.10 = (f32[2,8,512]{2,1,0:T(8,128)S(1)}, f32[2,8,512]{2,1,0:T(8,128)}, u32[]{:S(2)}) copy-start(f32[2,8,512]{2,1,0:T(8,128)} %constant.38.clone.wave_ref) | copy-start | bytes 98308
  7.6 28.4 %copy-start.2 = (bf16[2,512,512]{2,1,0:T(8,128)(2,1)S(1)}, bf16[2,512,512]{2,1,0:T(8,128)(2,1)}, u32[]{:S(2)}) copy-start(bf16[2,512,512]{2,1,0:T(8,128)(2,1)} %constant.32.clone.table_high) | copy-start | bytes 3145732
  10.1 14.7 %copy-start.13 = (f32[32,128]{1,0:T(8,128)S(1)}, f32[32,128]{1,0:T(8,128)}, u32[]{:S(2)}) copy-start(f32[32,128]{1,0:T(8,128)} %constant.39.clone.wave_y_ref) | copy-start | bytes 49156
  10.1 14.7 %all-to-all-start = ((f32[8,32,128]{2,1,0:T(8,128)}), f32[8,32,128]{2,1,0:T(8,128)S(1)}, u32[]{:S(2)}, u32[]{:S(2)}) async-start(f32[8,32,128]{2,1,0:T(8,128)} %get-tuple-element.14), calls=%async_computation | async-start | bytes 262144 | tf_op jit(solution)/shard_map/all_to_all | solution.py:537
  17.5 7.3 %copy-start.16 = (f32[16,128]{1,0:T(8,128)S(1)}, f32[16,128]{1,0:T(8,128)}, u32[]{:S(2)}) copy-start(f32[16,128]{1,0:T(8,128)} %constant.40.clone.wave_x_ref) | copy-start | bytes 24580
  25.9 10.0 %copy-start.7 = (bf16[128,128]{1,0:T(8,128)(2,1)S(1)}, bf16[128,128]{1,0:T(8,128)(2,1)}, u32[]{:S(2)}) copy-start(bf16[128,128]{1,0:T(8,128)(2,1)} %constant.35.clone.sine_low) | copy-start | bytes 98308
  26.0 10.0 %copy-start.9 = (bf16[128,128]{1,0:T(8,128)(2,1)S(1)}, bf16[128,128]{1,0:T(8,128)(2,1)}, u32[]{:S(2)}) copy-start(bf16[128,128]{1,0:T(8,128)(2,1)} %constant.34.clone.sine_high) | copy-start | bytes 98308
  26.0 10.0 %copy-start.11 = (f32[8,512]{1,0:T(8,128)S(1)}, f32[8,512]{1,0:T(8,128)}, u32[]{:S(2)}) copy-start(f32[8,512]{1,0:T(8,128)} %constant.42.clone.far_ref) | copy-start | bytes 49156
  26.0 10.0 %copy-start.12 = (f32[8,512]{1,0:T(8,128)S(1)}, f32[8,512]{1,0:T(8,128)}, u32[]{:S(2)}) copy-start(f32[8,512]{1,0:T(8,128)} %constant.41.clone.near_ref) | copy-start | bytes 49156
  35.9 3.4 %copy-start.4 = (s32[16,8,1024]{2,1,0:T(8,128)S(1)}, s32[16,8,1024]{2,1,0:T(8,128)}, u32[]{:S(2)}) copy-start(s32[16,8,1024]{2,1,0:T(8,128)} %bins_ref.3) | copy-start | bytes 1572868
  37.7 1.6 %collective-permute-start.1 = (f32[16,8,512]{2,1,0:T(8,128)S(1)}, f32[16,8,512]{2,1,0:T(8,128)S(1)}, u32[]{:S(2)}, u32[]{:S(2)}) collective-permute-start(f32[16,8,512]{2,1,0:T(8,128)S(1)} %get-tuple-element.18), channel_id=1, source_target_pairs={{0,1},{1,0},{2,3},{3,2},{4,5},{5,4},{6,7},{7,6},{8,9},{9,8},{10,11... | collective-permute-start | bytes 786440 | tf_op jit(solution)/shard_map/ppermute | solution.py:577

commit v2 on v1

--- a/solution.py
+++ b/solution.py
@@ -72,17 +72,29 @@
     return focus_base * jnp.exp(focus_step * focus_bins.astype(f32))
 
 
-def layer_terms(class_ref, layers, plane_tiles, axis):
-    weights = []
-    for layer in range(layers):
-        level = jnp.full((8, lanes), class_ref[layer], jnp.int32).astype(f32)
-        weights.append(weight_base * jnp.exp(weight_step * level))
+def layer_weights(class_ref, weight_ref):
+    for layer in range(weight_ref.shape[0]):
+        level = jnp.full(weight_ref.shape[1:], class_ref[layer], jnp.int32).astype(f32)
+        weight_ref[layer] = weight_base * jnp.exp(weight_step * level)
+
+
+def layer_terms(weight_ref, plane_tiles, axis):
+    layers = weight_ref.shape[0]
+    weights = [weight_ref[layer] for layer in range(layers)]
     couple = [coupling_scale * weights[k] * weights[k + 1] for k in range(layers - 1)]
 
     def spread(values):
         return [jnp.concatenate([value] * plane_tiles, axis=axis) for value in values]
 
     return spread(weights), spread(couple)
+
+
+def row_values(values, shape):
+    row = lax.broadcasted_iota(jnp.int32, shape, 0)
+    total = jnp.full(shape, float(values[0]), f32)
+    for index in range(1, len(values)):
+        total = jnp.where(row == index, float(values[index]), total)
+    return total
 
 
 def diagonal(layer, weights, couple, wave):
@@ -149,64 +161,146 @@
     return values if shift == 0 else pltpu.roll(values, shift, values.ndim - 1)
 
 
-def fold_kernel(dep_ref, residual_ref, bins_ref, own_ref, send_ref):
-    half = own_ref.shape[-1]
+def fold_kernel(
+    dep_ref,
+    residual_hbm,
+    bins_hbm,
+    class_hbm,
+    own_ref,
+    send_ref,
+    weight_ref,
+    residual_ref,
+    bins_ref,
+    class_ref,
+    sems,
+    class_sem,
+    *,
+    cuts,
+):
+    depth, _, half = own_ref.shape
+    size = depth // cuts
+    class_copy = pltpu.make_async_copy(class_hbm, class_ref, class_sem)
+    class_copy.start()
+    copies = []
+    for cut in range(cuts):
+        part = pl.ds(cut * size, size)
+        first = pltpu.make_async_copy(bins_hbm.at[part], bins_ref.at[part], sems.at[0, cut])
+        second = pltpu.make_async_copy(
+            residual_hbm.at[part], residual_ref.at[part], sems.at[1, cut]
+        )
+        first.start()
+        second.start()
+        copies.append((first, second))
     sign = jnp.where(dep_ref[0] == 0, 1.0, -1.0).astype(f32)
-    scaled = focusing(bins_ref[...]) * residual_ref[...]
-    left = scaled[..., :half]
-    right = sign * scaled[..., half:]
-    own_ref[...] = left + right
-    send_ref[...] = left - right
+    class_copy.wait()
+    layer_weights(class_ref, weight_ref)
+    for cut in range(cuts):
+        part = pl.ds(cut * size, size)
+        copies[cut][0].wait()
+        focus_map = focusing(bins_ref[part])
+        copies[cut][1].wait()
+        scaled = focus_map * residual_ref[part]
+        left = scaled[..., :half]
+        right = sign * scaled[..., half:]
+        own_ref[part] = left + right
+        send_ref[part] = left - right
+
+
+def to_modes(cells, table, sine):
+    depth, rows, half = cells.shape
+    waves = dot3(split(cells.reshape(depth * rows, half)), table)
+    return dot3(sine, split(waves)).reshape(depth, rows, half)
+
+
+def from_modes(modes, sine):
+    depth, rows, half = modes.shape
+    return dot3(sine, split(modes.reshape(depth * rows, half)))
+
+
+def parts_of(small_ref, block, depth):
+    cuts = np.cumsum([0, block, block, 2 * depth, 2 * depth])
+    pieces = [small_ref[low:high] for low, high in zip(cuts[:-1], cuts[1:])]
+    return (pieces[0], pieces[1]), (pieces[2], pieces[3])
+
+
+def prepare_kernel(
+    dep_ref,
+    spot_ref,
+    own_ref,
+    weight_ref,
+    table_hbm,
+    small_hbm,
+    inner_hbm,
+    outer_hbm,
+    modes_ref,
+    table_ref,
+    small_ref,
+    inverse_ref,
+    inverse_outer_ref,
+    inner_ref,
+    outer_ref,
+    sems,
+):
+    depth, rows, half = own_ref.shape
+    plane_rows = inverse_outer_ref.shape[1]
+    dep = dep_ref[0]
+    copies = [
+        pltpu.make_async_copy(inner_hbm.at[dep], inner_ref, sems.at[0]),
+        pltpu.make_async_copy(outer_hbm, outer_ref, sems.at[1]),
+        pltpu.make_async_copy(small_hbm, small_ref, sems.at[2]),
+        pltpu.make_async_copy(table_hbm.at[dep, 0], table_ref.at[0], sems.at[3]),
+        pltpu.make_async_copy(table_hbm.at[dep, 1], table_ref.at[1], sems.at[4]),
+    ]
+    for copy in copies:
+        copy.start()
+    copies[0].wait()
+    copies[1].wait()
+    weights, couple = layer_terms(weight_ref, half // lanes, 1)
+    factor(weights, couple, inner_ref[...], inverse_ref)
+    weights, couple = layer_terms(weight_ref, plane_rows // 8, 0)
+    wave = outer_ref[:plane_rows] + outer_ref[pl.ds(plane_rows + spot_ref[0], 1), :]
+    factor(weights, couple, damping + smoothing * wave, inverse_outer_ref)
+    for copy in copies[2:]:
+        copy.wait()
+    sine, _ = parts_of(small_ref, depth * rows, depth)
+    modes_ref[...] = to_modes(own_ref[...], (table_ref[0], table_ref[1]), sine)
 
 
 def interior_kernel(
     dep_ref,
-    class_ref,
-    own_ref,
+    modes_ref,
     recv_ref,
-    table_high,
-    table_low,
-    sine_high,
-    sine_low,
-    edge_high,
-    edge_low,
-    wave_ref,
+    table_ref,
+    small_ref,
+    weight_ref,
+    inverse_ref,
     packed_ref,
     source_ref,
-    inverse_ref,
     stage_ref,
     partial_ref,
 ):
-    depth, rows, half = own_ref.shape
+    depth, rows, half = recv_ref.shape
     layers = 2 * depth
+    block = depth * rows
     hor_count = packed_ref.shape[0]
     chunk = half // hor_count
     place = dep_ref[0] * depth
-    stage_ref[pl.ds(place, depth)] = own_ref[...]
-    stage_ref[pl.ds(depth - place, depth)] = recv_ref[...]
-    weights, couple = layer_terms(class_ref, layers, half // lanes, 1)
-    factor(weights, couple, wave_ref[0], inverse_ref)
-    cells = stage_ref[...].reshape(layers * rows, half)
-    waves = dot3(split(cells), (table_high[0], table_low[0]))
-    block = depth * rows
-    sine = (sine_high[...], sine_low[...])
-    for part in range(2):
-        piece = waves[part * block : (part + 1) * block]
-        source_ref[part * depth : (part + 1) * depth] = dot3(sine, split(piece)).reshape(
-            depth, rows, half
-        )
+    sine, edge = parts_of(small_ref, block, depth)
+    source_ref[pl.ds(place, depth)] = modes_ref[...]
+    source_ref[pl.ds(depth - place, depth)] = to_modes(
+        recv_ref[...], (table_ref[0], table_ref[1]), sine
+    )
+    weights, couple = layer_terms(weight_ref, half // lanes, 1)
     edge_row = lax.broadcasted_iota(jnp.int32, (rows, half), 0) == 0
 
     def emit(layer, values):
         stage_ref[layer] = jnp.where(edge_row, source_ref[layer], weights[layer] * values)
 
     substitute(couple, inverse_ref, partial_ref, lambda layer: source_ref[layer], emit)
-    edge = (edge_high[...], edge_low[...])
     lower = []
     upper = []
     for part in range(2):
-        piece = stage_ref[part * depth : (part + 1) * depth].reshape(block, half)
-        both = dot3(edge, split(piece))
+        both = from_modes(stage_ref[part * depth : (part + 1) * depth], edge)
         lower.append(both[:depth])
         upper.append(both[depth:])
     lower = jnp.concatenate(lower, axis=0)
@@ -255,22 +349,19 @@
 
 
 def interface_kernel(
-    spot_ref,
-    class_ref,
     packed_ref,
-    wave_y_ref,
-    wave_x_ref,
+    weight_ref,
+    inverse_ref,
     back_ref,
     sum_ref,
     wave_ref,
     answer_ref,
-    inverse_ref,
     partial_ref,
     *,
     chunk,
 ):
     hor_count, layers, _ = packed_ref.shape
-    rows = wave_y_ref.shape[0]
+    rows = inverse_ref.shape[1]
     subsets = lanes // chunk
     classes = max(1, hor_count // rows)
     repeats = max(1, rows // hor_count)
@@ -305,9 +396,7 @@
             lambda k, v: wave_ref.__setitem__(k, v),
             (layers, lanes),
         )
-    weights, couple = layer_terms(class_ref, layers, rows // 8, 0)
-    wave = damping + smoothing * (wave_y_ref[...] + wave_x_ref[pl.ds(spot_ref[0], 1), :])
-    factor(weights, couple, wave, inverse_ref)
+    weights, couple = layer_terms(weight_ref, rows // 8, 0)
     plane_lane = lax.broadcasted_iota(jnp.int32, (rows, lanes), 1)
     group = plane_lane // chunk % classes
 
@@ -360,22 +449,21 @@
 
 def finish_kernel(
     dep_ref,
-    class_ref,
     back_ref,
     source_ref,
+    table_ref,
+    small_ref,
+    weight_ref,
     inverse_ref,
-    table_high,
-    table_low,
-    sine_high,
-    sine_low,
-    near_ref,
-    far_ref,
-    own_ref,
     send_ref,
+    waves_ref,
     left_ref,
     right_ref,
     stage_ref,
     partial_ref,
+    *,
+    near_values,
+    far_values,
 ):
     layers, rows, half = source_ref.shape
     depth = layers // 2
@@ -395,9 +483,9 @@
             right = right_part if right is None else jnp.where(inside, right_part, right)
         left_ref[:, tile * lanes : (tile + 1) * lanes] = left
         right_ref[:, tile * lanes : (tile + 1) * lanes] = right
-    weights, couple = layer_terms(class_ref, layers, half // lanes, 1)
-    near = near_ref[...]
-    far = far_ref[...]
+    weights, couple = layer_terms(weight_ref, half // lanes, 1)
+    near = row_values(near_values, (rows, half))
+    far = row_values(far_values, (rows, half))
     edge_row = lax.broadcasted_iota(jnp.int32, (rows, half), 0) == 0
 
     def row_of(ref, layer):
@@ -411,47 +499,61 @@
         stage_ref[layer] = jnp.where(edge_row, row_of(left_ref, layer), values)
 
     substitute(couple, inverse_ref, partial_ref, source, emit)
-    block = depth * rows
-    sine = (sine_high[...], sine_low[...])
-    parts = []
-    for part in range(2):
-        piece = stage_ref[part * depth : (part + 1) * depth].reshape(block, half)
-        parts.append(dot3(sine, split(piece)))
-    waves = jnp.concatenate(parts, axis=0)
-    cells = dot3(split(waves), (table_high[0], table_low[0]), (((1,), (1,)), ((), ())))
-    stage_ref[...] = cells.reshape(layers, rows, half)
     place = dep_ref[0] * depth
-    own_ref[...] = stage_ref[pl.ds(place, depth)]
-    send_ref[...] = stage_ref[pl.ds(depth - place, depth)]
-
-
-def unfold_kernel(dep_ref, own_ref, recv_ref, bins_ref, out_ref, *, scale):
-    half = own_ref.shape[-1]
+    sine, _ = parts_of(small_ref, depth * rows, depth)
+    waves = from_modes(stage_ref[pl.ds(depth - place, depth)], sine)
+    cells = dot3(split(waves), (table_ref[0], table_ref[1]), (((1,), (1,)), ((), ())))
+    send_ref[...] = cells.reshape(depth, rows, half)
+    waves_ref[...] = stage_ref[pl.ds(place, depth)]
+
+
+def restore_kernel(waves_ref, bins_ref, table_ref, small_ref, own_ref, focus_ref):
+    depth, rows, half = own_ref.shape
+    focus_ref[...] = focusing(bins_ref[...])
+    sine, _ = parts_of(small_ref, depth * rows, depth)
+    waves = from_modes(waves_ref[...], sine)
+    cells = dot3(split(waves), (table_ref[0], table_ref[1]), (((1,), (1,)), ((), ())))
+    own_ref[...] = cells.reshape(depth, rows, half)
+
+
+def unfold_kernel(dep_ref, own_ref, recv_ref, focus_ref, out_hbm, out_ref, sems, *, scale, cuts):
+    depth, _, half = own_ref.shape
+    size = depth // cuts
     sign = jnp.where(dep_ref[0] == 0, scale, -scale).astype(f32)
-    focus_map = focusing(bins_ref[...])
-    own = own_ref[...]
-    recv = recv_ref[...]
-    out_ref[..., :half] = focus_map[..., :half] * ((own + recv) * scale)
-    out_ref[..., half:] = focus_map[..., half:] * ((own - recv) * sign)
-
-
-def whole(shape):
-    return pl.BlockSpec(shape, lambda i, *_: (0,) * len(shape))
-
-
-def call(kernel, scalars, in_specs, out_specs, out_shape, scratch=(), grid=(1,)):
+    copies = []
+    for cut in range(cuts):
+        part = pl.ds(cut * size, size)
+        own = own_ref[part]
+        recv = recv_ref[part]
+        focus_map = focus_ref[part]
+        out_ref[part, :, :half] = focus_map[..., :half] * ((own + recv) * scale)
+        out_ref[part, :, half:] = focus_map[..., half:] * ((own - recv) * sign)
+        copy = pltpu.make_async_copy(out_ref.at[part], out_hbm.at[part], sems.at[cut])
+        copy.start()
+        copies.append(copy)
+    for copy in copies:
+        copy.wait()
+
+
+def call(kernel, operands, out_shape, scratch=(), outside=False):
+    specs = []
+    values = []
+    for space, value in operands:
+        specs.append(pl.BlockSpec(memory_space=space))
+        if space is pltpu.HBM:
+            value = pltpu.with_memory_space_constraint(value, pltpu.HBM)
+        values.append(value)
+    out_space = pltpu.HBM if outside else pltpu.VMEM
+    single = not isinstance(out_shape, list)
+    out_specs = pl.BlockSpec(memory_space=out_space)
     return pl.pallas_call(
         kernel,
-        grid_spec=pltpu.PrefetchScalarGridSpec(
-            num_scalar_prefetch=scalars,
-            grid=grid,
-            in_specs=in_specs,
-            out_specs=out_specs,
-            scratch_shapes=list(scratch),
-        ),
+        in_specs=specs,
+        out_specs=out_specs if single else [out_specs] * len(out_shape),
         out_shape=out_shape,
+        scratch_shapes=list(scratch),
         compiler_params=pltpu.CompilerParams(vmem_limit_bytes=48 * 1024 * 1024),
-    )
+    )(*values)
 
 
 def body(residual, focus_bins, layer_class):
@@ -467,122 +569,110 @@
     dep_index = dep.reshape(1)
     spot = (hor * 2 + dep).reshape(1)
 
-    table_high, table_low = fold_tables(x_cells)
+    table = np.stack(fold_tables(x_cells), axis=1)
     sine = sine_matrix(rows)
-    sine_high, sine_low = split_table(np.kron(np.eye(depth), sine))
+    near = np.concatenate([[0.0], sine[1, 1:]])
+    far = np.concatenate([[0.0], sine[rows - 1, 1:]])
     lower_row = np.concatenate([[1.0], sine[1, 1:]])
-    upper_row = np.concatenate([[0.0], sine[rows - 1, 1:]])
-    edge_high, edge_low = split_table(
-        np.concatenate([np.kron(np.eye(depth), row[None, :]) for row in (lower_row, upper_row)])
-    )
+    edge = np.concatenate([np.kron(np.eye(depth), row[None, :]) for row in (lower_row, far)])
+    small = np.concatenate(split_table(np.kron(np.eye(depth), sine)) + split_table(edge))
     wave_x = np.stack(
         [symbol_of(2.0 * np.pi * (2 * np.arange(half) + parity) / x_cells) for parity in range(2)]
     )
     mode = symbol_of(np.pi * np.arange(rows) / rows)
-    wave_inner = damping + smoothing * (mode[None, :, None] + wave_x[:, None, :])
-    wave_inner = wave_inner.astype(np.float32)
-    near = np.broadcast_to((lower_row * (np.arange(rows) > 0))[:, None], (rows, half))
-    far = np.broadcast_to(upper_row[:, None], (rows, half))
+    inner = damping + smoothing * (mode[None, :, None] + wave_x[:, None, :])
     lane = np.arange(lanes)
     wave_number = (lane // chunk)[None, :] * plane_rows + np.arange(plane_rows)[:, None]
-    wave_y = symbol_of(2.0 * np.pi * wave_number / y_cells).astype(np.float32)
+    wave_y = symbol_of(2.0 * np.pi * wave_number / y_cells)
     spots = np.arange(hor_count)[:, None, None] * chunk + (lane % chunk)[None, None, :]
     spots = 2 * spots + np.arange(2)[None, :, None]
     wave_spots = symbol_of(2.0 * np.pi * spots / x_cells).reshape(2 * hor_count, lanes)
+    outer = np.concatenate([wave_y, wave_spots]).astype(np.float32)
 
     def shape(*dims):
         return jax.ShapeDtypeStruct(dims, f32)
 
+    def constant(value):
+        return (pltpu.HBM, jnp.asarray(value))
+
+    def scalar(value):
+        return (pltpu.SMEM, value)
+
+    def near_by(value):
+        return (pltpu.VMEM, value)
+
     slab = (depth, rows, half)
+    full = (depth, rows, x_cells)
     field = (layers, rows, half)
     packed = (hor_count, layers, lanes)
-    steps = 2
-    piece = depth // steps
-    cut = pl.BlockSpec((piece, rows, x_cells), lambda i, *_: (i, 0, 0))
-    cut_half = pl.BlockSpec((piece, rows, half), lambda i, *_: (i, 0, 0))
-    own, send = call(
-        fold_kernel, 1, [cut, cut], [cut_half, cut_half], [shape(*slab)] * 2, grid=(steps,)
-    )(dep_index, residual, focus_bins)
+    plane = (layers, plane_rows, lanes)
+    cuts = 4
+    own, send, weight = call(
+        functools.partial(fold_kernel, cuts=cuts),
+        [scalar(dep_index)]
+        + [(pltpu.HBM, value) for value in (residual, focus_bins, layer_class)],
+        [shape(*slab), shape(*slab), shape(layers, 8, lanes)],
+        [
+            pltpu.VMEM(full, f32),
+            pltpu.VMEM(full, jnp.int32),
+            pltpu.SMEM((layers,), jnp.int32),
+            pltpu.SemaphoreType.DMA((2, cuts)),
+            pltpu.SemaphoreType.DMA,
+        ],
+    )
     pairs = [(0, 1), (1, 0)]
     recv = lax.ppermute(send, "dep", pairs)
-
-    table_spec = pl.BlockSpec((1, half, half), lambda i, dep_ref, *_: (dep_ref[0], 0, 0))
-    sine_spec = whole(sine_high.shape)
-    edge_spec = whole(edge_high.shape)
-    wave_spec = pl.BlockSpec((1, rows, half), lambda i, dep_ref, *_: (dep_ref[0], 0, 0))
-    outgoing, source, inverse = call(
+    modes, table_here, small_here, inverse, inverse_outer = call(
+        prepare_kernel,
+        [scalar(dep_index), scalar(spot), near_by(own), near_by(weight)]
+        + [constant(value) for value in (table, small, inner.astype(np.float32), outer)],
+        [
+            shape(*slab),
+            jax.ShapeDtypeStruct((2, half, half), bf16),
+            jax.ShapeDtypeStruct(small.shape, bf16),
+            shape(*field),
+            shape(*plane),
+        ],
+        [
+            pltpu.VMEM((rows, half), f32),
+            pltpu.VMEM(outer.shape, f32),
+            pltpu.SemaphoreType.DMA((5,)),
+        ],
+    )
+    shared = [near_by(value) for value in (table_here, small_here, weight, inverse)]
+    outgoing, source = call(
         interior_kernel,
-        2,
-        [whole(slab)] * 2
-        + [table_spec] * 2
-        + [sine_spec] * 2
-        + [edge_spec] * 2
-        + [wave_spec],
-        [whole(packed), whole(field), whole(field)],
-        [shape(*packed), shape(*field), shape(*field)],
+        [scalar(dep_index), near_by(modes), near_by(recv)] + shared,
+        [shape(*packed), shape(*field)],
         [pltpu.VMEM(field, f32)] * 2,
-    )(
-        dep_index,
-        layer_class,
-        own,
-        recv,
-        jnp.asarray(table_high),
-        jnp.asarray(table_low),
-        jnp.asarray(sine_high),
-        jnp.asarray(sine_low),
-        jnp.asarray(edge_high),
-        jnp.asarray(edge_low),
-        jnp.asarray(wave_inner),
     )
     incoming = lax.all_to_all(outgoing, "hor", split_axis=0, concat_axis=0, tiled=True)
-    plane = (layers, plane_rows, lanes)
     answered = call(
         functools.partial(interface_kernel, chunk=chunk),
-        2,
-        [whole(packed), whole(wave_y.shape), whole(wave_spots.shape)],
-        whole(packed),
+        [near_by(incoming), near_by(weight), near_by(inverse_outer)],
         shape(*packed),
-        [pltpu.VMEM(packed, f32)] * 3 + [pltpu.VMEM(plane, f32)] * 2,
-    )(
-        spot,
-        layer_class,
-        incoming,
-        jnp.asarray(wave_y),
-        jnp.asarray(wave_spots.astype(np.float32)),
+        [pltpu.VMEM(packed, f32)] * 3 + [pltpu.VMEM(plane, f32)],
     )
     edges = lax.all_to_all(answered, "hor", split_axis=0, concat_axis=0, tiled=True)
-    own, send = call(
-        finish_kernel,
-        2,
-        [whole(packed), whole(field), whole(field)]
-        + [table_spec] * 2
-        + [sine_spec] * 2
-        + [whole((rows, half))] * 2,
-        [whole(slab)] * 2,
+    send, waves = call(
+        functools.partial(finish_kernel, near_values=near, far_values=far),
+        [scalar(dep_index), near_by(edges), near_by(source)] + shared,
         [shape(*slab)] * 2,
         [pltpu.VMEM((layers, half), f32)] * 2 + [pltpu.VMEM(field, f32)] * 2,
-    )(
-        dep_index,
-        layer_class,
-        edges,
-        source,
-        inverse,
-        jnp.asarray(table_high),
-        jnp.asarray(table_low),
-        jnp.asarray(sine_high),
-        jnp.asarray(sine_low),
-        jnp.asarray(near.astype(np.float32)),
-        jnp.asarray(far.astype(np.float32)),
     )
     recv = lax.ppermute(send, "dep", pairs)
+    own, focus_map = call(
+        restore_kernel,
+        [near_by(value) for value in (waves, focus_bins, table_here, small_here)],
+        [shape(*slab), shape(*full)],
+    )
     return call(
-        functools.partial(unfold_kernel, scale=1.0 / x_cells),
-        1,
-        [cut_half, cut_half, cut],
-        cut,
-        shape(depth, rows, x_cells),
-        grid=(steps,),
-    )(dep_index, own, recv, focus_bins)
+        functools.partial(unfold_kernel, scale=1.0 / x_cells, cuts=cuts),
+        [scalar(dep_index)] + [near_by(value) for value in (own, recv, focus_map)],
+        shape(*full),
+        [pltpu.VMEM(full, f32), pltpu.SemaphoreType.DMA((cuts,))],
+        outside=True,
+    )
 
 
 def solution(mesh):

time: 40.8 us -> 33.7 us (0.83)
  blocking collectives: 9.92 us -> 24.3 us
  waiting for transfers between devices: 10 us -> 0.58 us
  starting transfers between devices: 7.93 us -> 0.59 us
  local copies, waits for them, and re-layouts: 5.73 us -> 0.01 us
  Pallas kernels: 6.47 us -> 7.84 us
    all_to_all x0 -> x1, blocking collectives: none -> 14.4 us  [body(): lax.all_to_all(outgoing, 'hor', split_axis=0, concat_axis=0, tiled=True)]
    all_to_all x1 -> x0, starting transfers between devices: 7.34 us -> none  [body(): lax.all_to_all(outgoing, 'hor', split_axis=0, concat_axis=0, tiled=True)]
    all_to_all x1 -> x0, waiting for transfers between devices: 7.33 us -> none  [body(): lax.all_to_all(outgoing, 'hor', split_axis=0, concat_axis=0, tiled=True)]
    unnamed x36 -> x2, local copies, waits for them, and re-layouts: 5.73 us -> 0.01 us
    ppermute x2, waiting for transfers between devices: 2.68 us -> 0.58 us  [body(): recv = lax.ppermute(send, 'dep', pairs)]
    pallas_call x5 -> x7, Pallas kernels: 6.47 us -> 7.84 us  [call(): pl.pallas_call(kernel, in_specs=specs, out_specs=out_specs if single else...]
  transfers between devices with their start and end apart: 3 -> 2, of which waited for: 3 -> 1; matrix products, arithmetic and copies ran while one was open for 0% -> 0% of each run, Pallas kernels for 0% -> 9%
where the time goes in v2:
time: 33.7 us; the launch traced here: 33.4 us
  blocking collectives  24.3 us (72%)
  Pallas kernels  7.84 us (23%)
  starting transfers between devices  0.59 us (2%)
  waiting for transfers between devices  0.58 us (2%)
    all_to_all x1, blocking collectives, body(): lax.all_to_all(outgoing, 'hor', split_axis=0, concat_axis=0, tiled=True)  14.4 us
    all_to_all x1, blocking collectives, body(): lax.all_to_all(answered, 'hor', split_axis=0, concat_axis=0, tiled=True)  9.85 us
    pallas_call x7, Pallas kernels, call(): pl.pallas_call(kernel, in_specs=specs, out_specs=out_specs if single else...  7.84 us
  transfers between devices with their start and end apart: 2, of which 1 were waited for; matrix products, arithmetic and copies ran while one was open for 0% of the time, Pallas kernels for 9%

profile of v2, /device:TPU:0, one launch (start us, length us, event | category | flops | bytes accessed | tf_op | source)
XLA Modules:
  0.0 33.4 jit_solution(17730688349697399184)
XLA Ops:
  0.0 1.4 %shard_map.73 = (f32[16,8,512]{2,1,0:T(8,128)S(1)}, f32[16,8,512]{2,1,0:T(8,128)S(1)}, f32[32,8,128]{2,1,0:T(8,128)S(1)}) custom-call(s32[1]{0:T(128)} %bitcast.dep_ref, f32[16,8,1024]{2,1,0:T(8,128)} %residual_hbm.1, s32[16,8,1024]{2,1,0:T(8,128)} %bins_ref.1, s32[32]{0:T(128)} %class_hbm.1), custom_call_target="tpu_custom_call" | custom-call | tf_op jit(solution)/shard_map/pallas_call | solution.py:549
  1.4 0.5 %collective-permute-start = (f32[16,8,512]{2,1,0:T(8,128)S(1)}, f32[16,8,512]{2,1,0:T(8,128)S(1)}, u32[]{:S(2)}, u32[]{:S(2)}) collective-permute-start(f32[16,8,512]{2,1,0:T(8,128)S(1)} %get-tuple-element.22), channel_id=1, source_target_pairs={{0,1},{1,0},{2,3},{3,2},{4,5},{5,4},{6,7},{7,6},{8,9},{9,8},{10,11... | collective-permute-start | bytes 786440 | tf_op jit(solution)/shard_map/ppermute | solution.py:624
  1.9 2.0 %shard_map.74 = (f32[16,8,512]{2,1,0:T(8,128)S(1)}, bf16[2,512,512]{2,1,0:T(8,128)(2,1)S(1)}, bf16[320,128]{1,0:T(8,128)(2,1)S(1)}, f32[32,8,512]{2,1,0:T(8,128)S(1)}, f32[32,32,128]{2,1,0:T(8,128)S(1)}) custom-call(s32[1]{0:T(128)} %bitcast.dep_ref, s32[1]{0:T(128)} %bitcast.1.spot_ref, f32[16,8,512]{2,1,0:T(8,128)S(1)} %get-tuple-element.19.own_ref, ...), custom_call_target="tpu_custom_call" | custom-call | tf_op jit(solution)/shard_map/pallas_call | solution.py:549
  3.9 0.0 collective-permute-done.recv_ref
  3.9 1.1 %shard_map.75 = (f32[8,32,128]{2,1,0:T(8,128)S(1)}, f32[32,8,512]{2,1,0:T(8,128)S(1)}) custom-call(s32[1]{0:T(128)} %bitcast.dep_ref, f32[16,8,512]{2,1,0:T(8,128)S(1)} %get-tuple-element.21.modes_ref, f32[16,8,512]{2,1,0:T(8,128)S(1)} %collective-permute-done.recv_ref, bf16[2,512,512]{2,1,0:T(8,128)(2,1)S(1)} %get-tuple-element.23.table_ref, ...), custom_call_target="tpu_custom_call" | custom-call | tf_op jit(solution)/shard_map/pallas_call | solution.py:549
  5.0 0.0 copy-start
  5.0 14.4 %all_to_all.10.packed_ref = f32[8,32,128]{2,1,0:T(8,128)S(1)} all-to-all(f32[8,32,128]{2,1,0:T(8,128)S(1)} %get-tuple-element.26), channel_id=1, replica_groups=mesh['grp'=2,'hor'=8,'dep'=2] {'hor'}, dimensions={0} | all-to-all | bytes 262144 | tf_op jit(solution)/shard_map/all_to_all | solution.py:649
  19.4 0.5 %shard_map.76 = f32[8,32,128]{2,1,0:T(8,128)S(1)} custom-call(f32[8,32,128]{2,1,0:T(8,128)S(1)} %all_to_all.10.packed_ref, f32[32,8,128]{2,1,0:T(8,128)S(1)} %get-tuple-element.20.weight_ref, f32[32,32,128]{2,1,0:T(8,128)S(1)} %get-tuple-element.27.inverse_ref), custom_call_target="tpu_custom_call" | custom-call | tf_op jit(solution)/shard_map/pallas_call | solution.py:549
  19.9 9.9 %all_to_all.11.back_ref = f32[8,32,128]{2,1,0:T(8,128)S(1)} all-to-all(f32[8,32,128]{2,1,0:T(8,128)S(1)} %shard_map.76), channel_id=1, replica_groups=mesh['grp'=2,'hor'=8,'dep'=2] {'hor'}, dimensions={0} | all-to-all | bytes 262144 | tf_op jit(solution)/shard_map/all_to_all | solution.py:656
  29.7 1.2 %shard_map.77 = (f32[16,8,512]{2,1,0:T(8,128)S(1)}, f32[16,8,512]{2,1,0:T(8,128)S(1)}) custom-call(s32[1]{0:T(128)} %bitcast.dep_ref, f32[8,32,128]{2,1,0:T(8,128)S(1)} %all_to_all.11.back_ref, f32[32,8,512]{2,1,0:T(8,128)S(1)} %get-tuple-element.28.source_ref, bf16[2,512,512]{2,1,0:T(8,128)(2,1)S(1)} %get-tuple-element.23.table_ref, ...), custom_call_target="tpu_custom_call" | custom-call | tf_op jit(solution)/shard_map/pallas_call | solution.py:549
  30.9 0.1 collective-permute-start.1
  31.0 0.0 copy-done
  31.0 0.9 %shard_map.78 = (f32[16,8,512]{2,1,0:T(8,128)S(1)}, f32[16,8,1024]{2,1,0:T(8,128)S(1)}) custom-call(f32[16,8,512]{2,1,0:T(8,128)S(1)} %get-tuple-element.29.waves_ref, s32[16,8,1024]{2,1,0:T(8,128)S(1)} %copy-done, bf16[2,512,512]{2,1,0:T(8,128)(2,1)S(1)} %get-tuple-element.23.table_ref, bf16[320,128]{1,0:T(8,128)(2,1)S(1)} %get-tuple-element.24.small_ref), custom_call_target="tpu_custom_call" | custom-call | tf_op jit(solution)/shard_map/pallas_call | solution.py:549
  31.9 0.6 %collective-permute-done.1.recv_ref = f32[16,8,512]{2,1,0:T(8,128)S(1)} collective-permute-done((f32[16,8,512]{2,1,0:T(8,128)S(1)}, f32[16,8,512]{2,1,0:T(8,128)S(1)}, u32[]{:S(2)}, u32[]{:S(2)}) %collective-permute-start.1) | collective-permute-done | bytes 262176 | tf_op jit(solution)/shard_map/ppermute | solution.py:663
  32.5 0.8 %shard_map.79 = f32[16,8,1024]{2,1,0:T(8,128)} custom-call(s32[1]{0:T(128)} %bitcast.dep_ref, f32[16,8,512]{2,1,0:T(8,128)S(1)} %get-tuple-element.30.own_ref, f32[16,8,512]{2,1,0:T(8,128)S(1)} %collective-permute-done.1.recv_ref, f32[16,8,1024]{2,1,0:T(8,128)S(1)} %get-tuple-element.32.focus_ref), custom_call_target="tpu_custom_call" | custom-call | tf_op jit(solution)/shard_map/pallas_call | solution.py:549
Async XLA Ops:
  1.4 2.5 %collective-permute-start = (f32[16,8,512]{2,1,0:T(8,128)S(1)}, f32[16,8,512]{2,1,0:T(8,128)S(1)}, u32[]{:S(2)}, u32[]{:S(2)}) collective-permute-start(f32[16,8,512]{2,1,0:T(8,128)S(1)} %get-tuple-element.22), channel_id=1, source_target_pairs={{0,1},{1,0},{2,3},{3,2},{4,5},{5,4},{6,7},{7,6},{8,9},{9,8},{10,11... | collective-permute-start | bytes 786440 | tf_op jit(solution)/shard_map/ppermute | solution.py:624
  5.0 26.0 %copy-start = (s32[16,8,1024]{2,1,0:T(8,128)S(1)}, s32[16,8,1024]{2,1,0:T(8,128)}, u32[]{:S(2)}) copy-start(s32[16,8,1024]{2,1,0:T(8,128)} %bins_ref.1) | copy-start | bytes 1572868
  30.9 1.6 %collective-permute-start.1 = (f32[16,8,512]{2,1,0:T(8,128)S(1)}, f32[16,8,512]{2,1,0:T(8,128)S(1)}, u32[]{:S(2)}, u32[]{:S(2)}) collective-permute-start(f32[16,8,512]{2,1,0:T(8,128)S(1)} %get-tuple-element.31), channel_id=1, source_target_pairs={{0,1},{1,0},{2,3},{3,2},{4,5},{5,4},{6,7},{7,6},{8,9},{9,8},{10,11... | collective-permute-start | bytes 786440 | tf_op jit(solution)/shard_map/ppermute | solution.py:663

commit v3 on v2

--- a/solution.py
+++ b/solution.py
@@ -65,7 +65,9 @@
     dot = functools.partial(lax.dot_general, dimension_numbers=dims, preferred_element_type=f32)
     left_high, left_low = left
     right_high, right_low = right
-    return dot(left_high, right_high) + (dot(left_low, right_high) + dot(left_high, right_low))
+    rows = left_high.shape[0]
+    both = dot(jnp.concatenate([left_high, left_low], axis=0), right_high)
+    return both[:rows] + (both[rows:] + dot(left_high, right_low))
 
 
 def focusing(focus_bins):
@@ -166,14 +168,21 @@
     residual_hbm,
     bins_hbm,
     class_hbm,
+    small_hbm,
+    inner_hbm,
+    outer_hbm,
     own_ref,
     send_ref,
     weight_ref,
+    small_ref,
+    inner_ref,
+    outer_ref,
     residual_ref,
     bins_ref,
     class_ref,
     sems,
     class_sem,
+    table_sems,
     *,
     cuts,
 ):
@@ -191,6 +200,14 @@
         first.start()
         second.start()
         copies.append((first, second))
+    dep = dep_ref[0]
+    tables = [
+        pltpu.make_async_copy(inner_hbm.at[dep], inner_ref, table_sems.at[0]),
+        pltpu.make_async_copy(outer_hbm, outer_ref, table_sems.at[1]),
+        pltpu.make_async_copy(small_hbm, small_ref, table_sems.at[2]),
+    ]
+    for copy in tables:
+        copy.start()
     sign = jnp.where(dep_ref[0] == 0, 1.0, -1.0).astype(f32)
     class_copy.wait()
     layer_weights(class_ref, weight_ref)
@@ -204,12 +221,16 @@
         right = sign * scaled[..., half:]
         own_ref[part] = left + right
         send_ref[part] = left - right
+    for copy in tables:
+        copy.wait()
+
+
+def dot2(left, right):
+    return jnp.dot(left, right, preferred_element_type=f32)
 
 
 def to_modes(cells, table, sine):
-    depth, rows, half = cells.shape
-    waves = dot3(split(cells.reshape(depth * rows, half)), table)
-    return dot3(sine, split(waves)).reshape(depth, rows, half)
+    return dot3(split(from_modes(cells, sine)), table).reshape(cells.shape)
 
 
 def from_modes(modes, sine):
@@ -229,41 +250,36 @@
     own_ref,
     weight_ref,
     table_hbm,
-    small_hbm,
-    inner_hbm,
-    outer_hbm,
+    small_ref,
+    inner_ref,
+    outer_ref,
     modes_ref,
     table_ref,
-    small_ref,
     inverse_ref,
     inverse_outer_ref,
-    inner_ref,
-    outer_ref,
     sems,
 ):
-    depth, rows, half = own_ref.shape
-    plane_rows = inverse_outer_ref.shape[1]
-    dep = dep_ref[0]
     copies = [
-        pltpu.make_async_copy(inner_hbm.at[dep], inner_ref, sems.at[0]),
-        pltpu.make_async_copy(outer_hbm, outer_ref, sems.at[1]),
-        pltpu.make_async_copy(small_hbm, small_ref, sems.at[2]),
-        pltpu.make_async_copy(table_hbm.at[dep, 0], table_ref.at[0], sems.at[3]),
-        pltpu.make_async_copy(table_hbm.at[dep, 1], table_ref.at[1], sems.at[4]),
+        pltpu.make_async_copy(table_hbm.at[dep_ref[0], part], table_ref.at[part], sems.at[part])
+        for part in range(2)
     ]
     for copy in copies:
         copy.start()
-    copies[0].wait()
-    copies[1].wait()
+    depth, rows, half = own_ref.shape
+    plane_rows = inverse_outer_ref.shape[1]
     weights, couple = layer_terms(weight_ref, half // lanes, 1)
     factor(weights, couple, inner_ref[...], inverse_ref)
     weights, couple = layer_terms(weight_ref, plane_rows // 8, 0)
     wave = outer_ref[:plane_rows] + outer_ref[pl.ds(plane_rows + spot_ref[0], 1), :]
     factor(weights, couple, damping + smoothing * wave, inverse_outer_ref)
-    for copy in copies[2:]:
-        copy.wait()
     sine, _ = parts_of(small_ref, depth * rows, depth)
-    modes_ref[...] = to_modes(own_ref[...], (table_ref[0], table_ref[1]), sine)
+    high, low = split(from_modes(own_ref[...], sine))
+    block = depth * rows
+    copies[0].wait()
+    both = dot2(jnp.concatenate([high, low], axis=0), table_ref[0])
+    copies[1].wait()
+    total = both[:block] + (both[block:] + dot2(high, table_ref[1]))
+    modes_ref[...] = total.reshape(depth, rows, half)
 
 
 def interior_kernel(
@@ -607,37 +623,41 @@
     packed = (hor_count, layers, lanes)
     plane = (layers, plane_rows, lanes)
     cuts = 4
-    own, send, weight = call(
+    own, send, weight, small_here, inner_here, outer_here = call(
         functools.partial(fold_kernel, cuts=cuts),
         [scalar(dep_index)]
-        + [(pltpu.HBM, value) for value in (residual, focus_bins, layer_class)],
-        [shape(*slab), shape(*slab), shape(layers, 8, lanes)],
+        + [(pltpu.HBM, value) for value in (residual, focus_bins, layer_class)]
+        + [constant(value) for value in (small, inner.astype(np.float32), outer)],
+        [
+            shape(*slab),
+            shape(*slab),
+            shape(layers, 8, lanes),
+            jax.ShapeDtypeStruct(small.shape, bf16),
+            shape(rows, half),
+            shape(*outer.shape),
+        ],
         [
             pltpu.VMEM(full, f32),
             pltpu.VMEM(full, jnp.int32),
             pltpu.SMEM((layers,), jnp.int32),
             pltpu.SemaphoreType.DMA((2, cuts)),
             pltpu.SemaphoreType.DMA,
+            pltpu.SemaphoreType.DMA((3,)),
         ],
     )
     pairs = [(0, 1), (1, 0)]
     recv = lax.ppermute(send, "dep", pairs)
-    modes, table_here, small_here, inverse, inverse_outer = call(
+    modes, table_here, inverse, inverse_outer = call(
         prepare_kernel,
-        [scalar(dep_index), scalar(spot), near_by(own), near_by(weight)]
-        + [constant(value) for value in (table, small, inner.astype(np.float32), outer)],
+        [scalar(dep_index), scalar(spot), near_by(own), near_by(weight), constant(table)]
+        + [near_by(value) for value in (small_here, inner_here, outer_here)],
         [
             shape(*slab),
             jax.ShapeDtypeStruct((2, half, half), bf16),
-            jax.ShapeDtypeStruct(small.shape, bf16),
             shape(*field),
             shape(*plane),
         ],
-        [
-            pltpu.VMEM((rows, half), f32),
-            pltpu.VMEM(outer.shape, f32),
-            pltpu.SemaphoreType.DMA((5,)),
-        ],
+        [pltpu.SemaphoreType.DMA((2,))],
     )
     shared = [near_by(value) for value in (table_here, small_here, weight, inverse)]
     outgoing, source = call(

time: 33.7 us -> 32.9 us (0.976)
  Pallas kernels: 7.84 us -> 6.94 us
    pallas_call x7, Pallas kernels: 7.84 us -> 6.94 us  [call(): pl.pallas_call(kernel, in_specs=specs, out_specs=out_specs if single else...]
  transfers between devices with their start and end apart: 2 -> 2, of which waited for: 1 -> 1; matrix products, arithmetic and copies ran while one was open for 0% -> 0% of each run, Pallas kernels for 9% -> 7%
where the time goes in v3:
time: 32.9 us; the launch traced here: 32.7 us
  blocking collectives  24.3 us (74%)
  Pallas kernels  6.94 us (21%)
  waiting for transfers between devices  0.8 us (2%)
  starting transfers between devices  0.59 us (2%)
    all_to_all x1, blocking collectives, body(): lax.all_to_all(outgoing, 'hor', split_axis=0, concat_axis=0, tiled=True)  14.4 us
    all_to_all x1, blocking collectives, body(): lax.all_to_all(answered, 'hor', split_axis=0, concat_axis=0, tiled=True)  9.85 us
    pallas_call x7, Pallas kernels, call(): pl.pallas_call(kernel, in_specs=specs, out_specs=out_specs if single else...  6.94 us
    ppermute x2, waiting for transfers between devices, body(): recv = lax.ppermute(send, 'dep', pairs)  0.8 us
  transfers between devices with their start and end apart: 2, of which 1 were waited for; matrix products, arithmetic and copies ran while one was open for 0% of the time, Pallas kernels for 7%

profile of v3, /device:TPU:0, one launch (start us, length us, event | category | flops | bytes accessed | tf_op | source)
XLA Modules:
  0.0 32.7 jit_solution(9728982004984528352)
XLA Ops:
  0.0 1.4 %shard_map.73 = (f32[16,8,512]{2,1,0:T(8,128)S(1)}, f32[16,8,512]{2,1,0:T(8,128)S(1)}, f32[32,8,128]{2,1,0:T(8,128)S(1)}, bf16[320,128]{1,0:T(8,128)(2,1)S(1)}, ...) custom-call(s32[1]{0:T(128)} %bitcast.dep_ref, f32[16,8,1024]{2,1,0:T(8,128)} %residual_hbm.1, s32[16,8,1024]{2,1,0:T(8,128)} %bins_ref.1, ...), custom_call_target="tpu_custom_call" | custom-call | tf_op jit(solution)/shard_map/pallas_call | solution.py:565
  1.4 0.5 %collective-permute-start = (f32[16,8,512]{2,1,0:T(8,128)S(1)}, f32[16,8,512]{2,1,0:T(8,128)S(1)}, u32[]{:S(2)}, u32[]{:S(2)}) collective-permute-start(f32[16,8,512]{2,1,0:T(8,128)S(1)} %get-tuple-element.27), channel_id=1, source_target_pairs={{0,1},{1,0},{2,3},{3,2},{4,5},{5,4},{6,7},{7,6},{8,9},{9,8},{10,11... | collective-permute-start | bytes 786440 | tf_op jit(solution)/shard_map/ppermute | solution.py:649
  2.0 1.5 %shard_map.74 = (f32[16,8,512]{2,1,0:T(8,128)S(1)}, bf16[2,512,512]{2,1,0:T(8,128)(2,1)S(1)}, f32[32,8,512]{2,1,0:T(8,128)S(1)}, f32[32,32,128]{2,1,0:T(8,128)S(1)}) custom-call(s32[1]{0:T(128)} %bitcast.dep_ref, s32[1]{0:T(128)} %bitcast.1.spot_ref, f32[16,8,512]{2,1,0:T(8,128)S(1)} %get-tuple-element.21.own_ref, ...), custom_call_target="tpu_custom_call" | custom-call | tf_op jit(solution)/shard_map/pallas_call | solution.py:565
  3.4 0.0 collective-permute-done.recv_ref
  3.5 1.0 %shard_map.75 = (f32[8,32,128]{2,1,0:T(8,128)S(1)}, f32[32,8,512]{2,1,0:T(8,128)S(1)}) custom-call(s32[1]{0:T(128)} %bitcast.dep_ref, f32[16,8,512]{2,1,0:T(8,128)S(1)} %get-tuple-element.26.modes_ref, f32[16,8,512]{2,1,0:T(8,128)S(1)} %collective-permute-done.recv_ref, bf16[2,512,512]{2,1,0:T(8,128)(2,1)S(1)} %get-tuple-element.28.table_ref, ...), custom_call_target="tpu_custom_call" | custom-call | tf_op jit(solution)/shard_map/pallas_call | solution.py:565
  4.5 0.0 copy-start
  4.5 14.4 %all_to_all.10.packed_ref = f32[8,32,128]{2,1,0:T(8,128)S(1)} all-to-all(f32[8,32,128]{2,1,0:T(8,128)S(1)} %get-tuple-element.30), channel_id=1, replica_groups=mesh['grp'=2,'hor'=8,'dep'=2] {'hor'}, dimensions={0} | all-to-all | bytes 262144 | tf_op jit(solution)/shard_map/all_to_all | solution.py:669
  18.9 0.5 %shard_map.76 = f32[8,32,128]{2,1,0:T(8,128)S(1)} custom-call(f32[8,32,128]{2,1,0:T(8,128)S(1)} %all_to_all.10.packed_ref, f32[32,8,128]{2,1,0:T(8,128)S(1)} %get-tuple-element.22.weight_ref, f32[32,32,128]{2,1,0:T(8,128)S(1)} %get-tuple-element.31.inverse_ref), custom_call_target="tpu_custom_call" | custom-call | tf_op jit(solution)/shard_map/pallas_call | solution.py:565
  19.4 9.9 %all_to_all.11.back_ref = f32[8,32,128]{2,1,0:T(8,128)S(1)} all-to-all(f32[8,32,128]{2,1,0:T(8,128)S(1)} %shard_map.76), channel_id=1, replica_groups=mesh['grp'=2,'hor'=8,'dep'=2] {'hor'}, dimensions={0} | all-to-all | bytes 262144 | tf_op jit(solution)/shard_map/all_to_all | solution.py:676
  29.3 1.0 %shard_map.77 = (f32[16,8,512]{2,1,0:T(8,128)S(1)}, f32[16,8,512]{2,1,0:T(8,128)S(1)}) custom-call(s32[1]{0:T(128)} %bitcast.dep_ref, f32[8,32,128]{2,1,0:T(8,128)S(1)} %all_to_all.11.back_ref, f32[32,8,512]{2,1,0:T(8,128)S(1)} %get-tuple-element.32.source_ref, bf16[2,512,512]{2,1,0:T(8,128)(2,1)S(1)} %get-tuple-element.28.table_ref, ...), custom_call_target="tpu_custom_call" | custom-call | tf_op jit(solution)/shard_map/pallas_call | solution.py:565
  30.2 0.1 collective-permute-start.1
  30.3 0.0 copy-done
  30.3 0.7 %shard_map.78 = (f32[16,8,512]{2,1,0:T(8,128)S(1)}, f32[16,8,1024]{2,1,0:T(8,128)S(1)}) custom-call(f32[16,8,512]{2,1,0:T(8,128)S(1)} %get-tuple-element.33.waves_ref, s32[16,8,1024]{2,1,0:T(8,128)S(1)} %copy-done, bf16[2,512,512]{2,1,0:T(8,128)(2,1)S(1)} %get-tuple-element.28.table_ref, bf16[320,128]{1,0:T(8,128)(2,1)S(1)} %get-tuple-element.23.small_ref), custom_call_target="tpu_custom_call" | custom-call | tf_op jit(solution)/shard_map/pallas_call | solution.py:565
  31.0 0.8 %collective-permute-done.1.recv_ref = f32[16,8,512]{2,1,0:T(8,128)S(1)} collective-permute-done((f32[16,8,512]{2,1,0:T(8,128)S(1)}, f32[16,8,512]{2,1,0:T(8,128)S(1)}, u32[]{:S(2)}, u32[]{:S(2)}) %collective-permute-start.1) | collective-permute-done | bytes 262176 | tf_op jit(solution)/shard_map/ppermute | solution.py:683
  31.8 0.8 %shard_map.79 = f32[16,8,1024]{2,1,0:T(8,128)} custom-call(s32[1]{0:T(128)} %bitcast.dep_ref, f32[16,8,512]{2,1,0:T(8,128)S(1)} %get-tuple-element.34.own_ref, f32[16,8,512]{2,1,0:T(8,128)S(1)} %collective-permute-done.1.recv_ref, f32[16,8,1024]{2,1,0:T(8,128)S(1)} %get-tuple-element.36.focus_ref), custom_call_target="tpu_custom_call" | custom-call | tf_op jit(solution)/shard_map/pallas_call | solution.py:565
Async XLA Ops:
  1.4 2.0 %collective-permute-start = (f32[16,8,512]{2,1,0:T(8,128)S(1)}, f32[16,8,512]{2,1,0:T(8,128)S(1)}, u32[]{:S(2)}, u32[]{:S(2)}) collective-permute-start(f32[16,8,512]{2,1,0:T(8,128)S(1)} %get-tuple-element.27), channel_id=1, source_target_pairs={{0,1},{1,0},{2,3},{3,2},{4,5},{5,4},{6,7},{7,6},{8,9},{9,8},{10,11... | collective-permute-start | bytes 786440 | tf_op jit(solution)/shard_map/ppermute | solution.py:649
  4.5 25.8 %copy-start = (s32[16,8,1024]{2,1,0:T(8,128)S(1)}, s32[16,8,1024]{2,1,0:T(8,128)}, u32[]{:S(2)}) copy-start(s32[16,8,1024]{2,1,0:T(8,128)} %bins_ref.1) | copy-start | bytes 1572868
  30.2 1.6 %collective-permute-start.1 = (f32[16,8,512]{2,1,0:T(8,128)S(1)}, f32[16,8,512]{2,1,0:T(8,128)S(1)}, u32[]{:S(2)}, u32[]{:S(2)}) collective-permute-start(f32[16,8,512]{2,1,0:T(8,128)S(1)} %get-tuple-element.35), channel_id=1, source_target_pairs={{0,1},{1,0},{2,3},{3,2},{4,5},{5,4},{6,7},{7,6},{8,9},{9,8},{10,11... | collective-permute-start | bytes 786440 | tf_op jit(solution)/shard_map/ppermute | solution.py:683

commit v4 on v3

--- a/solution.py
+++ b/solution.py
@@ -200,9 +200,8 @@
         first.start()
         second.start()
         copies.append((first, second))
-    dep = dep_ref[0]
     tables = [
-        pltpu.make_async_copy(inner_hbm.at[dep], inner_ref, table_sems.at[0]),
+        pltpu.make_async_copy(inner_hbm, inner_ref, table_sems.at[0]),
         pltpu.make_async_copy(outer_hbm, outer_ref, table_sems.at[1]),
         pltpu.make_async_copy(small_hbm, small_ref, table_sems.at[2]),
     ]
@@ -256,6 +255,7 @@
     modes_ref,
     table_ref,
     inverse_ref,
+    inverse_other_ref,
     inverse_outer_ref,
     sems,
 ):
@@ -268,7 +268,8 @@
     depth, rows, half = own_ref.shape
     plane_rows = inverse_outer_ref.shape[1]
     weights, couple = layer_terms(weight_ref, half // lanes, 1)
-    factor(weights, couple, inner_ref[...], inverse_ref)
+    factor(weights, couple, inner_ref[dep_ref[0]], inverse_ref)
+    factor(weights, couple, inner_ref[1 - dep_ref[0]], inverse_other_ref)
     weights, couple = layer_terms(weight_ref, plane_rows // 8, 0)
     wave = outer_ref[:plane_rows] + outer_ref[pl.ds(plane_rows + spot_ref[0], 1), :]
     factor(weights, couple, damping + smoothing * wave, inverse_outer_ref)
@@ -291,7 +292,10 @@
     weight_ref,
     inverse_ref,
     packed_ref,
+    keep_ref,
+    give_ref,
     source_ref,
+    solved_ref,
     stage_ref,
     partial_ref,
 ):
@@ -310,9 +314,12 @@
     edge_row = lax.broadcasted_iota(jnp.int32, (rows, half), 0) == 0
 
     def emit(layer, values):
+        solved_ref[layer] = values
         stage_ref[layer] = jnp.where(edge_row, source_ref[layer], weights[layer] * values)
 
     substitute(couple, inverse_ref, partial_ref, lambda layer: source_ref[layer], emit)
+    keep_ref[...] = solved_ref[pl.ds(place, depth)]
+    give_ref[...] = solved_ref[pl.ds(depth - place, depth)]
     lower = []
     upper = []
     for part in range(2):
@@ -463,26 +470,22 @@
         back_ref[index] = jnp.where(first, sum_ref[index], sum_ref[(index + 1) % hor_count])
 
 
-def finish_kernel(
+def extend(
     dep_ref,
     back_ref,
-    source_ref,
-    table_ref,
+    solved_ref,
+    table,
     small_ref,
     weight_ref,
     inverse_ref,
-    send_ref,
-    waves_ref,
     left_ref,
     right_ref,
     stage_ref,
     partial_ref,
-    *,
-    near_values,
-    far_values,
+    ends,
 ):
-    layers, rows, half = source_ref.shape
-    depth = layers // 2
+    depth, rows, half = solved_ref.shape
+    layers = 2 * depth
     hor_count = back_ref.shape[0]
     chunk = half // hor_count
     lane = lax.broadcasted_iota(jnp.int32, (layers, lanes), 1)
@@ -500,47 +503,96 @@
         left_ref[:, tile * lanes : (tile + 1) * lanes] = left
         right_ref[:, tile * lanes : (tile + 1) * lanes] = right
     weights, couple = layer_terms(weight_ref, half // lanes, 1)
-    near = row_values(near_values, (rows, half))
-    far = row_values(far_values, (rows, half))
-    edge_row = lax.broadcasted_iota(jnp.int32, (rows, half), 0) == 0
+    near = row_values(ends[0], (rows, half))
+    far = row_values(ends[1], (rows, half))
 
     def row_of(ref, layer):
         return jnp.broadcast_to(ref[pl.ds(layer, 1), :], (rows, half))
 
     def source(layer):
         pull = near * row_of(left_ref, layer) + far * row_of(right_ref, layer)
-        return source_ref[layer] + weights[layer] * pull
+        return weights[layer] * pull
 
     def emit(layer, values):
-        stage_ref[layer] = jnp.where(edge_row, row_of(left_ref, layer), values)
+        stage_ref[layer] = values
 
     substitute(couple, inverse_ref, partial_ref, source, emit)
-    place = dep_ref[0] * depth
+    place = pl.multiple_of(dep_ref[0] * depth, depth)
+    edge_row = lax.broadcasted_iota(jnp.int32, (depth, rows, half), 1) == 0
+    edge = left_ref[pl.ds(place, depth), :]
+    modes = jnp.where(edge_row, edge[:, None, :], solved_ref[...] + stage_ref[pl.ds(place, depth)])
     sine, _ = parts_of(small_ref, depth * rows, depth)
-    waves = from_modes(stage_ref[pl.ds(depth - place, depth)], sine)
-    cells = dot3(split(waves), (table_ref[0], table_ref[1]), (((1,), (1,)), ((), ())))
-    send_ref[...] = cells.reshape(depth, rows, half)
-    waves_ref[...] = stage_ref[pl.ds(place, depth)]
-
-
-def restore_kernel(waves_ref, bins_ref, table_ref, small_ref, own_ref, focus_ref):
-    depth, rows, half = own_ref.shape
+    waves = from_modes(modes, sine)
+    cells = dot3(split(waves), table, (((1,), (1,)), ((), ())))
+    return cells.reshape(depth, rows, half)
+
+
+def restore_kernel(
+    dep_ref,
+    back_ref,
+    solved_ref,
+    table_ref,
+    small_ref,
+    weight_ref,
+    inverse_ref,
+    bins_ref,
+    own_ref,
+    focus_ref,
+    *scratch,
+    ends,
+):
+    own_ref[...] = extend(
+        dep_ref,
+        back_ref,
+        solved_ref,
+        (table_ref[0], table_ref[1]),
+        small_ref,
+        weight_ref,
+        inverse_ref,
+        *scratch,
+        ends,
+    )
     focus_ref[...] = focusing(bins_ref[...])
-    sine, _ = parts_of(small_ref, depth * rows, depth)
-    waves = from_modes(waves_ref[...], sine)
-    cells = dot3(split(waves), (table_ref[0], table_ref[1]), (((1,), (1,)), ((), ())))
-    own_ref[...] = cells.reshape(depth, rows, half)
-
-
-def unfold_kernel(dep_ref, own_ref, recv_ref, focus_ref, out_hbm, out_ref, sems, *, scale, cuts):
+
+
+def unfold_kernel(
+    dep_ref,
+    back_ref,
+    solved_ref,
+    table_ref,
+    small_ref,
+    weight_ref,
+    inverse_ref,
+    own_ref,
+    focus_ref,
+    out_hbm,
+    out_ref,
+    sems,
+    *scratch,
+    ends,
+    scale,
+    cuts,
+):
     depth, _, half = own_ref.shape
     size = depth // cuts
+    other = 1 - dep_ref[0]
+    cells = extend(
+        dep_ref,
+        back_ref,
+        solved_ref,
+        (table_ref[other, 0], table_ref[other, 1]),
+        small_ref,
+        weight_ref,
+        inverse_ref,
+        *scratch,
+        ends,
+    )
     sign = jnp.where(dep_ref[0] == 0, scale, -scale).astype(f32)
     copies = []
     for cut in range(cuts):
         part = pl.ds(cut * size, size)
         own = own_ref[part]
-        recv = recv_ref[part]
+        recv = cells[cut * size : (cut + 1) * size]
         focus_map = focus_ref[part]
         out_ref[part, :, :half] = focus_map[..., :half] * ((own + recv) * scale)
         out_ref[part, :, half:] = focus_map[..., half:] * ((own - recv) * sign)
@@ -568,7 +620,7 @@
         out_specs=out_specs if single else [out_specs] * len(out_shape),
         out_shape=out_shape,
         scratch_shapes=list(scratch),
-        compiler_params=pltpu.CompilerParams(vmem_limit_bytes=48 * 1024 * 1024),
+        compiler_params=pltpu.CompilerParams(vmem_limit_bytes=16 * 1024 * 1024),
     )(*values)
 
 
@@ -624,7 +676,7 @@
     plane = (layers, plane_rows, lanes)
     cuts = 4
     own, send, weight, small_here, inner_here, outer_here = call(
-        functools.partial(fold_kernel, cuts=cuts),
+        functools.partial(fold_kernel, cuts=cuts // 2),
         [scalar(dep_index)]
         + [(pltpu.HBM, value) for value in (residual, focus_bins, layer_class)]
         + [constant(value) for value in (small, inner.astype(np.float32), outer)],
@@ -633,21 +685,21 @@
             shape(*slab),
             shape(layers, 8, lanes),
             jax.ShapeDtypeStruct(small.shape, bf16),
-            shape(rows, half),
+            shape(2, rows, half),
             shape(*outer.shape),
         ],
         [
             pltpu.VMEM(full, f32),
             pltpu.VMEM(full, jnp.int32),
             pltpu.SMEM((layers,), jnp.int32),
-            pltpu.SemaphoreType.DMA((2, cuts)),
+            pltpu.SemaphoreType.DMA((2, cuts // 2)),
             pltpu.SemaphoreType.DMA,
             pltpu.SemaphoreType.DMA((3,)),
         ],
     )
     pairs = [(0, 1), (1, 0)]
     recv = lax.ppermute(send, "dep", pairs)
-    modes, table_here, inverse, inverse_outer = call(
+    modes, table_here, inverse, inverse_other, inverse_outer = call(
         prepare_kernel,
         [scalar(dep_index), scalar(spot), near_by(own), near_by(weight), constant(table)]
         + [near_by(value) for value in (small_here, inner_here, outer_here)],
@@ -655,18 +707,21 @@
             shape(*slab),
             jax.ShapeDtypeStruct((2, half, half), bf16),
             shape(*field),
+            shape(*field),
             shape(*plane),
         ],
         [pltpu.SemaphoreType.DMA((2,))],
     )
-    shared = [near_by(value) for value in (table_here, small_here, weight, inverse)]
-    outgoing, source = call(
+    outgoing, keep, give = call(
         interior_kernel,
-        [scalar(dep_index), near_by(modes), near_by(recv)] + shared,
-        [shape(*packed), shape(*field)],
-        [pltpu.VMEM(field, f32)] * 2,
-    )
+        [scalar(dep_index)]
+        + [near_by(v) for v in (modes, recv, table_here, small_here, weight, inverse)],
+        [shape(*packed), shape(*slab), shape(*slab)],
+        [pltpu.VMEM(field, f32)] * 4,
+    )
+    got = lax.ppermute(give, "dep", pairs)
     incoming = lax.all_to_all(outgoing, "hor", split_axis=0, concat_axis=0, tiled=True)
+    incoming, got = lax.optimization_barrier((incoming, got))
     answered = call(
         functools.partial(interface_kernel, chunk=chunk),
         [near_by(incoming), near_by(weight), near_by(inverse_outer)],
@@ -674,23 +729,36 @@
         [pltpu.VMEM(packed, f32)] * 3 + [pltpu.VMEM(plane, f32)],
     )
     edges = lax.all_to_all(answered, "hor", split_axis=0, concat_axis=0, tiled=True)
-    send, waves = call(
-        functools.partial(finish_kernel, near_values=near, far_values=far),
-        [scalar(dep_index), near_by(edges), near_by(source)] + shared,
-        [shape(*slab)] * 2,
-        [pltpu.VMEM((layers, half), f32)] * 2 + [pltpu.VMEM(field, f32)] * 2,
-    )
-    recv = lax.ppermute(send, "dep", pairs)
+    other_edges = lax.ppermute(edges, "dep", pairs)
+    scratch = [pltpu.VMEM((layers, half), f32)] * 2 + [pltpu.VMEM(field, f32)] * 2
     own, focus_map = call(
-        restore_kernel,
-        [near_by(value) for value in (waves, focus_bins, table_here, small_here)],
+        functools.partial(restore_kernel, ends=(near, far)),
+        [scalar(dep_index)]
+        + [
+            near_by(v)
+            for v in (edges, keep, table_here, small_here, weight, inverse, focus_bins)
+        ],
         [shape(*slab), shape(*full)],
+        scratch,
     )
     return call(
-        functools.partial(unfold_kernel, scale=1.0 / x_cells, cuts=cuts),
-        [scalar(dep_index)] + [near_by(value) for value in (own, recv, focus_map)],
+        functools.partial(unfold_kernel, ends=(near, far), scale=1.0 / x_cells, cuts=cuts),
+        [scalar(dep_index)]
+        + [
+            near_by(v)
+            for v in (
+                other_edges,
+                got,
+                jnp.asarray(table),
+                small_here,
+                weight,
+                inverse_other,
+                own,
+                focus_map,
+            )
+        ],
         shape(*full),
-        [pltpu.VMEM(full, f32), pltpu.SemaphoreType.DMA((cuts,))],
+        [pltpu.VMEM(full, f32), pltpu.SemaphoreType.DMA((cuts,))] + scratch,
         outside=True,
     )
 

time: 32.9 us -> 32.6 us (level)
  waiting for transfers between devices: 0.8 us -> 0.33 us
    ppermute x2 -> x1, waiting for transfers between devices: 0.8 us -> 0.01 us  [body(): recv = lax.ppermute(send, 'dep', pairs)]
    pallas_call x7 -> x6, Pallas kernels: 6.94 us -> 7.07 us  [call(): pl.pallas_call(kernel, in_specs=specs, out_specs=out_specs if single else...]
  transfers between devices with their start and end apart: 2 -> 3, of which waited for: 1 -> 1; matrix products, arithmetic and copies ran while one was open for 0% -> 0% of each run, Pallas kernels for 7% -> 8%
where the time goes in v4:
time: 32.6 us; the launch traced here: 32.4 us
  blocking collectives  24.3 us (75%)
  Pallas kernels  7.07 us (22%)
  starting transfers between devices  0.64 us (2%)
  waiting for transfers between devices  0.33 us (1%)
    all_to_all x1, blocking collectives, body(): lax.all_to_all(outgoing, 'hor', split_axis=0, concat_axis=0, tiled=True)  14.5 us
    all_to_all x1, blocking collectives, body(): lax.all_to_all(answered, 'hor', split_axis=0, concat_axis=0, tiled=True)  9.74 us
    pallas_call x6, Pallas kernels, call(): pl.pallas_call(kernel, in_specs=specs, out_specs=out_specs if single else...  7.07 us
  transfers between devices with their start and end apart: 3, of which 1 were waited for; matrix products, arithmetic and copies ran while one was open for 0% of the time, Pallas kernels for 8%

profile of v4, /device:TPU:0, one launch (start us, length us, event | category | flops | bytes accessed | tf_op | source)
XLA Modules:
  0.0 32.4 jit_solution(6044091172034922912)
XLA Ops:
  0.0 1.3 %shard_map.73 = (f32[16,8,512]{2,1,0:T(8,128)S(1)}, f32[16,8,512]{2,1,0:T(8,128)S(1)}, f32[32,8,128]{2,1,0:T(8,128)S(1)}, bf16[320,128]{1,0:T(8,128)(2,1)S(1)}, ...) custom-call(s32[1]{0:T(128)} %bitcast.dep_ref, f32[16,8,1024]{2,1,0:T(8,128)} %residual_hbm.1, s32[16,8,1024]{2,1,0:T(8,128)} %bins_ref.1, ...), custom_call_target="tpu_custom_call" | custom-call | tf_op jit(solution)/shard_map/pallas_call | solution.py:617
  1.3 0.5 %collective-permute-start = (f32[16,8,512]{2,1,0:T(8,128)S(1)}, f32[16,8,512]{2,1,0:T(8,128)S(1)}, u32[]{:S(2)}, u32[]{:S(2)}) collective-permute-start(f32[16,8,512]{2,1,0:T(8,128)S(1)} %get-tuple-element.29), channel_id=1, source_target_pairs={{0,1},{1,0},{2,3},{3,2},{4,5},{5,4},{6,7},{7,6},{8,9},{9,8},{10,11... | collective-permute-start | bytes 786440 | tf_op jit(solution)/shard_map/ppermute | solution.py:701
  1.9 1.5 %shard_map.74 = (f32[16,8,512]{2,1,0:T(8,128)S(1)}, bf16[2,512,512]{2,1,0:T(8,128)(2,1)S(1)}, f32[32,8,512]{2,1,0:T(8,128)S(1)}, f32[32,8,512]{2,1,0:T(8,128)S(1)}, f32[32,32,128]{2,1,0:T(8,128)S(1)}) custom-call(s32[1]{0:T(128)} %bitcast.dep_ref, s32[1]{0:T(128)} %bitcast.1.spot_ref, f32[16,8,512]{2,1,0:T(8,128)S(1)} %get-tuple-element.23.own_ref, ...), custom_call_target="tpu_custom_call" | custom-call | tf_op jit(solution)/shard_map/pallas_call | solution.py:617
  3.4 0.0 copy-start.1
  3.4 0.0 collective-permute-done.recv_ref
  3.4 1.0 %shard_map.75 = (f32[8,32,128]{2,1,0:T(8,128)S(1)}, f32[16,8,512]{2,1,0:T(8,128)S(1)}, f32[16,8,512]{2,1,0:T(8,128)S(1)}) custom-call(s32[1]{0:T(128)} %bitcast.dep_ref, f32[16,8,512]{2,1,0:T(8,128)S(1)} %get-tuple-element.28.modes_ref, f32[16,8,512]{2,1,0:T(8,128)S(1)} %collective-permute-done.recv_ref, ...), custom_call_target="tpu_custom_call" | custom-call | tf_op jit(solution)/shard_map/pallas_call | solution.py:617
  4.4 0.0 copy-start
  4.4 0.1 collective-permute-start.1
  4.6 14.5 %all_to_all.10.packed_ref = f32[8,32,128]{2,1,0:T(8,128)S(1)} all-to-all(f32[8,32,128]{2,1,0:T(8,128)S(1)} %get-tuple-element.32), channel_id=1, replica_groups=mesh['grp'=2,'hor'=8,'dep'=2] {'hor'}, dimensions={0} | all-to-all | bytes 262144 | tf_op jit(solution)/shard_map/all_to_all | solution.py:723
  19.1 0.0 collective-permute-done.1.solved_ref
  19.1 0.5 %shard_map.76 = f32[8,32,128]{2,1,0:T(8,128)S(1)} custom-call(f32[8,32,128]{2,1,0:T(8,128)S(1)} %all_to_all.10.packed_ref, f32[32,8,128]{2,1,0:T(8,128)S(1)} %get-tuple-element.24.weight_ref, f32[32,32,128]{2,1,0:T(8,128)S(1)} %get-tuple-element.35.inverse_ref), custom_call_target="tpu_custom_call" | custom-call | tf_op jit(solution)/shard_map/pallas_call | solution.py:617
  19.6 9.7 %all_to_all.11.back_ref = f32[8,32,128]{2,1,0:T(8,128)S(1)} all-to-all(f32[8,32,128]{2,1,0:T(8,128)S(1)} %shard_map.76), channel_id=1, replica_groups=mesh['grp'=2,'hor'=8,'dep'=2] {'hor'}, dimensions={0} | all-to-all | bytes 262144 | tf_op jit(solution)/shard_map/all_to_all | solution.py:731
  29.3 0.0 collective-permute-start.2
  29.3 0.0 copy-done.1
  29.3 1.0 %shard_map.77 = (f32[16,8,512]{2,1,0:T(8,128)S(1)}, f32[16,8,1024]{2,1,0:T(8,128)S(1)}) custom-call(s32[1]{0:T(128)} %bitcast.dep_ref, f32[8,32,128]{2,1,0:T(8,128)S(1)} %all_to_all.11.back_ref, f32[16,8,512]{2,1,0:T(8,128)S(1)} %get-tuple-element.38.solved_ref, bf16[2,512,512]{2,1,0:T(8,128)(2,1)S(1)} %get-tuple-element.30.table_ref, ...), custom_call_target="tpu_custom_call" | custom-call | tf_op jit(solution)/shard_map/pallas_call | solution.py:617
  30.4 0.3 %collective-permute-done.2.back_ref = f32[8,32,128]{2,1,0:T(8,128)S(1)} collective-permute-done((f32[8,32,128]{2,1,0:T(8,128)S(1)}, f32[8,32,128]{2,1,0:T(8,128)S(1)}, u32[]{:S(2)}, u32[]{:S(2)}) %collective-permute-start.2) | collective-permute-done | bytes 131104 | tf_op jit(solution)/shard_map/ppermute | solution.py:732
  30.7 0.0 copy-done
  30.7 1.7 %shard_map.78 = f32[16,8,1024]{2,1,0:T(8,128)} custom-call(s32[1]{0:T(128)} %bitcast.dep_ref, f32[8,32,128]{2,1,0:T(8,128)S(1)} %collective-permute-done.2.back_ref, f32[16,8,512]{2,1,0:T(8,128)S(1)} %collective-permute-done.1.solved_ref, bf16[2,2,512,512]{3,2,1,0:T(8,128)(2,1)S(1)} %copy-done, bf16[320,128]{1,0:T(8,128)(2,1)S(1)} %get-tuple-element.25.small_ref, ...), custom_call_target="tpu_custom_call" | custom-call | tf_op jit(solution)/shard_map/pallas_call | solution.py:617
Async XLA Ops:
  1.3 2.0 %collective-permute-start = (f32[16,8,512]{2,1,0:T(8,128)S(1)}, f32[16,8,512]{2,1,0:T(8,128)S(1)}, u32[]{:S(2)}, u32[]{:S(2)}) collective-permute-start(f32[16,8,512]{2,1,0:T(8,128)S(1)} %get-tuple-element.29), channel_id=1, source_target_pairs={{0,1},{1,0},{2,3},{3,2},{4,5},{5,4},{6,7},{7,6},{8,9},{9,8},{10,11... | collective-permute-start | bytes 786440 | tf_op jit(solution)/shard_map/ppermute | solution.py:701
  3.4 26.0 %copy-start.1 = (s32[16,8,1024]{2,1,0:T(8,128)S(1)}, s32[16,8,1024]{2,1,0:T(8,128)}, u32[]{:S(2)}) copy-start(s32[16,8,1024]{2,1,0:T(8,128)} %bins_ref.1) | copy-start | bytes 1572868
  4.4 26.3 %copy-start = (bf16[2,2,512,512]{3,2,1,0:T(8,128)(2,1)S(1)}, bf16[2,2,512,512]{3,2,1,0:T(8,128)(2,1)}, u32[]{:S(2)}) copy-start(bf16[2,2,512,512]{3,2,1,0:T(8,128)(2,1)} %constant.21.clone.table_hbm.table_ref) | copy-start | bytes 6291460
  4.4 14.7 %collective-permute-start.1 = (f32[16,8,512]{2,1,0:T(8,128)S(1)}, f32[16,8,512]{2,1,0:T(8,128)S(1)}, u32[]{:S(2)}, u32[]{:S(2)}) collective-permute-start(f32[16,8,512]{2,1,0:T(8,128)S(1)} %get-tuple-element.33), channel_id=1, source_target_pairs={{0,1},{1,0},{2,3},{3,2},{4,5},{5,4},{6,7},{7,6},{8,9},{9,8},{10,11... | collective-permute-start | bytes 786440 | tf_op jit(solution)/shard_map/ppermute | solution.py:722
  29.3 1.3 %collective-permute-start.2 = (f32[8,32,128]{2,1,0:T(8,128)S(1)}, f32[8,32,128]{2,1,0:T(8,128)S(1)}, u32[]{:S(2)}, u32[]{:S(2)}) collective-permute-start(f32[8,32,128]{2,1,0:T(8,128)S(1)} %all_to_all.11.back_ref), channel_id=1, source_target_pairs={{0,1},{1,0},{2,3},{3,2},{4,5},{5,4},{6,7},{7,6},{8,9},{9,8},{10,11... | collective-permute-start | bytes 393224 | tf_op jit(solution)/shard_map/ppermute | solution.py:732

commit v5 on v4

--- a/solution.py
+++ b/solution.py
@@ -329,6 +329,13 @@
     lower = jnp.concatenate(lower, axis=0)
     upper = jnp.concatenate(upper, axis=0)
     lane = lax.broadcasted_iota(jnp.int32, (layers, lanes), 1)
+    if 2 * chunk == lanes:
+        for tile in range(hor_count // 2):
+            here = lower[:, tile * lanes : (tile + 1) * lanes]
+            there = turn(upper[:, tile * lanes : (tile + 1) * lanes], chunk)
+            packed_ref[2 * tile] = jnp.where(lane < chunk, here, there)
+            packed_ref[2 * tile + 1] = jnp.where(lane < chunk, there, here)
+        return
     for index in range(hor_count):
         tile = index * chunk // lanes * lanes
         offset = index * chunk % lanes
@@ -339,7 +346,29 @@
         )
 
 
+def hartley_8(read, write):
+    parts = [read(index) for index in range(8)]
+    plus = [parts[index] + parts[index + 4] for index in range(4)]
+    minus = [parts[index] - parts[index + 4] for index in range(4)]
+    root = math.sqrt(2.0)
+    one, three = minus[1] * root, minus[3] * root
+    same, cross = plus[0] + plus[2], plus[1] + plus[3]
+    write(0, same + cross)
+    write(4, same - cross)
+    same, cross = plus[0] - plus[2], plus[1] - plus[3]
+    write(2, same + cross)
+    write(6, same - cross)
+    same, cross = minus[0] + minus[2], minus[0] - minus[2]
+    write(1, same + one)
+    write(5, same - one)
+    write(3, cross + three)
+    write(7, cross - three)
+
+
 def small_hartley(count, read, write, shape):
+    if count == 8:
+        hartley_8(read, write)
+        return
     if count <= 8:
         table = cas(2.0 * np.pi * (np.outer(np.arange(count), np.arange(count)) % count) / count)
         parts = [read(index) for index in range(count)]
@@ -372,6 +401,7 @@
 
 
 def interface_kernel(
+    spot_ref,
     packed_ref,
     weight_ref,
     inverse_ref,
@@ -389,7 +419,8 @@
     classes = max(1, hor_count // rows)
     repeats = max(1, rows // hor_count)
     lane = lax.broadcasted_iota(jnp.int32, (layers, lanes), 1)
-    first = lane % (2 * chunk) < chunk
+    swapped = spot_ref[0] // 2 % 2 if 2 * chunk == lanes else 0
+    first = lane // chunk % 2 == swapped
 
     def halves(index):
         values = packed_ref[index]
@@ -410,7 +441,14 @@
         sum_ref[index] = values
 
     if hor_count <= 8:
-        small_hartley(hor_count, joined, lambda k, v: wave_ref.__setitem__(k, v), (layers, lanes))
+        pairs = []
+        for index in range(hor_count):
+            here = halves(index)
+            there = turn(here, chunk)
+            back = there if 2 * chunk == lanes else turn(here, -chunk)
+            pairs.append((jnp.where(first, here, there), jnp.where(first, back, here)))
+        joint = [pairs[index][0] + pairs[index - 1][1] for index in range(hor_count)]
+        small_hartley(hor_count, joint.__getitem__, lambda k, v: wave_ref.__setitem__(k, v), (layers, lanes))
     else:
         lax.fori_loop(0, hor_count, lambda k, c: (put_sum(k, joined(k)), c)[1], 0)
         small_hartley(
@@ -489,7 +527,14 @@
     hor_count = back_ref.shape[0]
     chunk = half // hor_count
     lane = lax.broadcasted_iota(jnp.int32, (layers, lanes), 1)
-    for tile in range(half // lanes):
+    for tile in range(half // lanes if 2 * chunk == lanes else 0):
+        even = back_ref[2 * tile]
+        odd = back_ref[2 * tile + 1]
+        inside = lane < chunk
+        left_ref[:, tile * lanes : (tile + 1) * lanes] = jnp.where(inside, even, odd)
+        right = turn(jnp.where(inside, odd, even), chunk)
+        right_ref[:, tile * lanes : (tile + 1) * lanes] = right
+    for tile in range(0 if 2 * chunk == lanes else half // lanes):
         left = None
         right = None
         for index in range(tile * lanes // chunk, (tile + 1) * lanes // chunk):
@@ -536,12 +581,17 @@
     weight_ref,
     inverse_ref,
     bins_ref,
-    own_ref,
-    focus_ref,
+    base_ref,
+    gain_ref,
     *scratch,
     ends,
+    scale,
 ):
-    own_ref[...] = extend(
+    half = solved_ref.shape[-1]
+    sign = jnp.where(dep_ref[0] == 0, -scale, scale).astype(f32)
+    gain_ref[:, :, :half] = focusing(bins_ref[:, :, :half]) * scale
+    gain_ref[:, :, half:] = focusing(bins_ref[:, :, half:]) * sign
+    cells = extend(
         dep_ref,
         back_ref,
         solved_ref,
@@ -552,7 +602,8 @@
         *scratch,
         ends,
     )
-    focus_ref[...] = focusing(bins_ref[...])
+    base_ref[:, :, :half] = gain_ref[:, :, :half] * cells
+    base_ref[:, :, half:] = -(gain_ref[:, :, half:] * cells)
 
 
 def unfold_kernel(
@@ -563,17 +614,16 @@
     small_ref,
     weight_ref,
     inverse_ref,
-    own_ref,
-    focus_ref,
+    base_ref,
+    gain_ref,
     out_hbm,
     out_ref,
     sems,
     *scratch,
     ends,
-    scale,
     cuts,
 ):
-    depth, _, half = own_ref.shape
+    depth, _, half = solved_ref.shape
     size = depth // cuts
     other = 1 - dep_ref[0]
     cells = extend(
@@ -587,15 +637,11 @@
         *scratch,
         ends,
     )
-    sign = jnp.where(dep_ref[0] == 0, scale, -scale).astype(f32)
     copies = []
     for cut in range(cuts):
-        part = pl.ds(cut * size, size)
-        own = own_ref[part]
-        recv = cells[cut * size : (cut + 1) * size]
-        focus_map = focus_ref[part]
-        out_ref[part, :, :half] = focus_map[..., :half] * ((own + recv) * scale)
-        out_ref[part, :, half:] = focus_map[..., half:] * ((own - recv) * sign)
+        part = slice(cut * size, (cut + 1) * size)
+        out_ref[part, :, :half] = base_ref[part, :, :half] + gain_ref[part, :, :half] * cells[part]
+        out_ref[part, :, half:] = base_ref[part, :, half:] + gain_ref[part, :, half:] * cells[part]
         copy = pltpu.make_async_copy(out_ref.at[part], out_hbm.at[part], sems.at[cut])
         copy.start()
         copies.append(copy)
@@ -724,25 +770,25 @@
     incoming, got = lax.optimization_barrier((incoming, got))
     answered = call(
         functools.partial(interface_kernel, chunk=chunk),
-        [near_by(incoming), near_by(weight), near_by(inverse_outer)],
+        [scalar(spot), near_by(incoming), near_by(weight), near_by(inverse_outer)],
         shape(*packed),
         [pltpu.VMEM(packed, f32)] * 3 + [pltpu.VMEM(plane, f32)],
     )
     edges = lax.all_to_all(answered, "hor", split_axis=0, concat_axis=0, tiled=True)
     other_edges = lax.ppermute(edges, "dep", pairs)
     scratch = [pltpu.VMEM((layers, half), f32)] * 2 + [pltpu.VMEM(field, f32)] * 2
-    own, focus_map = call(
-        functools.partial(restore_kernel, ends=(near, far)),
+    base, gain = call(
+        functools.partial(restore_kernel, ends=(near, far), scale=1.0 / x_cells),
         [scalar(dep_index)]
         + [
             near_by(v)
             for v in (edges, keep, table_here, small_here, weight, inverse, focus_bins)
         ],
-        [shape(*slab), shape(*full)],
+        [shape(*full)] * 2,
         scratch,
     )
     return call(
-        functools.partial(unfold_kernel, ends=(near, far), scale=1.0 / x_cells, cuts=cuts),
+        functools.partial(unfold_kernel, ends=(near, far), cuts=cuts),
         [scalar(dep_index)]
         + [
             near_by(v)
@@ -753,8 +799,8 @@
                 small_here,
                 weight,
                 inverse_other,
-                own,
-                focus_map,
+                base,
+                gain,
             )
         ],
         shape(*full),

time: 32.6 us -> 32.6 us (level)
  transfers between devices with their start and end apart: 3 -> 3, of which waited for: 1 -> 1; matrix products, arithmetic and copies ran while one was open for 0% -> 0% of each run, Pallas kernels for 8% -> 7%
where the time goes in v5:
time: 32.6 us; the launch traced here: 32.4 us
  blocking collectives  24.3 us (75%)
  Pallas kernels  6.95 us (21%)
  starting transfers between devices  0.64 us (2%)
  waiting for transfers between devices  0.4 us (1%)
    all_to_all x1, blocking collectives, body(): lax.all_to_all(outgoing, 'hor', split_axis=0, concat_axis=0, tiled=True)  14.5 us
    all_to_all x1, blocking collectives, body(): lax.all_to_all(answered, 'hor', split_axis=0, concat_axis=0, tiled=True)  9.74 us
    pallas_call x6, Pallas kernels, call(): pl.pallas_call(kernel, in_specs=specs, out_specs=out_specs if single else...  6.95 us
  transfers between devices with their start and end apart: 3, of which 1 were waited for; matrix products, arithmetic and copies ran while one was open for 0% of the time, Pallas kernels for 7%

profile of v5, /device:TPU:0, one launch (start us, length us, event | category | flops | bytes accessed | tf_op | source)
XLA Modules:
  0.0 32.4 jit_solution(2628142793833328826)
XLA Ops:
  0.0 1.3 %shard_map.73 = (f32[16,8,512]{2,1,0:T(8,128)S(1)}, f32[16,8,512]{2,1,0:T(8,128)S(1)}, f32[32,8,128]{2,1,0:T(8,128)S(1)}, bf16[320,128]{1,0:T(8,128)(2,1)S(1)}, ...) custom-call(s32[1]{0:T(128)} %bitcast.dep_ref, f32[16,8,1024]{2,1,0:T(8,128)} %residual_hbm.1, s32[16,8,1024]{2,1,0:T(8,128)} %bins_ref.1, ...), custom_call_target="tpu_custom_call" | custom-call | tf_op jit(solution)/shard_map/pallas_call | solution.py:663
  1.3 0.5 %collective-permute-start = (f32[16,8,512]{2,1,0:T(8,128)S(1)}, f32[16,8,512]{2,1,0:T(8,128)S(1)}, u32[]{:S(2)}, u32[]{:S(2)}) collective-permute-start(f32[16,8,512]{2,1,0:T(8,128)S(1)} %get-tuple-element.29), channel_id=1, source_target_pairs={{0,1},{1,0},{2,3},{3,2},{4,5},{5,4},{6,7},{7,6},{8,9},{9,8},{10,11... | collective-permute-start | bytes 786440 | tf_op jit(solution)/shard_map/ppermute | solution.py:747
  1.9 1.5 %shard_map.74 = (f32[16,8,512]{2,1,0:T(8,128)S(1)}, bf16[2,512,512]{2,1,0:T(8,128)(2,1)S(1)}, f32[32,8,512]{2,1,0:T(8,128)S(1)}, f32[32,8,512]{2,1,0:T(8,128)S(1)}, f32[32,32,128]{2,1,0:T(8,128)S(1)}) custom-call(s32[1]{0:T(128)} %bitcast.dep_ref, s32[1]{0:T(128)} %bitcast.1.spot_ref, f32[16,8,512]{2,1,0:T(8,128)S(1)} %get-tuple-element.23.own_ref, ...), custom_call_target="tpu_custom_call" | custom-call | tf_op jit(solution)/shard_map/pallas_call | solution.py:663
  3.4 0.0 copy-start.1
  3.4 0.0 collective-permute-done.recv_ref
  3.4 1.0 %shard_map.75 = (f32[8,32,128]{2,1,0:T(8,128)S(1)}, f32[16,8,512]{2,1,0:T(8,128)S(1)}, f32[16,8,512]{2,1,0:T(8,128)S(1)}) custom-call(s32[1]{0:T(128)} %bitcast.dep_ref, f32[16,8,512]{2,1,0:T(8,128)S(1)} %get-tuple-element.28.modes_ref, f32[16,8,512]{2,1,0:T(8,128)S(1)} %collective-permute-done.recv_ref, ...), custom_call_target="tpu_custom_call" | custom-call | tf_op jit(solution)/shard_map/pallas_call | solution.py:663
  4.4 0.0 copy-start
  4.4 0.1 collective-permute-start.1
  4.5 14.5 %all_to_all.10.packed_ref = f32[8,32,128]{2,1,0:T(8,128)S(1)} all-to-all(f32[8,32,128]{2,1,0:T(8,128)S(1)} %get-tuple-element.32), channel_id=1, replica_groups=mesh['grp'=2,'hor'=8,'dep'=2] {'hor'}, dimensions={0} | all-to-all | bytes 262144 | tf_op jit(solution)/shard_map/all_to_all | solution.py:769
  19.1 0.0 collective-permute-done.1.solved_ref
  19.1 0.5 %shard_map.76 = f32[8,32,128]{2,1,0:T(8,128)S(1)} custom-call(s32[1]{0:T(128)} %bitcast.1.spot_ref, f32[8,32,128]{2,1,0:T(8,128)S(1)} %all_to_all.10.packed_ref, f32[32,8,128]{2,1,0:T(8,128)S(1)} %get-tuple-element.24.weight_ref, f32[32,32,128]{2,1,0:T(8,128)S(1)} %get-tuple-element.35.inverse_ref), custom_call_target="tpu_custom_call" | custom-call | tf_op jit(solution)/shard_map/pallas_call | solution.py:663
  19.6 9.7 %all_to_all.11.back_ref = f32[8,32,128]{2,1,0:T(8,128)S(1)} all-to-all(f32[8,32,128]{2,1,0:T(8,128)S(1)} %shard_map.76), channel_id=1, replica_groups=mesh['grp'=2,'hor'=8,'dep'=2] {'hor'}, dimensions={0} | all-to-all | bytes 262144 | tf_op jit(solution)/shard_map/all_to_all | solution.py:777
  29.3 0.0 collective-permute-start.2
  29.3 0.0 copy-done.1
  29.3 0.9 %shard_map.77 = (f32[16,8,1024]{2,1,0:T(8,128)S(1)}, f32[16,8,1024]{2,1,0:T(8,128)S(1)}) custom-call(s32[1]{0:T(128)} %bitcast.dep_ref, f32[8,32,128]{2,1,0:T(8,128)S(1)} %all_to_all.11.back_ref, f32[16,8,512]{2,1,0:T(8,128)S(1)} %get-tuple-element.38.solved_ref, bf16[2,512,512]{2,1,0:T(8,128)(2,1)S(1)} %get-tuple-element.30.table_ref, ...), custom_call_target="tpu_custom_call" | custom-call | tf_op jit(solution)/shard_map/pallas_call | solution.py:663
  30.3 0.4 %collective-permute-done.2.back_ref = f32[8,32,128]{2,1,0:T(8,128)S(1)} collective-permute-done((f32[8,32,128]{2,1,0:T(8,128)S(1)}, f32[8,32,128]{2,1,0:T(8,128)S(1)}, u32[]{:S(2)}, u32[]{:S(2)}) %collective-permute-start.2) | collective-permute-done | bytes 131104 | tf_op jit(solution)/shard_map/ppermute | solution.py:778
  30.7 0.0 copy-done
  30.7 1.7 %shard_map.78 = f32[16,8,1024]{2,1,0:T(8,128)} custom-call(s32[1]{0:T(128)} %bitcast.dep_ref, f32[8,32,128]{2,1,0:T(8,128)S(1)} %collective-permute-done.2.back_ref, f32[16,8,512]{2,1,0:T(8,128)S(1)} %collective-permute-done.1.solved_ref, bf16[2,2,512,512]{3,2,1,0:T(8,128)(2,1)S(1)} %copy-done, bf16[320,128]{1,0:T(8,128)(2,1)S(1)} %get-tuple-element.25.small_ref, ...), custom_call_target="tpu_custom_call" | custom-call | tf_op jit(solution)/shard_map/pallas_call | solution.py:663
Async XLA Ops:
  1.3 2.0 %collective-permute-start = (f32[16,8,512]{2,1,0:T(8,128)S(1)}, f32[16,8,512]{2,1,0:T(8,128)S(1)}, u32[]{:S(2)}, u32[]{:S(2)}) collective-permute-start(f32[16,8,512]{2,1,0:T(8,128)S(1)} %get-tuple-element.29), channel_id=1, source_target_pairs={{0,1},{1,0},{2,3},{3,2},{4,5},{5,4},{6,7},{7,6},{8,9},{9,8},{10,11... | collective-permute-start | bytes 786440 | tf_op jit(solution)/shard_map/ppermute | solution.py:747
  3.4 26.0 %copy-start.1 = (s32[16,8,1024]{2,1,0:T(8,128)S(1)}, s32[16,8,1024]{2,1,0:T(8,128)}, u32[]{:S(2)}) copy-start(s32[16,8,1024]{2,1,0:T(8,128)} %bins_ref.1) | copy-start | bytes 1572868
  4.4 26.3 %copy-start = (bf16[2,2,512,512]{3,2,1,0:T(8,128)(2,1)S(1)}, bf16[2,2,512,512]{3,2,1,0:T(8,128)(2,1)}, u32[]{:S(2)}) copy-start(bf16[2,2,512,512]{3,2,1,0:T(8,128)(2,1)} %constant.21.clone.table_hbm.table_ref) | copy-start | bytes 6291460
  4.4 14.7 %collective-permute-start.1 = (f32[16,8,512]{2,1,0:T(8,128)S(1)}, f32[16,8,512]{2,1,0:T(8,128)S(1)}, u32[]{:S(2)}, u32[]{:S(2)}) collective-permute-start(f32[16,8,512]{2,1,0:T(8,128)S(1)} %get-tuple-element.33), channel_id=1, source_target_pairs={{0,1},{1,0},{2,3},{3,2},{4,5},{5,4},{6,7},{7,6},{8,9},{9,8},{10,11... | collective-permute-start | bytes 786440 | tf_op jit(solution)/shard_map/ppermute | solution.py:768
  29.3 1.3 %collective-permute-start.2 = (f32[8,32,128]{2,1,0:T(8,128)S(1)}, f32[8,32,128]{2,1,0:T(8,128)S(1)}, u32[]{:S(2)}, u32[]{:S(2)}) collective-permute-start(f32[8,32,128]{2,1,0:T(8,128)S(1)} %all_to_all.11.back_ref), channel_id=1, source_target_pairs={{0,1},{1,0},{2,3},{3,2},{4,5},{5,4},{6,7},{7,6},{8,9},{9,8},{10,11... | collective-permute-start | bytes 393224 | tf_op jit(solution)/shard_map/ppermute | solution.py:778

commit v6 on v5

--- a/solution.py
+++ b/solution.py
@@ -234,13 +234,12 @@
 
 def from_modes(modes, sine):
     depth, rows, half = modes.shape
-    return dot3(sine, split(modes.reshape(depth * rows, half)))
+    high, low = split(modes.reshape(depth * rows, half))
+    return dot2(sine, jnp.concatenate([high, low, high], axis=0))
 
 
 def parts_of(small_ref, block, depth):
-    cuts = np.cumsum([0, block, block, 2 * depth, 2 * depth])
-    pieces = [small_ref[low:high] for low, high in zip(cuts[:-1], cuts[1:])]
-    return (pieces[0], pieces[1]), (pieces[2], pieces[3])
+    return small_ref[:block], small_ref[block : block + 2 * depth]
 
 
 def prepare_kernel(
@@ -458,12 +457,13 @@
             (layers, lanes),
         )
     weights, couple = layer_terms(weight_ref, rows // 8, 0)
+    turned = jnp.swapaxes(wave_ref[...], 0, 1) if classes == 1 else None
     plane_lane = lax.broadcasted_iota(jnp.int32, (rows, lanes), 1)
     group = plane_lane // chunk % classes
 
     def source(layer):
         if classes == 1:
-            return jnp.concatenate([wave_ref[:, layer, :]] * repeats, axis=0)
+            return jnp.concatenate([turned[layer]] * repeats, axis=0)
         total = wave_ref[0:rows, layer, :]
         for part in range(1, classes):
             piece = wave_ref[part * rows : (part + 1) * rows, layer, :]
@@ -475,14 +475,17 @@
             total = values[0:hor_count]
             for part in range(1, repeats):
                 total = total + values[part * hor_count : (part + 1) * hor_count]
-            answer_ref[:, layer, :] = total
+            gathering[layer] = total
             return
         for part in range(classes):
             answer_ref[part * rows : (part + 1) * rows, layer, :] = jnp.where(
                 group == part, values, 0.0
             )
 
+    gathering = [None] * layers
     substitute(couple, inverse_ref, partial_ref, source, emit)
+    if classes == 1:
+        answer_ref[...] = jnp.swapaxes(jnp.stack(gathering), 0, 1)
 
     def gathered(index):
         values = answer_ref[index]
@@ -689,7 +692,8 @@
     far = np.concatenate([[0.0], sine[rows - 1, 1:]])
     lower_row = np.concatenate([[1.0], sine[1, 1:]])
     edge = np.concatenate([np.kron(np.eye(depth), row[None, :]) for row in (lower_row, far)])
-    small = np.concatenate(split_table(np.kron(np.eye(depth), sine)) + split_table(edge))
+    high, low = split_table(np.concatenate([np.kron(np.eye(depth), sine), edge]))
+    small = np.concatenate([high, high, low], axis=1)
     wave_x = np.stack(
         [symbol_of(2.0 * np.pi * (2 * np.arange(half) + parity) / x_cells) for parity in range(2)]
     )

time: 32.6 us -> 32.4 us (level)
  no operation moved by 1% of the time
where the time goes in v6:
time: 32.4 us; the launch traced here: 32.2 us
  blocking collectives  24.3 us (75%)
  Pallas kernels  6.78 us (21%)
  starting transfers between devices  0.64 us (2%)
  waiting for transfers between devices  0.43 us (1%)
    all_to_all x1, blocking collectives, body(): lax.all_to_all(outgoing, 'hor', split_axis=0, concat_axis=0, tiled=True)  14.5 us
    all_to_all x1, blocking collectives, body(): lax.all_to_all(answered, 'hor', split_axis=0, concat_axis=0, tiled=True)  9.74 us
    pallas_call x6, Pallas kernels, call(): pl.pallas_call(kernel, in_specs=specs, out_specs=out_specs if single else...  6.78 us
  transfers between devices with their start and end apart: 3, of which 1 were waited for; matrix products, arithmetic and copies ran while one was open for 0% of the time, Pallas kernels for 7%

profile of v6, /device:TPU:0, one launch (start us, length us, event | category | flops | bytes accessed | tf_op | source)
XLA Modules:
  0.0 32.2 jit_solution(13972274315167228068)
XLA Ops:
  0.0 1.3 %shard_map.73 = (f32[16,8,512]{2,1,0:T(8,128)S(1)}, f32[16,8,512]{2,1,0:T(8,128)S(1)}, f32[32,8,128]{2,1,0:T(8,128)S(1)}, bf16[160,384]{1,0:T(8,128)(2,1)S(1)}, ...) custom-call(s32[1]{0:T(128)} %bitcast.dep_ref, f32[16,8,1024]{2,1,0:T(8,128)} %residual_hbm.1, s32[16,8,1024]{2,1,0:T(8,128)} %bins_ref.1, ...), custom_call_target="tpu_custom_call" | custom-call | tf_op jit(solution)/shard_map/pallas_call | solution.py:666
  1.3 0.5 %collective-permute-start = (f32[16,8,512]{2,1,0:T(8,128)S(1)}, f32[16,8,512]{2,1,0:T(8,128)S(1)}, u32[]{:S(2)}, u32[]{:S(2)}) collective-permute-start(f32[16,8,512]{2,1,0:T(8,128)S(1)} %get-tuple-element.29), channel_id=1, source_target_pairs={{0,1},{1,0},{2,3},{3,2},{4,5},{5,4},{6,7},{7,6},{8,9},{9,8},{10,11... | collective-permute-start | bytes 786440 | tf_op jit(solution)/shard_map/ppermute | solution.py:751
  1.9 1.5 %shard_map.74 = (f32[16,8,512]{2,1,0:T(8,128)S(1)}, bf16[2,512,512]{2,1,0:T(8,128)(2,1)S(1)}, f32[32,8,512]{2,1,0:T(8,128)S(1)}, f32[32,8,512]{2,1,0:T(8,128)S(1)}, f32[32,32,128]{2,1,0:T(8,128)S(1)}) custom-call(s32[1]{0:T(128)} %bitcast.dep_ref, s32[1]{0:T(128)} %bitcast.1.spot_ref, f32[16,8,512]{2,1,0:T(8,128)S(1)} %get-tuple-element.23.own_ref, ...), custom_call_target="tpu_custom_call" | custom-call | tf_op jit(solution)/shard_map/pallas_call | solution.py:666
  3.4 0.0 copy-start.1
  3.4 0.0 collective-permute-done.recv_ref
  3.4 1.0 %shard_map.75 = (f32[8,32,128]{2,1,0:T(8,128)S(1)}, f32[16,8,512]{2,1,0:T(8,128)S(1)}, f32[16,8,512]{2,1,0:T(8,128)S(1)}) custom-call(s32[1]{0:T(128)} %bitcast.dep_ref, f32[16,8,512]{2,1,0:T(8,128)S(1)} %get-tuple-element.28.modes_ref, f32[16,8,512]{2,1,0:T(8,128)S(1)} %collective-permute-done.recv_ref, ...), custom_call_target="tpu_custom_call" | custom-call | tf_op jit(solution)/shard_map/pallas_call | solution.py:666
  4.4 0.1 collective-permute-start.1
  4.5 0.0 copy-start
  4.5 14.5 %all_to_all.10.packed_ref = f32[8,32,128]{2,1,0:T(8,128)S(1)} all-to-all(f32[8,32,128]{2,1,0:T(8,128)S(1)} %get-tuple-element.32), channel_id=1, replica_groups=mesh['grp'=2,'hor'=8,'dep'=2] {'hor'}, dimensions={0} | all-to-all | bytes 262144 | tf_op jit(solution)/shard_map/all_to_all | solution.py:773
  19.1 0.0 collective-permute-done.1.solved_ref
  19.1 0.4 %shard_map.76 = f32[8,32,128]{2,1,0:T(8,128)S(1)} custom-call(s32[1]{0:T(128)} %bitcast.1.spot_ref, f32[8,32,128]{2,1,0:T(8,128)S(1)} %all_to_all.10.packed_ref, f32[32,8,128]{2,1,0:T(8,128)S(1)} %get-tuple-element.24.weight_ref, f32[32,32,128]{2,1,0:T(8,128)S(1)} %get-tuple-element.35.inverse_ref), custom_call_target="tpu_custom_call" | custom-call | tf_op jit(solution)/shard_map/pallas_call | solution.py:666
  19.4 9.7 %all_to_all.11.back_ref = f32[8,32,128]{2,1,0:T(8,128)S(1)} all-to-all(f32[8,32,128]{2,1,0:T(8,128)S(1)} %shard_map.76), channel_id=1, replica_groups=mesh['grp'=2,'hor'=8,'dep'=2] {'hor'}, dimensions={0} | all-to-all | bytes 262144 | tf_op jit(solution)/shard_map/all_to_all | solution.py:781
  29.2 0.0 collective-permute-start.2
  29.2 0.0 copy-done.1
  29.2 0.9 %shard_map.77 = (f32[16,8,1024]{2,1,0:T(8,128)S(1)}, f32[16,8,1024]{2,1,0:T(8,128)S(1)}) custom-call(s32[1]{0:T(128)} %bitcast.dep_ref, f32[8,32,128]{2,1,0:T(8,128)S(1)} %all_to_all.11.back_ref, f32[16,8,512]{2,1,0:T(8,128)S(1)} %get-tuple-element.38.solved_ref, bf16[2,512,512]{2,1,0:T(8,128)(2,1)S(1)} %get-tuple-element.30.table_ref, ...), custom_call_target="tpu_custom_call" | custom-call | tf_op jit(solution)/shard_map/pallas_call | solution.py:666
  30.1 0.4 %collective-permute-done.2.back_ref = f32[8,32,128]{2,1,0:T(8,128)S(1)} collective-permute-done((f32[8,32,128]{2,1,0:T(8,128)S(1)}, f32[8,32,128]{2,1,0:T(8,128)S(1)}, u32[]{:S(2)}, u32[]{:S(2)}) %collective-permute-start.2) | collective-permute-done | bytes 131104 | tf_op jit(solution)/shard_map/ppermute | solution.py:782
  30.5 0.0 copy-done
  30.5 1.7 %shard_map.78 = f32[16,8,1024]{2,1,0:T(8,128)} custom-call(s32[1]{0:T(128)} %bitcast.dep_ref, f32[8,32,128]{2,1,0:T(8,128)S(1)} %collective-permute-done.2.back_ref, f32[16,8,512]{2,1,0:T(8,128)S(1)} %collective-permute-done.1.solved_ref, bf16[2,2,512,512]{3,2,1,0:T(8,128)(2,1)S(1)} %copy-done, bf16[160,384]{1,0:T(8,128)(2,1)S(1)} %get-tuple-element.25.small_ref, ...), custom_call_target="tpu_custom_call" | custom-call | tf_op jit(solution)/shard_map/pallas_call | solution.py:666
Async XLA Ops:
  1.3 2.0 %collective-permute-start = (f32[16,8,512]{2,1,0:T(8,128)S(1)}, f32[16,8,512]{2,1,0:T(8,128)S(1)}, u32[]{:S(2)}, u32[]{:S(2)}) collective-permute-start(f32[16,8,512]{2,1,0:T(8,128)S(1)} %get-tuple-element.29), channel_id=1, source_target_pairs={{0,1},{1,0},{2,3},{3,2},{4,5},{5,4},{6,7},{7,6},{8,9},{9,8},{10,11... | collective-permute-start | bytes 786440 | tf_op jit(solution)/shard_map/ppermute | solution.py:751
  3.4 25.8 %copy-start.1 = (s32[16,8,1024]{2,1,0:T(8,128)S(1)}, s32[16,8,1024]{2,1,0:T(8,128)}, u32[]{:S(2)}) copy-start(s32[16,8,1024]{2,1,0:T(8,128)} %bins_ref.1) | copy-start | bytes 1572868
  4.4 14.7 %collective-permute-start.1 = (f32[16,8,512]{2,1,0:T(8,128)S(1)}, f32[16,8,512]{2,1,0:T(8,128)S(1)}, u32[]{:S(2)}, u32[]{:S(2)}) collective-permute-start(f32[16,8,512]{2,1,0:T(8,128)S(1)} %get-tuple-element.33), channel_id=1, source_target_pairs={{0,1},{1,0},{2,3},{3,2},{4,5},{5,4},{6,7},{7,6},{8,9},{9,8},{10,11... | collective-permute-start | bytes 786440 | tf_op jit(solution)/shard_map/ppermute | solution.py:772
  4.5 26.0 %copy-start = (bf16[2,2,512,512]{3,2,1,0:T(8,128)(2,1)S(1)}, bf16[2,2,512,512]{3,2,1,0:T(8,128)(2,1)}, u32[]{:S(2)}) copy-start(bf16[2,2,512,512]{3,2,1,0:T(8,128)(2,1)} %constant.21.clone.table_hbm.table_ref) | copy-start | bytes 6291460
  29.2 1.3 %collective-permute-start.2 = (f32[8,32,128]{2,1,0:T(8,128)S(1)}, f32[8,32,128]{2,1,0:T(8,128)S(1)}, u32[]{:S(2)}, u32[]{:S(2)}) collective-permute-start(f32[8,32,128]{2,1,0:T(8,128)S(1)} %all_to_all.11.back_ref), channel_id=1, source_target_pairs={{0,1},{1,0},{2,3},{3,2},{4,5},{5,4},{6,7},{7,6},{8,9},{9,8},{10,11... | collective-permute-start | bytes 393224 | tf_op jit(solution)/shard_map/ppermute | solution.py:782

commit v7 on v6

--- a/solution.py
+++ b/solution.py
@@ -130,7 +130,7 @@
         inverse_ref[high] = bottom
 
 
-def substitute(couple, inverse_ref, partial_ref, source, emit):
+def substitute(couple, inverse_ref, partial_ref, source, emit, side=None):
     layers = len(couple) + 1
     half = layers // 2
     top = source(0)
@@ -147,15 +147,19 @@
     link = couple[half - 1]
     bottom = (bottom + link * inverse_ref[half - 1] * top) * inverse_ref[half]
     top = (top + link * bottom) * inverse_ref[half - 1]
-    emit(half, bottom)
-    emit(half - 1, top)
+    if side != 0:
+        emit(half, bottom)
+    if side != 1:
+        emit(half - 1, top)
     for step in range(1, half):
-        low = half - 1 - step
-        top = (partial_ref[low] + couple[low] * top) * inverse_ref[low]
-        emit(low, top)
-        high = half + step
-        bottom = (partial_ref[high] + couple[high - 1] * bottom) * inverse_ref[high]
-        emit(high, bottom)
+        if side != 1:
+            low = half - 1 - step
+            top = (partial_ref[low] + couple[low] * top) * inverse_ref[low]
+            emit(low, top)
+        if side != 0:
+            high = half + step
+            bottom = (partial_ref[high] + couple[high - 1] * bottom) * inverse_ref[high]
+            emit(high, bottom)
 
 
 def turn(values, shift):
@@ -512,7 +516,7 @@
 
 
 def extend(
-    dep_ref,
+    side,
     back_ref,
     solved_ref,
     table,
@@ -521,7 +525,6 @@
     inverse_ref,
     left_ref,
     right_ref,
-    stage_ref,
     partial_ref,
     ends,
 ):
@@ -561,14 +564,17 @@
         pull = near * row_of(left_ref, layer) + far * row_of(right_ref, layer)
         return weights[layer] * pull
 
+    edge_row = lax.broadcasted_iota(jnp.int32, (rows, half), 0) == 0
+    place = side * depth
+    found = [None] * depth
+
     def emit(layer, values):
-        stage_ref[layer] = values
-
-    substitute(couple, inverse_ref, partial_ref, source, emit)
-    place = pl.multiple_of(dep_ref[0] * depth, depth)
-    edge_row = lax.broadcasted_iota(jnp.int32, (depth, rows, half), 1) == 0
-    edge = left_ref[pl.ds(place, depth), :]
-    modes = jnp.where(edge_row, edge[:, None, :], solved_ref[...] + stage_ref[pl.ds(place, depth)])
+        layer_here = layer - place
+        total = solved_ref[layer_here] + values
+        found[layer_here] = jnp.where(edge_row, row_of(left_ref, layer), total)
+
+    substitute(couple, inverse_ref, partial_ref, source, emit, side)
+    modes = jnp.stack(found)
     sine, _ = parts_of(small_ref, depth * rows, depth)
     waves = from_modes(modes, sine)
     cells = dot3(split(waves), table, (((1,), (1,)), ((), ())))
@@ -591,22 +597,22 @@
     scale,
 ):
     half = solved_ref.shape[-1]
-    sign = jnp.where(dep_ref[0] == 0, -scale, scale).astype(f32)
-    gain_ref[:, :, :half] = focusing(bins_ref[:, :, :half]) * scale
-    gain_ref[:, :, half:] = focusing(bins_ref[:, :, half:]) * sign
-    cells = extend(
-        dep_ref,
-        back_ref,
-        solved_ref,
-        (table_ref[0], table_ref[1]),
-        small_ref,
-        weight_ref,
-        inverse_ref,
-        *scratch,
-        ends,
-    )
-    base_ref[:, :, :half] = gain_ref[:, :, :half] * cells
-    base_ref[:, :, half:] = -(gain_ref[:, :, half:] * cells)
+
+    def work(side):
+        sign = scale if side else -scale
+        left = focusing(bins_ref[:, :, :half]) * scale
+        right = focusing(bins_ref[:, :, half:]) * sign
+        gain_ref[:, :, :half] = left
+        gain_ref[:, :, half:] = right
+        table = (table_ref[0], table_ref[1])
+        cells = extend(
+            side, back_ref, solved_ref, table, small_ref, weight_ref, inverse_ref, *scratch, ends
+        )
+        base_ref[:, :, :half] = gain_ref[:, :, :half] * cells
+        base_ref[:, :, half:] = -(gain_ref[:, :, half:] * cells)
+
+    pl.when(dep_ref[0] == 0)(lambda: work(0))
+    pl.when(dep_ref[0] == 1)(lambda: work(1))
 
 
 def unfold_kernel(
@@ -628,28 +634,27 @@
 ):
     depth, _, half = solved_ref.shape
     size = depth // cuts
-    other = 1 - dep_ref[0]
-    cells = extend(
-        dep_ref,
-        back_ref,
-        solved_ref,
-        (table_ref[other, 0], table_ref[other, 1]),
-        small_ref,
-        weight_ref,
-        inverse_ref,
-        *scratch,
-        ends,
-    )
-    copies = []
-    for cut in range(cuts):
-        part = slice(cut * size, (cut + 1) * size)
-        out_ref[part, :, :half] = base_ref[part, :, :half] + gain_ref[part, :, :half] * cells[part]
-        out_ref[part, :, half:] = base_ref[part, :, half:] + gain_ref[part, :, half:] * cells[part]
-        copy = pltpu.make_async_copy(out_ref.at[part], out_hbm.at[part], sems.at[cut])
-        copy.start()
-        copies.append(copy)
-    for copy in copies:
-        copy.wait()
+
+    def work(side):
+        table = (table_ref[1 - side, 0], table_ref[1 - side, 1])
+        cells = extend(
+            side, back_ref, solved_ref, table, small_ref, weight_ref, inverse_ref, *scratch, ends
+        )
+        copies = []
+        for cut in range(cuts):
+            part = slice(cut * size, (cut + 1) * size)
+            for ends_here in (slice(0, half), slice(half, 2 * half)):
+                out_ref[part, :, ends_here] = (
+                    base_ref[part, :, ends_here] + gain_ref[part, :, ends_here] * cells[part]
+                )
+            copy = pltpu.make_async_copy(out_ref.at[part], out_hbm.at[part], sems.at[cut])
+            copy.start()
+            copies.append(copy)
+        for copy in copies:
+            copy.wait()
+
+    pl.when(dep_ref[0] == 0)(lambda: work(0))
+    pl.when(dep_ref[0] == 1)(lambda: work(1))
 
 
 def call(kernel, operands, out_shape, scratch=(), outside=False):
@@ -780,7 +785,7 @@
     )
     edges = lax.all_to_all(answered, "hor", split_axis=0, concat_axis=0, tiled=True)
     other_edges = lax.ppermute(edges, "dep", pairs)
-    scratch = [pltpu.VMEM((layers, half), f32)] * 2 + [pltpu.VMEM(field, f32)] * 2
+    scratch = [pltpu.VMEM((layers, half), f32)] * 2 + [pltpu.VMEM(field, f32)]
     base, gain = call(
         functools.partial(restore_kernel, ends=(near, far), scale=1.0 / x_cells),
         [scalar(dep_index)]

time: 32.4 us -> 32.4 us (level)
  no operation moved by 1% of the time
where the time goes in v7:
time: 32.4 us; the launch traced here: 32.2 us
  blocking collectives  24.3 us (75%)
  Pallas kernels  6.71 us (21%)
  starting transfers between devices  0.64 us (2%)
  waiting for transfers between devices  0.46 us (1%)
    all_to_all x1, blocking collectives, body(): lax.all_to_all(outgoing, 'hor', split_axis=0, concat_axis=0, tiled=True)  14.5 us
    all_to_all x1, blocking collectives, body(): lax.all_to_all(answered, 'hor', split_axis=0, concat_axis=0, tiled=True)  9.74 us
    pallas_call x6, Pallas kernels, call(): pl.pallas_call(kernel, in_specs=specs, out_specs=out_specs if single else...  6.71 us
  transfers between devices with their start and end apart: 3, of which 1 were waited for; matrix products, arithmetic and copies ran while one was open for 0% of the time, Pallas kernels for 7%

profile of v7, /device:TPU:0, one launch (start us, length us, event | category | flops | bytes accessed | tf_op | source)
XLA Modules:
  0.0 32.2 jit_solution(2705036679175616985)
XLA Ops:
  0.0 1.3 %shard_map.73 = (f32[16,8,512]{2,1,0:T(8,128)S(1)}, f32[16,8,512]{2,1,0:T(8,128)S(1)}, f32[32,8,128]{2,1,0:T(8,128)S(1)}, bf16[160,384]{1,0:T(8,128)(2,1)S(1)}, ...) custom-call(s32[1]{0:T(128)} %bitcast.dep_ref, f32[16,8,1024]{2,1,0:T(8,128)} %residual_hbm.1, s32[16,8,1024]{2,1,0:T(8,128)} %bins_ref.1, ...), custom_call_target="tpu_custom_call" | custom-call | tf_op jit(solution)/shard_map/pallas_call | solution.py:671
  1.3 0.5 %collective-permute-start = (f32[16,8,512]{2,1,0:T(8,128)S(1)}, f32[16,8,512]{2,1,0:T(8,128)S(1)}, u32[]{:S(2)}, u32[]{:S(2)}) collective-permute-start(f32[16,8,512]{2,1,0:T(8,128)S(1)} %get-tuple-element.29), channel_id=1, source_target_pairs={{0,1},{1,0},{2,3},{3,2},{4,5},{5,4},{6,7},{7,6},{8,9},{9,8},{10,11... | collective-permute-start | bytes 786440 | tf_op jit(solution)/shard_map/ppermute | solution.py:756
  1.9 1.5 %shard_map.74 = (f32[16,8,512]{2,1,0:T(8,128)S(1)}, bf16[2,512,512]{2,1,0:T(8,128)(2,1)S(1)}, f32[32,8,512]{2,1,0:T(8,128)S(1)}, f32[32,8,512]{2,1,0:T(8,128)S(1)}, f32[32,32,128]{2,1,0:T(8,128)S(1)}) custom-call(s32[1]{0:T(128)} %bitcast.dep_ref, s32[1]{0:T(128)} %bitcast.1.spot_ref, f32[16,8,512]{2,1,0:T(8,128)S(1)} %get-tuple-element.23.own_ref, ...), custom_call_target="tpu_custom_call" | custom-call | tf_op jit(solution)/shard_map/pallas_call | solution.py:671
  3.4 0.0 copy-start.1
  3.4 0.0 collective-permute-done.recv_ref
  3.4 1.0 %shard_map.75 = (f32[8,32,128]{2,1,0:T(8,128)S(1)}, f32[16,8,512]{2,1,0:T(8,128)S(1)}, f32[16,8,512]{2,1,0:T(8,128)S(1)}) custom-call(s32[1]{0:T(128)} %bitcast.dep_ref, f32[16,8,512]{2,1,0:T(8,128)S(1)} %get-tuple-element.28.modes_ref, f32[16,8,512]{2,1,0:T(8,128)S(1)} %collective-permute-done.recv_ref, ...), custom_call_target="tpu_custom_call" | custom-call | tf_op jit(solution)/shard_map/pallas_call | solution.py:671
  4.4 0.1 collective-permute-start.1
  4.5 0.0 copy-start
  4.5 14.5 %all_to_all.10.packed_ref = f32[8,32,128]{2,1,0:T(8,128)S(1)} all-to-all(f32[8,32,128]{2,1,0:T(8,128)S(1)} %get-tuple-element.32), channel_id=1, replica_groups=mesh['grp'=2,'hor'=8,'dep'=2] {'hor'}, dimensions={0} | all-to-all | bytes 262144 | tf_op jit(solution)/shard_map/all_to_all | solution.py:778
  19.1 0.0 collective-permute-done.1.solved_ref
  19.1 0.4 %shard_map.76 = f32[8,32,128]{2,1,0:T(8,128)S(1)} custom-call(s32[1]{0:T(128)} %bitcast.1.spot_ref, f32[8,32,128]{2,1,0:T(8,128)S(1)} %all_to_all.10.packed_ref, f32[32,8,128]{2,1,0:T(8,128)S(1)} %get-tuple-element.24.weight_ref, f32[32,32,128]{2,1,0:T(8,128)S(1)} %get-tuple-element.35.inverse_ref), custom_call_target="tpu_custom_call" | custom-call | tf_op jit(solution)/shard_map/pallas_call | solution.py:671
  19.4 9.7 %all_to_all.11.back_ref = f32[8,32,128]{2,1,0:T(8,128)S(1)} all-to-all(f32[8,32,128]{2,1,0:T(8,128)S(1)} %shard_map.76), channel_id=1, replica_groups=mesh['grp'=2,'hor'=8,'dep'=2] {'hor'}, dimensions={0} | all-to-all | bytes 262144 | tf_op jit(solution)/shard_map/all_to_all | solution.py:786
  29.2 0.0 collective-permute-start.2
  29.2 0.0 copy-done.1
  29.2 0.9 %shard_map.77 = (f32[16,8,1024]{2,1,0:T(8,128)S(1)}, f32[16,8,1024]{2,1,0:T(8,128)S(1)}) custom-call(s32[1]{0:T(128)} %bitcast.dep_ref, f32[8,32,128]{2,1,0:T(8,128)S(1)} %all_to_all.11.back_ref, f32[16,8,512]{2,1,0:T(8,128)S(1)} %get-tuple-element.38.solved_ref, bf16[2,512,512]{2,1,0:T(8,128)(2,1)S(1)} %get-tuple-element.30.table_ref, ...), custom_call_target="tpu_custom_call" | custom-call | tf_op jit(solution)/shard_map/pallas_call | solution.py:671
  30.1 0.5 %collective-permute-done.2.back_ref = f32[8,32,128]{2,1,0:T(8,128)S(1)} collective-permute-done((f32[8,32,128]{2,1,0:T(8,128)S(1)}, f32[8,32,128]{2,1,0:T(8,128)S(1)}, u32[]{:S(2)}, u32[]{:S(2)}) %collective-permute-start.2) | collective-permute-done | bytes 131104 | tf_op jit(solution)/shard_map/ppermute | solution.py:787
  30.5 0.0 copy-done
  30.5 1.6 %shard_map.78 = f32[16,8,1024]{2,1,0:T(8,128)} custom-call(s32[1]{0:T(128)} %bitcast.dep_ref, f32[8,32,128]{2,1,0:T(8,128)S(1)} %collective-permute-done.2.back_ref, f32[16,8,512]{2,1,0:T(8,128)S(1)} %collective-permute-done.1.solved_ref, bf16[2,2,512,512]{3,2,1,0:T(8,128)(2,1)S(1)} %copy-done, bf16[160,384]{1,0:T(8,128)(2,1)S(1)} %get-tuple-element.25.small_ref, ...), custom_call_target="tpu_custom_call" | custom-call | tf_op jit(solution)/shard_map/pallas_call | solution.py:671
Async XLA Ops:
  1.3 2.0 %collective-permute-start = (f32[16,8,512]{2,1,0:T(8,128)S(1)}, f32[16,8,512]{2,1,0:T(8,128)S(1)}, u32[]{:S(2)}, u32[]{:S(2)}) collective-permute-start(f32[16,8,512]{2,1,0:T(8,128)S(1)} %get-tuple-element.29), channel_id=1, source_target_pairs={{0,1},{1,0},{2,3},{3,2},{4,5},{5,4},{6,7},{7,6},{8,9},{9,8},{10,11... | collective-permute-start | bytes 786440 | tf_op jit(solution)/shard_map/ppermute | solution.py:756
  3.4 25.8 %copy-start.1 = (s32[16,8,1024]{2,1,0:T(8,128)S(1)}, s32[16,8,1024]{2,1,0:T(8,128)}, u32[]{:S(2)}) copy-start(s32[16,8,1024]{2,1,0:T(8,128)} %bins_ref.1) | copy-start | bytes 1572868
  4.4 14.7 %collective-permute-start.1 = (f32[16,8,512]{2,1,0:T(8,128)S(1)}, f32[16,8,512]{2,1,0:T(8,128)S(1)}, u32[]{:S(2)}, u32[]{:S(2)}) collective-permute-start(f32[16,8,512]{2,1,0:T(8,128)S(1)} %get-tuple-element.33), channel_id=1, source_target_pairs={{0,1},{1,0},{2,3},{3,2},{4,5},{5,4},{6,7},{7,6},{8,9},{9,8},{10,11... | collective-permute-start | bytes 786440 | tf_op jit(solution)/shard_map/ppermute | solution.py:777
  4.5 26.0 %copy-start = (bf16[2,2,512,512]{3,2,1,0:T(8,128)(2,1)S(1)}, bf16[2,2,512,512]{3,2,1,0:T(8,128)(2,1)}, u32[]{:S(2)}) copy-start(bf16[2,2,512,512]{3,2,1,0:T(8,128)(2,1)} %constant.21.clone.table_hbm.table_ref) | copy-start | bytes 6291460
  29.2 1.3 %collective-permute-start.2 = (f32[8,32,128]{2,1,0:T(8,128)S(1)}, f32[8,32,128]{2,1,0:T(8,128)S(1)}, u32[]{:S(2)}, u32[]{:S(2)}) collective-permute-start(f32[8,32,128]{2,1,0:T(8,128)S(1)} %all_to_all.11.back_ref), channel_id=1, source_target_pairs={{0,1},{1,0},{2,3},{3,2},{4,5},{5,4},{6,7},{7,6},{8,9},{9,8},{10,11... | collective-permute-start | bytes 393224 | tf_op jit(solution)/shard_map/ppermute | solution.py:787

commit v8 on v7

--- a/solution.py
+++ b/solution.py
@@ -525,6 +525,7 @@
     inverse_ref,
     left_ref,
     right_ref,
+    sum_ref,
     partial_ref,
     ends,
 ):
@@ -554,15 +555,17 @@
         left_ref[:, tile * lanes : (tile + 1) * lanes] = left
         right_ref[:, tile * lanes : (tile + 1) * lanes] = right
     weights, couple = layer_terms(weight_ref, half // lanes, 1)
-    near = row_values(ends[0], (rows, half))
-    far = row_values(ends[1], (rows, half))
+    near = row_values(ends[0], (rows, lanes))
+    odd = lax.broadcasted_iota(jnp.int32, (rows, half), 0) % 2 == 1
+    sum_ref[...] = left_ref[...] + right_ref[...]
+    right_ref[...] = left_ref[...] - right_ref[...]
 
     def row_of(ref, layer):
         return jnp.broadcast_to(ref[pl.ds(layer, 1), :], (rows, half))
 
     def source(layer):
-        pull = near * row_of(left_ref, layer) + far * row_of(right_ref, layer)
-        return weights[layer] * pull
+        factors = jnp.concatenate([weight_ref[layer] * near] * (half // lanes), axis=1)
+        return factors * jnp.where(odd, row_of(sum_ref, layer), row_of(right_ref, layer))
 
     edge_row = lax.broadcasted_iota(jnp.int32, (rows, half), 0) == 0
     place = side * depth
@@ -785,9 +788,9 @@
     )
     edges = lax.all_to_all(answered, "hor", split_axis=0, concat_axis=0, tiled=True)
     other_edges = lax.ppermute(edges, "dep", pairs)
-    scratch = [pltpu.VMEM((layers, half), f32)] * 2 + [pltpu.VMEM(field, f32)]
+    scratch = [pltpu.VMEM((layers, half), f32)] * 3 + [pltpu.VMEM(field, f32)]
     base, gain = call(
-        functools.partial(restore_kernel, ends=(near, far), scale=1.0 / x_cells),
+        functools.partial(restore_kernel, ends=(near,), scale=1.0 / x_cells),
         [scalar(dep_index)]
         + [
             near_by(v)
@@ -797,7 +800,7 @@
         scratch,
     )
     return call(
-        functools.partial(unfold_kernel, ends=(near, far), cuts=cuts),
+        functools.partial(unfold_kernel, ends=(near,), cuts=cuts),
         [scalar(dep_index)]
         + [
             near_by(v)

time: 32.4 us -> 32.4 us (level)
  no operation moved by 1% of the time
where the time goes in v8:
time: 32.4 us; the launch traced here: 32.1 us
  blocking collectives  24.3 us (75%)
  Pallas kernels  6.69 us (21%)
  starting transfers between devices  0.64 us (2%)
  waiting for transfers between devices  0.46 us (1%)
    all_to_all x1, blocking collectives, body(): lax.all_to_all(outgoing, 'hor', split_axis=0, concat_axis=0, tiled=True)  14.5 us
    all_to_all x1, blocking collectives, body(): lax.all_to_all(answered, 'hor', split_axis=0, concat_axis=0, tiled=True)  9.74 us
    pallas_call x6, Pallas kernels, call(): pl.pallas_call(kernel, in_specs=specs, out_specs=out_specs if single else...  6.69 us
  transfers between devices with their start and end apart: 3, of which 1 were waited for; matrix products, arithmetic and copies ran while one was open for 0% of the time, Pallas kernels for 7%

profile of v8, /device:TPU:0, one launch (start us, length us, event | category | flops | bytes accessed | tf_op | source)
XLA Modules:
  0.0 32.1 jit_solution(17471864284849785673)
XLA Ops:
  0.0 1.3 %shard_map.73 = (f32[16,8,512]{2,1,0:T(8,128)S(1)}, f32[16,8,512]{2,1,0:T(8,128)S(1)}, f32[32,8,128]{2,1,0:T(8,128)S(1)}, bf16[160,384]{1,0:T(8,128)(2,1)S(1)}, ...) custom-call(s32[1]{0:T(128)} %bitcast.dep_ref, f32[16,8,1024]{2,1,0:T(8,128)} %residual_hbm.1, s32[16,8,1024]{2,1,0:T(8,128)} %bins_ref.1, ...), custom_call_target="tpu_custom_call" | custom-call | tf_op jit(solution)/shard_map/pallas_call | solution.py:674
  1.3 0.5 %collective-permute-start = (f32[16,8,512]{2,1,0:T(8,128)S(1)}, f32[16,8,512]{2,1,0:T(8,128)S(1)}, u32[]{:S(2)}, u32[]{:S(2)}) collective-permute-start(f32[16,8,512]{2,1,0:T(8,128)S(1)} %get-tuple-element.29), channel_id=1, source_target_pairs={{0,1},{1,0},{2,3},{3,2},{4,5},{5,4},{6,7},{7,6},{8,9},{9,8},{10,11... | collective-permute-start | bytes 786440 | tf_op jit(solution)/shard_map/ppermute | solution.py:759
  1.9 1.5 %shard_map.74 = (f32[16,8,512]{2,1,0:T(8,128)S(1)}, bf16[2,512,512]{2,1,0:T(8,128)(2,1)S(1)}, f32[32,8,512]{2,1,0:T(8,128)S(1)}, f32[32,8,512]{2,1,0:T(8,128)S(1)}, f32[32,32,128]{2,1,0:T(8,128)S(1)}) custom-call(s32[1]{0:T(128)} %bitcast.dep_ref, s32[1]{0:T(128)} %bitcast.1.spot_ref, f32[16,8,512]{2,1,0:T(8,128)S(1)} %get-tuple-element.23.own_ref, ...), custom_call_target="tpu_custom_call" | custom-call | tf_op jit(solution)/shard_map/pallas_call | solution.py:674
  3.4 0.0 copy-start.1
  3.4 0.0 collective-permute-done.recv_ref
  3.4 1.0 %shard_map.75 = (f32[8,32,128]{2,1,0:T(8,128)S(1)}, f32[16,8,512]{2,1,0:T(8,128)S(1)}, f32[16,8,512]{2,1,0:T(8,128)S(1)}) custom-call(s32[1]{0:T(128)} %bitcast.dep_ref, f32[16,8,512]{2,1,0:T(8,128)S(1)} %get-tuple-element.28.modes_ref, f32[16,8,512]{2,1,0:T(8,128)S(1)} %collective-permute-done.recv_ref, ...), custom_call_target="tpu_custom_call" | custom-call | tf_op jit(solution)/shard_map/pallas_call | solution.py:674
  4.4 0.1 collective-permute-start.1
  4.5 0.0 copy-start
  4.5 14.5 %all_to_all.10.packed_ref = f32[8,32,128]{2,1,0:T(8,128)S(1)} all-to-all(f32[8,32,128]{2,1,0:T(8,128)S(1)} %get-tuple-element.32), channel_id=1, replica_groups=mesh['grp'=2,'hor'=8,'dep'=2] {'hor'}, dimensions={0} | all-to-all | bytes 262144 | tf_op jit(solution)/shard_map/all_to_all | solution.py:781
  19.1 0.0 collective-permute-done.1.solved_ref
  19.1 0.4 %shard_map.76 = f32[8,32,128]{2,1,0:T(8,128)S(1)} custom-call(s32[1]{0:T(128)} %bitcast.1.spot_ref, f32[8,32,128]{2,1,0:T(8,128)S(1)} %all_to_all.10.packed_ref, f32[32,8,128]{2,1,0:T(8,128)S(1)} %get-tuple-element.24.weight_ref, f32[32,32,128]{2,1,0:T(8,128)S(1)} %get-tuple-element.35.inverse_ref), custom_call_target="tpu_custom_call" | custom-call | tf_op jit(solution)/shard_map/pallas_call | solution.py:674
  19.4 9.7 %all_to_all.11.back_ref = f32[8,32,128]{2,1,0:T(8,128)S(1)} all-to-all(f32[8,32,128]{2,1,0:T(8,128)S(1)} %shard_map.76), channel_id=1, replica_groups=mesh['grp'=2,'hor'=8,'dep'=2] {'hor'}, dimensions={0} | all-to-all | bytes 262144 | tf_op jit(solution)/shard_map/all_to_all | solution.py:789
  29.2 0.0 collective-permute-start.2
  29.2 0.0 copy-done.1
  29.2 0.9 %shard_map.77 = (f32[16,8,1024]{2,1,0:T(8,128)S(1)}, f32[16,8,1024]{2,1,0:T(8,128)S(1)}) custom-call(s32[1]{0:T(128)} %bitcast.dep_ref, f32[8,32,128]{2,1,0:T(8,128)S(1)} %all_to_all.11.back_ref, f32[16,8,512]{2,1,0:T(8,128)S(1)} %get-tuple-element.38.solved_ref, bf16[2,512,512]{2,1,0:T(8,128)(2,1)S(1)} %get-tuple-element.30.table_ref, ...), custom_call_target="tpu_custom_call" | custom-call | tf_op jit(solution)/shard_map/pallas_call | solution.py:674
  30.1 0.5 %collective-permute-done.2.back_ref = f32[8,32,128]{2,1,0:T(8,128)S(1)} collective-permute-done((f32[8,32,128]{2,1,0:T(8,128)S(1)}, f32[8,32,128]{2,1,0:T(8,128)S(1)}, u32[]{:S(2)}, u32[]{:S(2)}) %collective-permute-start.2) | collective-permute-done | bytes 131104 | tf_op jit(solution)/shard_map/ppermute | solution.py:790
  30.5 0.0 copy-done
  30.5 1.6 %shard_map.78 = f32[16,8,1024]{2,1,0:T(8,128)} custom-call(s32[1]{0:T(128)} %bitcast.dep_ref, f32[8,32,128]{2,1,0:T(8,128)S(1)} %collective-permute-done.2.back_ref, f32[16,8,512]{2,1,0:T(8,128)S(1)} %collective-permute-done.1.solved_ref, bf16[2,2,512,512]{3,2,1,0:T(8,128)(2,1)S(1)} %copy-done, bf16[160,384]{1,0:T(8,128)(2,1)S(1)} %get-tuple-element.25.small_ref, ...), custom_call_target="tpu_custom_call" | custom-call | tf_op jit(solution)/shard_map/pallas_call | solution.py:674
Async XLA Ops:
  1.3 2.0 %collective-permute-start = (f32[16,8,512]{2,1,0:T(8,128)S(1)}, f32[16,8,512]{2,1,0:T(8,128)S(1)}, u32[]{:S(2)}, u32[]{:S(2)}) collective-permute-start(f32[16,8,512]{2,1,0:T(8,128)S(1)} %get-tuple-element.29), channel_id=1, source_target_pairs={{0,1},{1,0},{2,3},{3,2},{4,5},{5,4},{6,7},{7,6},{8,9},{9,8},{10,11... | collective-permute-start | bytes 786440 | tf_op jit(solution)/shard_map/ppermute | solution.py:759
  3.4 25.8 %copy-start.1 = (s32[16,8,1024]{2,1,0:T(8,128)S(1)}, s32[16,8,1024]{2,1,0:T(8,128)}, u32[]{:S(2)}) copy-start(s32[16,8,1024]{2,1,0:T(8,128)} %bins_ref.1) | copy-start | bytes 1572868
  4.4 14.7 %collective-permute-start.1 = (f32[16,8,512]{2,1,0:T(8,128)S(1)}, f32[16,8,512]{2,1,0:T(8,128)S(1)}, u32[]{:S(2)}, u32[]{:S(2)}) collective-permute-start(f32[16,8,512]{2,1,0:T(8,128)S(1)} %get-tuple-element.33), channel_id=1, source_target_pairs={{0,1},{1,0},{2,3},{3,2},{4,5},{5,4},{6,7},{7,6},{8,9},{9,8},{10,11... | collective-permute-start | bytes 786440 | tf_op jit(solution)/shard_map/ppermute | solution.py:780
  4.5 26.0 %copy-start = (bf16[2,2,512,512]{3,2,1,0:T(8,128)(2,1)S(1)}, bf16[2,2,512,512]{3,2,1,0:T(8,128)(2,1)}, u32[]{:S(2)}) copy-start(bf16[2,2,512,512]{3,2,1,0:T(8,128)(2,1)} %constant.21.clone.table_hbm.table_ref) | copy-start | bytes 6291460
  29.2 1.3 %collective-permute-start.2 = (f32[8,32,128]{2,1,0:T(8,128)S(1)}, f32[8,32,128]{2,1,0:T(8,128)S(1)}, u32[]{:S(2)}, u32[]{:S(2)}) collective-permute-start(f32[8,32,128]{2,1,0:T(8,128)S(1)} %all_to_all.11.back_ref), channel_id=1, source_target_pairs={{0,1},{1,0},{2,3},{3,2},{4,5},{5,4},{6,7},{7,6},{8,9},{9,8},{10,11... | collective-permute-start | bytes 393224 | tf_op jit(solution)/shard_map/ppermute | solution.py:790

commit v9 on v8

--- a/solution.py
+++ b/solution.py
@@ -528,6 +528,7 @@
     sum_ref,
     partial_ref,
     ends,
+    turned=False,
 ):
     depth, rows, half = solved_ref.shape
     layers = 2 * depth
@@ -580,7 +581,7 @@
     modes = jnp.stack(found)
     sine, _ = parts_of(small_ref, depth * rows, depth)
     waves = from_modes(modes, sine)
-    cells = dot3(split(waves), table, (((1,), (1,)), ((), ())))
+    cells = dot3(split(waves), table, (((1,), (0 if turned else 1,)), ((), ())))
     return cells.reshape(depth, rows, half)
 
 
@@ -593,8 +594,10 @@
     weight_ref,
     inverse_ref,
     bins_ref,
+    both_ref,
     base_ref,
     gain_ref,
+    turned_ref,
     *scratch,
     ends,
     scale,
@@ -613,6 +616,8 @@
         )
         base_ref[:, :, :half] = gain_ref[:, :, :half] * cells
         base_ref[:, :, half:] = -(gain_ref[:, :, half:] * cells)
+        for part in range(2):
+            turned_ref[part] = both_ref[1 - side, part].T
 
     pl.when(dep_ref[0] == 0)(lambda: work(0))
     pl.when(dep_ref[0] == 1)(lambda: work(1))
@@ -639,9 +644,18 @@
     size = depth // cuts
 
     def work(side):
-        table = (table_ref[1 - side, 0], table_ref[1 - side, 1])
+        table = (table_ref[0], table_ref[1])
         cells = extend(
-            side, back_ref, solved_ref, table, small_ref, weight_ref, inverse_ref, *scratch, ends
+            side,
+            back_ref,
+            solved_ref,
+            table,
+            small_ref,
+            weight_ref,
+            inverse_ref,
+            *scratch,
+            ends,
+            True,
         )
         copies = []
         for cut in range(cuts):
@@ -789,14 +803,15 @@
     edges = lax.all_to_all(answered, "hor", split_axis=0, concat_axis=0, tiled=True)
     other_edges = lax.ppermute(edges, "dep", pairs)
     scratch = [pltpu.VMEM((layers, half), f32)] * 3 + [pltpu.VMEM(field, f32)]
-    base, gain = call(
+    both = jnp.asarray(table)
+    base, gain, turned = call(
         functools.partial(restore_kernel, ends=(near,), scale=1.0 / x_cells),
         [scalar(dep_index)]
         + [
             near_by(v)
-            for v in (edges, keep, table_here, small_here, weight, inverse, focus_bins)
+            for v in (edges, keep, table_here, small_here, weight, inverse, focus_bins, both)
         ],
-        [shape(*full)] * 2,
+        [shape(*full)] * 2 + [jax.ShapeDtypeStruct((2, half, half), bf16)],
         scratch,
     )
     return call(
@@ -807,7 +822,7 @@
             for v in (
                 other_edges,
                 got,
-                jnp.asarray(table),
+                turned,
                 small_here,
                 weight,
                 inverse_other,

time: 32.4 us -> 32.2 us (level)
  no operation moved by 1% of the time
where the time goes in v9:
time: 32.2 us; the launch traced here: 32 us
  blocking collectives  24.1 us (75%)
  Pallas kernels  6.69 us (21%)
  starting transfers between devices  0.65 us (2%)
  waiting for transfers between devices  0.44 us (1%)
    all_to_all x1, blocking collectives, body(): lax.all_to_all(outgoing, 'hor', split_axis=0, concat_axis=0, tiled=True)  14.4 us
    all_to_all x1, blocking collectives, body(): lax.all_to_all(answered, 'hor', split_axis=0, concat_axis=0, tiled=True)  9.74 us
    pallas_call x6, Pallas kernels, call(): pl.pallas_call(kernel, in_specs=specs, out_specs=out_specs if single else...  6.69 us
  transfers between devices with their start and end apart: 3, of which 1 were waited for; matrix products, arithmetic and copies ran while one was open for 0% of the time, Pallas kernels for 7%

profile of v9, /device:TPU:0, one launch (start us, length us, event | category | flops | bytes accessed | tf_op | source)
XLA Modules:
  0.0 32.0 jit_solution(11864332470589615996)
XLA Ops:
  0.0 1.3 %shard_map.73 = (f32[16,8,512]{2,1,0:T(8,128)S(1)}, f32[16,8,512]{2,1,0:T(8,128)S(1)}, f32[32,8,128]{2,1,0:T(8,128)S(1)}, bf16[160,384]{1,0:T(8,128)(2,1)S(1)}, ...) custom-call(s32[1]{0:T(128)} %bitcast.dep_ref, f32[16,8,1024]{2,1,0:T(8,128)} %residual_hbm.1, s32[16,8,1024]{2,1,0:T(8,128)} %bins_ref.1, ...), custom_call_target="tpu_custom_call" | custom-call | tf_op jit(solution)/shard_map/pallas_call | solution.py:688
  1.3 0.5 %collective-permute-start = (f32[16,8,512]{2,1,0:T(8,128)S(1)}, f32[16,8,512]{2,1,0:T(8,128)S(1)}, u32[]{:S(2)}, u32[]{:S(2)}) collective-permute-start(f32[16,8,512]{2,1,0:T(8,128)S(1)} %get-tuple-element.30), channel_id=1, source_target_pairs={{0,1},{1,0},{2,3},{3,2},{4,5},{5,4},{6,7},{7,6},{8,9},{9,8},{10,11... | collective-permute-start | bytes 786440 | tf_op jit(solution)/shard_map/ppermute | solution.py:773
  1.9 1.5 %shard_map.74 = (f32[16,8,512]{2,1,0:T(8,128)S(1)}, bf16[2,512,512]{2,1,0:T(8,128)(2,1)S(1)}, f32[32,8,512]{2,1,0:T(8,128)S(1)}, f32[32,8,512]{2,1,0:T(8,128)S(1)}, f32[32,32,128]{2,1,0:T(8,128)S(1)}) custom-call(s32[1]{0:T(128)} %bitcast.dep_ref, s32[1]{0:T(128)} %bitcast.1.spot_ref, f32[16,8,512]{2,1,0:T(8,128)S(1)} %get-tuple-element.24.own_ref, ...), custom_call_target="tpu_custom_call" | custom-call | tf_op jit(solution)/shard_map/pallas_call | solution.py:688
  3.4 0.0 copy-start
  3.4 0.0 copy-start.1
  3.4 0.0 collective-permute-done.recv_ref
  3.4 1.0 %shard_map.75 = (f32[8,32,128]{2,1,0:T(8,128)S(1)}, f32[16,8,512]{2,1,0:T(8,128)S(1)}, f32[16,8,512]{2,1,0:T(8,128)S(1)}) custom-call(s32[1]{0:T(128)} %bitcast.dep_ref, f32[16,8,512]{2,1,0:T(8,128)S(1)} %get-tuple-element.29.modes_ref, f32[16,8,512]{2,1,0:T(8,128)S(1)} %collective-permute-done.recv_ref, ...), custom_call_target="tpu_custom_call" | custom-call | tf_op jit(solution)/shard_map/pallas_call | solution.py:688
  4.4 0.1 collective-permute-start.1
  4.6 14.4 %all_to_all.10.packed_ref = f32[8,32,128]{2,1,0:T(8,128)S(1)} all-to-all(f32[8,32,128]{2,1,0:T(8,128)S(1)} %get-tuple-element.33), channel_id=1, replica_groups=mesh['grp'=2,'hor'=8,'dep'=2] {'hor'}, dimensions={0} | all-to-all | bytes 262144 | tf_op jit(solution)/shard_map/all_to_all | solution.py:795
  19.0 0.0 collective-permute-done.1.solved_ref
  19.0 0.4 %shard_map.76 = f32[8,32,128]{2,1,0:T(8,128)S(1)} custom-call(s32[1]{0:T(128)} %bitcast.1.spot_ref, f32[8,32,128]{2,1,0:T(8,128)S(1)} %all_to_all.10.packed_ref, f32[32,8,128]{2,1,0:T(8,128)S(1)} %get-tuple-element.25.weight_ref, f32[32,32,128]{2,1,0:T(8,128)S(1)} %get-tuple-element.36.inverse_ref), custom_call_target="tpu_custom_call" | custom-call | tf_op jit(solution)/shard_map/pallas_call | solution.py:688
  19.3 9.7 %all_to_all.11.back_ref = f32[8,32,128]{2,1,0:T(8,128)S(1)} all-to-all(f32[8,32,128]{2,1,0:T(8,128)S(1)} %shard_map.76), channel_id=1, replica_groups=mesh['grp'=2,'hor'=8,'dep'=2] {'hor'}, dimensions={0} | all-to-all | bytes 262144 | tf_op jit(solution)/shard_map/all_to_all | solution.py:803
  29.1 0.0 collective-permute-start.2
  29.1 0.0 copy-done
  29.1 0.0 copy-done.1
  29.1 0.9 %shard_map.77 = (f32[16,8,1024]{2,1,0:T(8,128)S(1)}, f32[16,8,1024]{2,1,0:T(8,128)S(1)}, bf16[2,512,512]{2,1,0:T(8,128)(2,1)S(1)}) custom-call(s32[1]{0:T(128)} %bitcast.dep_ref, f32[8,32,128]{2,1,0:T(8,128)S(1)} %all_to_all.11.back_ref, f32[16,8,512]{2,1,0:T(8,128)S(1)} %get-tuple-element.38.solved_ref, ...), custom_call_target="tpu_custom_call" | custom-call | tf_op jit(solution)/shard_map/pallas_call | solution.py:688
  30.0 0.4 %collective-permute-done.2.back_ref = f32[8,32,128]{2,1,0:T(8,128)S(1)} collective-permute-done((f32[8,32,128]{2,1,0:T(8,128)S(1)}, f32[8,32,128]{2,1,0:T(8,128)S(1)}, u32[]{:S(2)}, u32[]{:S(2)}) %collective-permute-start.2) | collective-permute-done | bytes 131104 | tf_op jit(solution)/shard_map/ppermute | solution.py:804
  30.4 1.6 %shard_map.78 = f32[16,8,1024]{2,1,0:T(8,128)} custom-call(s32[1]{0:T(128)} %bitcast.dep_ref, f32[8,32,128]{2,1,0:T(8,128)S(1)} %collective-permute-done.2.back_ref, f32[16,8,512]{2,1,0:T(8,128)S(1)} %collective-permute-done.1.solved_ref, bf16[2,512,512]{2,1,0:T(8,128)(2,1)S(1)} %get-tuple-element.39.table_ref, ...), custom_call_target="tpu_custom_call" | custom-call | tf_op jit(solution)/shard_map/pallas_call | solution.py:688
Async XLA Ops:
  1.3 2.0 %collective-permute-start = (f32[16,8,512]{2,1,0:T(8,128)S(1)}, f32[16,8,512]{2,1,0:T(8,128)S(1)}, u32[]{:S(2)}, u32[]{:S(2)}) collective-permute-start(f32[16,8,512]{2,1,0:T(8,128)S(1)} %get-tuple-element.30), channel_id=1, source_target_pairs={{0,1},{1,0},{2,3},{3,2},{4,5},{5,4},{6,7},{7,6},{8,9},{9,8},{10,11... | collective-permute-start | bytes 786440 | tf_op jit(solution)/shard_map/ppermute | solution.py:773
  3.4 25.7 %copy-start = (bf16[2,2,512,512]{3,2,1,0:T(8,128)(2,1)S(1)}, bf16[2,2,512,512]{3,2,1,0:T(8,128)(2,1)}, u32[]{:S(2)}) copy-start(bf16[2,2,512,512]{3,2,1,0:T(8,128)(2,1)} %constant.21.clone.table_hbm.both_ref) | copy-start | bytes 6291460
  3.4 25.7 %copy-start.1 = (s32[16,8,1024]{2,1,0:T(8,128)S(1)}, s32[16,8,1024]{2,1,0:T(8,128)}, u32[]{:S(2)}) copy-start(s32[16,8,1024]{2,1,0:T(8,128)} %bins_ref.1) | copy-start | bytes 1572868
  4.4 14.5 %collective-permute-start.1 = (f32[16,8,512]{2,1,0:T(8,128)S(1)}, f32[16,8,512]{2,1,0:T(8,128)S(1)}, u32[]{:S(2)}, u32[]{:S(2)}) collective-permute-start(f32[16,8,512]{2,1,0:T(8,128)S(1)} %get-tuple-element.34), channel_id=1, source_target_pairs={{0,1},{1,0},{2,3},{3,2},{4,5},{5,4},{6,7},{7,6},{8,9},{9,8},{10,11... | collective-permute-start | bytes 786440 | tf_op jit(solution)/shard_map/ppermute | solution.py:794
  29.1 1.3 %collective-permute-start.2 = (f32[8,32,128]{2,1,0:T(8,128)S(1)}, f32[8,32,128]{2,1,0:T(8,128)S(1)}, u32[]{:S(2)}, u32[]{:S(2)}) collective-permute-start(f32[8,32,128]{2,1,0:T(8,128)S(1)} %all_to_all.11.back_ref), channel_id=1, source_target_pairs={{0,1},{1,0},{2,3},{3,2},{4,5},{5,4},{6,7},{7,6},{8,9},{9,8},{10,11... | collective-permute-start | bytes 393224 | tf_op jit(solution)/shard_map/ppermute | solution.py:804

commit v10 on v9

--- a/solution.py
+++ b/solution.py
@@ -297,9 +297,6 @@
     packed_ref,
     keep_ref,
     give_ref,
-    source_ref,
-    solved_ref,
-    stage_ref,
     partial_ref,
 ):
     depth, rows, half = recv_ref.shape
@@ -307,30 +304,42 @@
     block = depth * rows
     hor_count = packed_ref.shape[0]
     chunk = half // hor_count
-    place = dep_ref[0] * depth
-    sine, edge = parts_of(small_ref, block, depth)
-    source_ref[pl.ds(place, depth)] = modes_ref[...]
-    source_ref[pl.ds(depth - place, depth)] = to_modes(
-        recv_ref[...], (table_ref[0], table_ref[1]), sine
-    )
-    weights, couple = layer_terms(weight_ref, half // lanes, 1)
-    edge_row = lax.broadcasted_iota(jnp.int32, (rows, half), 0) == 0
-
-    def emit(layer, values):
-        solved_ref[layer] = values
-        stage_ref[layer] = jnp.where(edge_row, source_ref[layer], weights[layer] * values)
-
-    substitute(couple, inverse_ref, partial_ref, lambda layer: source_ref[layer], emit)
-    keep_ref[...] = solved_ref[pl.ds(place, depth)]
-    give_ref[...] = solved_ref[pl.ds(depth - place, depth)]
-    lower = []
-    upper = []
-    for part in range(2):
-        both = from_modes(stage_ref[part * depth : (part + 1) * depth], edge)
-        lower.append(both[:depth])
-        upper.append(both[depth:])
-    lower = jnp.concatenate(lower, axis=0)
-    upper = jnp.concatenate(upper, axis=0)
+
+    def work(side):
+        sine, edge = parts_of(small_ref, block, depth)
+        modes = to_modes(recv_ref[...], (table_ref[0], table_ref[1]), sine)
+        weights, couple = layer_terms(weight_ref, half // lanes, 1)
+        edge_row = lax.broadcasted_iota(jnp.int32, (rows, half), 0) == 0
+        staged = [None] * layers
+
+        def source(layer):
+            if layer // depth == side:
+                return modes_ref[layer - side * depth]
+            return modes[layer - (1 - side) * depth]
+
+        def emit(layer, values):
+            if layer // depth == side:
+                keep_ref[layer - side * depth] = values
+            else:
+                give_ref[layer - (1 - side) * depth] = values
+            staged[layer] = jnp.where(edge_row, source(layer), weights[layer] * values)
+
+        substitute(couple, inverse_ref, partial_ref, source, emit)
+        lower = []
+        upper = []
+        for part in range(2):
+            both = from_modes(jnp.stack(staged[part * depth : (part + 1) * depth]), edge)
+            lower.append(both[:depth])
+            upper.append(both[depth:])
+        pack(jnp.concatenate(lower, axis=0), jnp.concatenate(upper, axis=0), packed_ref)
+
+    pl.when(dep_ref[0] == 0)(lambda: work(0))
+    pl.when(dep_ref[0] == 1)(lambda: work(1))
+
+
+def pack(lower, upper, packed_ref):
+    hor_count, layers, _ = packed_ref.shape
+    chunk = lower.shape[1] // hor_count
     lane = lax.broadcasted_iota(jnp.int32, (layers, lanes), 1)
     if 2 * chunk == lanes:
         for tile in range(hor_count // 2):
@@ -789,7 +798,7 @@
         [scalar(dep_index)]
         + [near_by(v) for v in (modes, recv, table_here, small_here, weight, inverse)],
         [shape(*packed), shape(*slab), shape(*slab)],
-        [pltpu.VMEM(field, f32)] * 4,
+        [pltpu.VMEM(field, f32)],
     )
     got = lax.ppermute(give, "dep", pairs)
     incoming = lax.all_to_all(outgoing, "hor", split_axis=0, concat_axis=0, tiled=True)

time: 32.2 us -> 32.2 us (level)
  transfers between devices with their start and end apart: 3 -> 3, of which waited for: 1 -> 1; matrix products, arithmetic and copies ran while one was open for 0% -> 0% of each run, Pallas kernels for 7% -> 8%
where the time goes in v10:
time: 32.2 us; the launch traced here: 31.9 us
  blocking collectives  24.1 us (75%)
  Pallas kernels  6.71 us (21%)
  starting transfers between devices  0.59 us (2%)
  waiting for transfers between devices  0.43 us (1%)
    all_to_all x1, blocking collectives, body(): lax.all_to_all(outgoing, 'hor', split_axis=0, concat_axis=0, tiled=True)  14.4 us
    all_to_all x1, blocking collectives, body(): lax.all_to_all(answered, 'hor', split_axis=0, concat_axis=0, tiled=True)  9.74 us
    pallas_call x6, Pallas kernels, call(): pl.pallas_call(kernel, in_specs=specs, out_specs=out_specs if single else...  6.71 us
  transfers between devices with their start and end apart: 3, of which 1 were waited for; matrix products, arithmetic and copies ran while one was open for 0% of the time, Pallas kernels for 8%

profile of v10, /device:TPU:0, one launch (start us, length us, event | category | flops | bytes accessed | tf_op | source)
XLA Modules:
  0.0 31.9 jit_solution(13378709312693661811)
XLA Ops:
  0.0 1.3 %shard_map.73 = (f32[16,8,512]{2,1,0:T(8,128)S(1)}, f32[16,8,512]{2,1,0:T(8,128)S(1)}, f32[32,8,128]{2,1,0:T(8,128)S(1)}, bf16[160,384]{1,0:T(8,128)(2,1)S(1)}, ...) custom-call(s32[1]{0:T(128)} %bitcast.dep_ref, f32[16,8,1024]{2,1,0:T(8,128)} %residual_hbm.1, s32[16,8,1024]{2,1,0:T(8,128)} %bins_ref.1, ...), custom_call_target="tpu_custom_call" | custom-call | tf_op jit(solution)/shard_map/pallas_call | solution.py:697
  1.3 0.5 %collective-permute-start = (f32[16,8,512]{2,1,0:T(8,128)S(1)}, f32[16,8,512]{2,1,0:T(8,128)S(1)}, u32[]{:S(2)}, u32[]{:S(2)}) collective-permute-start(f32[16,8,512]{2,1,0:T(8,128)S(1)} %get-tuple-element.30), channel_id=1, source_target_pairs={{0,1},{1,0},{2,3},{3,2},{4,5},{5,4},{6,7},{7,6},{8,9},{9,8},{10,11... | collective-permute-start | bytes 786440 | tf_op jit(solution)/shard_map/ppermute | solution.py:782
  1.9 1.5 %shard_map.74 = (f32[16,8,512]{2,1,0:T(8,128)S(1)}, bf16[2,512,512]{2,1,0:T(8,128)(2,1)S(1)}, f32[32,8,512]{2,1,0:T(8,128)S(1)}, f32[32,8,512]{2,1,0:T(8,128)S(1)}, f32[32,32,128]{2,1,0:T(8,128)S(1)}) custom-call(s32[1]{0:T(128)} %bitcast.dep_ref, s32[1]{0:T(128)} %bitcast.1.spot_ref, f32[16,8,512]{2,1,0:T(8,128)S(1)} %get-tuple-element.24.own_ref, ...), custom_call_target="tpu_custom_call" | custom-call | tf_op jit(solution)/shard_map/pallas_call | solution.py:697
  3.4 0.0 copy-start
  3.4 0.0 copy-start.1
  3.4 0.0 collective-permute-done.recv_ref
  3.4 1.0 %shard_map.75 = (f32[8,32,128]{2,1,0:T(8,128)S(1)}, f32[16,8,512]{2,1,0:T(8,128)S(1)}, f32[16,8,512]{2,1,0:T(8,128)S(1)}) custom-call(s32[1]{0:T(128)} %bitcast.dep_ref, f32[16,8,512]{2,1,0:T(8,128)S(1)} %get-tuple-element.29.modes_ref, f32[16,8,512]{2,1,0:T(8,128)S(1)} %collective-permute-done.recv_ref, ...), custom_call_target="tpu_custom_call" | custom-call | tf_op jit(solution)/shard_map/pallas_call | solution.py:697
  4.4 0.1 collective-permute-start.1
  4.5 14.4 %all_to_all.10.packed_ref = f32[8,32,128]{2,1,0:T(8,128)S(1)} all-to-all(f32[8,32,128]{2,1,0:T(8,128)S(1)} %get-tuple-element.33), channel_id=1, replica_groups=mesh['grp'=2,'hor'=8,'dep'=2] {'hor'}, dimensions={0} | all-to-all | bytes 262144 | tf_op jit(solution)/shard_map/all_to_all | solution.py:804
  18.9 0.0 collective-permute-done.1.solved_ref
  18.9 0.4 %shard_map.76 = f32[8,32,128]{2,1,0:T(8,128)S(1)} custom-call(s32[1]{0:T(128)} %bitcast.1.spot_ref, f32[8,32,128]{2,1,0:T(8,128)S(1)} %all_to_all.10.packed_ref, f32[32,8,128]{2,1,0:T(8,128)S(1)} %get-tuple-element.25.weight_ref, f32[32,32,128]{2,1,0:T(8,128)S(1)} %get-tuple-element.36.inverse_ref), custom_call_target="tpu_custom_call" | custom-call | tf_op jit(solution)/shard_map/pallas_call | solution.py:697
  19.3 9.7 %all_to_all.11.back_ref = f32[8,32,128]{2,1,0:T(8,128)S(1)} all-to-all(f32[8,32,128]{2,1,0:T(8,128)S(1)} %shard_map.76), channel_id=1, replica_groups=mesh['grp'=2,'hor'=8,'dep'=2] {'hor'}, dimensions={0} | all-to-all | bytes 262144 | tf_op jit(solution)/shard_map/all_to_all | solution.py:812
  29.0 0.0 collective-permute-start.2
  29.0 0.0 copy-done
  29.0 0.0 copy-done.1
  29.0 0.9 %shard_map.77 = (f32[16,8,1024]{2,1,0:T(8,128)S(1)}, f32[16,8,1024]{2,1,0:T(8,128)S(1)}, bf16[2,512,512]{2,1,0:T(8,128)(2,1)S(1)}) custom-call(s32[1]{0:T(128)} %bitcast.dep_ref, f32[8,32,128]{2,1,0:T(8,128)S(1)} %all_to_all.11.back_ref, f32[16,8,512]{2,1,0:T(8,128)S(1)} %get-tuple-element.38.solved_ref, ...), custom_call_target="tpu_custom_call" | custom-call | tf_op jit(solution)/shard_map/pallas_call | solution.py:697
  29.9 0.4 %collective-permute-done.2.back_ref = f32[8,32,128]{2,1,0:T(8,128)S(1)} collective-permute-done((f32[8,32,128]{2,1,0:T(8,128)S(1)}, f32[8,32,128]{2,1,0:T(8,128)S(1)}, u32[]{:S(2)}, u32[]{:S(2)}) %collective-permute-start.2) | collective-permute-done | bytes 131104 | tf_op jit(solution)/shard_map/ppermute | solution.py:813
  30.4 1.6 %shard_map.78 = f32[16,8,1024]{2,1,0:T(8,128)} custom-call(s32[1]{0:T(128)} %bitcast.dep_ref, f32[8,32,128]{2,1,0:T(8,128)S(1)} %collective-permute-done.2.back_ref, f32[16,8,512]{2,1,0:T(8,128)S(1)} %collective-permute-done.1.solved_ref, bf16[2,512,512]{2,1,0:T(8,128)(2,1)S(1)} %get-tuple-element.39.table_ref, ...), custom_call_target="tpu_custom_call" | custom-call | tf_op jit(solution)/shard_map/pallas_call | solution.py:697
Async XLA Ops:
  1.3 2.0 %collective-permute-start = (f32[16,8,512]{2,1,0:T(8,128)S(1)}, f32[16,8,512]{2,1,0:T(8,128)S(1)}, u32[]{:S(2)}, u32[]{:S(2)}) collective-permute-start(f32[16,8,512]{2,1,0:T(8,128)S(1)} %get-tuple-element.30), channel_id=1, source_target_pairs={{0,1},{1,0},{2,3},{3,2},{4,5},{5,4},{6,7},{7,6},{8,9},{9,8},{10,11... | collective-permute-start | bytes 786440 | tf_op jit(solution)/shard_map/ppermute | solution.py:782
  3.4 25.7 %copy-start = (bf16[2,2,512,512]{3,2,1,0:T(8,128)(2,1)S(1)}, bf16[2,2,512,512]{3,2,1,0:T(8,128)(2,1)}, u32[]{:S(2)}) copy-start(bf16[2,2,512,512]{3,2,1,0:T(8,128)(2,1)} %constant.21.clone.table_hbm.both_ref) | copy-start | bytes 6291460
  3.4 25.7 %copy-start.1 = (s32[16,8,1024]{2,1,0:T(8,128)S(1)}, s32[16,8,1024]{2,1,0:T(8,128)}, u32[]{:S(2)}) copy-start(s32[16,8,1024]{2,1,0:T(8,128)} %bins_ref.1) | copy-start | bytes 1572868
  4.4 14.5 %collective-permute-start.1 = (f32[16,8,512]{2,1,0:T(8,128)S(1)}, f32[16,8,512]{2,1,0:T(8,128)S(1)}, u32[]{:S(2)}, u32[]{:S(2)}) collective-permute-start(f32[16,8,512]{2,1,0:T(8,128)S(1)} %get-tuple-element.34), channel_id=1, source_target_pairs={{0,1},{1,0},{2,3},{3,2},{4,5},{5,4},{6,7},{7,6},{8,9},{9,8},{10,11... | collective-permute-start | bytes 786440 | tf_op jit(solution)/shard_map/ppermute | solution.py:803
  29.0 1.3 %collective-permute-start.2 = (f32[8,32,128]{2,1,0:T(8,128)S(1)}, f32[8,32,128]{2,1,0:T(8,128)S(1)}, u32[]{:S(2)}, u32[]{:S(2)}) collective-permute-start(f32[8,32,128]{2,1,0:T(8,128)S(1)} %all_to_all.11.back_ref), channel_id=1, source_target_pairs={{0,1},{1,0},{2,3},{3,2},{4,5},{5,4},{6,7},{7,6},{8,9},{9,8},{10,11... | collective-permute-start | bytes 393224 | tf_op jit(solution)/shard_map/ppermute | solution.py:813
